TPU v7x, 32 devices: a whole 2x2x4 slice. The times are simulated.
32 devices in a mesh: groups: 2 (over y), expert: 8 (over z, core), attn: 2 (over x).
Axes of the slice: x: 2, y: 2, z: 4, core: 2. Of those that a mesh axis runs over, the one named last changes fastest.
Arguments:
- tokens: bfloat16 [512, 3584], P(('groups', 'expert')), parts along dimension 0, may hold values from -6 to 6
- gates: float32 [512, 8], P(('groups', 'expert')), parts along dimension 0, may hold values from 0.05 to 0.6
- slots: int32 [512, 8], P(('groups', 'expert')), parts along dimension 0, may hold values from 0 to 15, all different within a row; in each aligned block of 32 rows (0 to 31, 32 to 63, ...) at most 20 rows name the same one
- plan: int32 [16], P('groups'), parts along dimension 0, may hold values from 0 to 7, as said below
- gate_proj: bfloat16 [8, 3584, 1024], P('expert', None, 'attn'), may hold values from -0.09375 to 0.09375
- up_proj: bfloat16 [8, 3584, 1024], P('expert', None, 'attn'), may hold values from -0.09375 to 0.09375
- down_proj: bfloat16 [8, 3584, 1024], P('expert', None, 'attn'), may hold values from -0.1875 to 0.1875
Outputs:
- moe_out: bfloat16 [512, 3584], P(('groups', 'expert')), parts along dimension 0
There are 2 independent parts, one for each index of `groups`. A program takes and returns all parts, laid end to end along the dimension named above; an argument that names none is the same for every part. Nothing has to cross between parts.
Inputs may be any that keep to these rules, and one draw needn't show every extreme that they name: A row's 8 slots are distinct; among the 32 rows of one index of expert (aligned blocks) no slot is named more than 20 times, a bound that some block reaches. plan[d] is never d; no expert is named by more than 2 entries of plan, and some expert by exactly 2.
All inputs are finite; a program needn't handle non-finite values.
Results may differ from a plain program's by a relative error of at most 0.014.
Values may be sent and summed in bfloat16 or wider, within the bound.
No kernel may reach another device: no remote copies, remote signals or barrier semaphores. Data moves between devices by JAX's collectives and lax.ppermute only.
A program may use at most 128 MiB of HBM per device.

v0:
```python
import jax
import jax.numpy as jnp
from jax import lax
from jax.sharding import PartitionSpec as P

MULT = 2


def expert_rows(rows, w_gate, w_up, w_down):
    gate_act = jnp.dot(rows, w_gate, preferred_element_type=jnp.float32)
    up_act = jnp.dot(rows, w_up, preferred_element_type=jnp.float32)
    hidden = (jax.nn.silu(gate_act) * up_act).astype(jnp.bfloat16)
    down_out = jnp.einsum("rf,df->rd", hidden, w_down, preferred_element_type=jnp.float32)
    return down_out.astype(jnp.bfloat16)


def slot_ranks(slot_keys, key_count):
    onehot = (slot_keys[:, None] == jnp.arange(key_count, dtype=jnp.int32)[None, :]).astype(
        jnp.int32
    )
    return jnp.sum(jnp.cumsum(onehot, axis=0) * onehot, axis=1) - 1


def spread_rows(row_index, row_total, tok_count, top_count):
    matches = (
        row_index.reshape(tok_count, top_count)[None, :, :]
        == jnp.arange(row_total, dtype=jnp.int32)[:, None, None]
    )
    return jnp.sum(matches.astype(jnp.int32), axis=2).astype(jnp.bfloat16)


def body(tokens, gates, slots, plan, gate_proj, up_proj, down_proj):
    experts = lax.axis_size("expert")
    tok_count, model_width = tokens.shape
    top_count = slots.shape[1]
    capacity = max(2, min(tok_count, tok_count * top_count * 5 // (8 * experts)))
    flat_slots = slots.reshape(-1)
    device = flat_slots // 2
    slot_kind = flat_slots % 2
    owner_device = jnp.where(slot_kind == 0, device, plan[device])
    per_owner = (1 + MULT) * capacity
    position = slot_ranks(owner_device, experts)
    row_index = owner_device * per_owner + position
    row_total = experts * per_owner
    dispatch = spread_rows(row_index, row_total, tok_count, top_count)
    outgoing = jnp.dot(dispatch, tokens, preferred_element_type=jnp.float32).astype(jnp.bfloat16)
    outgoing = outgoing.reshape(experts, per_owner, model_width)
    incoming = lax.all_to_all(outgoing, "expert", split_axis=0, concat_axis=0, tiled=True)
    results = expert_rows(
        incoming.reshape(row_total, model_width), gate_proj[0], up_proj[0], down_proj[0]
    )
    results = results.reshape(experts, per_owner, model_width)
    returned = lax.all_to_all(results, "expert", split_axis=0, concat_axis=0, tiled=True).reshape(
        row_total, model_width
    )
    choice_rows = row_index.reshape(tok_count, top_count)
    partial_value = jnp.zeros((tok_count, returned.shape[1]), jnp.float32)
    for column in range(top_count):
        partial_value = (
            partial_value
            + returned[choice_rows[:, column]].astype(jnp.float32) * gates[:, column][:, None]
        )
    return lax.psum(partial_value.astype(jnp.bfloat16), "attn")


def solution(mesh):
    return jax.shard_map(
        body,
        mesh=mesh,
        in_specs=(
            P(("groups", "expert"), None),
            P(("groups", "expert"), None),
            P(("groups", "expert"), None),
            P("groups"),
            P("expert", None, "attn"),
            P("expert", None, "attn"),
            P("expert", None, "attn"),
        ),
        out_specs=P(("groups", "expert"), None),
        check_vma=False,
    )
```

profile of v0, /device:TPU:0, one launch (start us, length us, event | category | flops | bytes accessed | tf_op | source)
XLA Modules:
  0.0 286.4 jit_solution(9104749936648108147)
XLA Ops:
  6.5 0.8 copy.23
  7.3 0.1 reshape.197
  7.6 1.6 fusion.32
  9.2 4.3 %compare_select_fusion.9 = (s32[256,1]{0,1:T(1,128)S(1)}, s32[256,1]{0,1:T(1,128)S(1)}) fusion(s32[]{:T(128)} %bitcast.1, s32[]{:T(128)} %bitcast.2, s32[]{:T(128)} %bitcast.3, s32[]{:T(128)} %bitcast.4, s32[]{:T(128)} %bitcast.5, s32[]{:T(128)} %bitcast.7, s32[]{:T(128)} %bitcast.6, s32[256,1]{0,1:T(1,128)S(1)} %reshape.197), kind=kLoop, calls=%fused_computation.66 | loop fusion | flops 7680 | bytes 3100 | tf_op jit(solution)/shard_map/gather | solution.py:40
  13.6 0.7 compare_select_fusion.19
  14.3 0.6 reduce-window.6
  14.9 0.2 slice_reduce_fusion
  15.2 0.1 fusion.29
  15.4 0.2 convert_reduce_fusion
  15.7 2.9 convolution_convert_fusion.1
  18.5 4.6 %reshape.201 = bf16[8,60,3584]{2,1,0:T(8,128)(2,1)} reshape(bf16[480,3584]{1,0:T(8,128)(2,1)} %convolution_convert_fusion.1) | data formatting | bytes 6881280 | tf_op jit(solution)/shard_map/reshape | solution.py:47
  23.1 89.2 %all_to_all.10 = bf16[8,60,3584]{2,1,0:T(8,128)(2,1)} all-to-all(bf16[8,60,3584]{2,1,0:T(8,128)(2,1)} %reshape.201), channel_id=1, replica_groups=mesh['groups'=2,'expert'=8,'attn'=2] {'expert'}, dimensions={0} | all-to-all | bytes 6881280 | tf_op jit(solution)/shard_map/all_to_all | solution.py:48
  112.3 4.6 %reshape.202 = bf16[480,3584]{1,0:T(8,128)(2,1)} reshape(bf16[8,60,3584]{2,1,0:T(8,128)(2,1)} %all_to_all.10) | data formatting | bytes 6881280 | tf_op jit(solution)/shard_map/reshape | solution.py:50
  116.9 5.0 %fusion.3 = f32[480,512]{1,0:T(8,128)S(1)} fusion(bf16[480,3584]{1,0:T(8,128)(2,1)} %reshape.202, bf16[1,3584,512]{2,1,0:T(8,128)(2,1)} %param.11), kind=kOutput, calls=%fused_computation.13 | convolution fusion | flops 1761607680 | bytes 8093696 | tf_op jit(solution)/shard_map/dot_general | solution.py:10
  121.9 9.7 %convolution_convert_fusion = bf16[480,3584]{1,0:T(8,128)(2,1)} fusion(bf16[1,3584,512]{2,1,0:T(8,128)(2,1)} %param.13, bf16[480,3584]{1,0:T(8,128)(2,1)} %reshape.202, bf16[1,3584,512]{2,1,0:T(8,128)(2,1)} %param.12, f32[480,512]{1,0:T(8,128)S(1)} %fusion.3), kind=kOutput, calls=%fused_computation.8 | convolution fusion | flops 3526410240 | bytes 15204352 | tf_op jit(solution)/shard_map/rf,df->rd/dot_general | solution.py:13
  131.7 4.6 %reshape.203 = bf16[8,60,3584]{2,1,0:T(8,128)(2,1)} reshape(bf16[480,3584]{1,0:T(8,128)(2,1)} %convolution_convert_fusion) | data formatting | bytes 6881280 | tf_op jit(solution)/shard_map/reshape | solution.py:52
  136.3 4.6 %all-to-all-start.1 = ((bf16[8,60,3584]{2,1,0:T(8,128)(2,1)}), bf16[8,60,3584]{2,1,0:T(8,128)(2,1)}, u32[]{:S(2)}, u32[]{:S(2)}) async-start(bf16[8,60,3584]{2,1,0:T(8,128)(2,1)} %reshape.203), calls=%async_computation.1 | async-start | bytes 7340032 | tf_op jit(solution)/shard_map/all_to_all | solution.py:53
  140.9 0.2 all-reduce.2.cloned.1.call-start
  141.2 0.3 fusion.19
  141.6 82.1 %all-to-all-done.1 = bf16[8,60,3584]{2,1,0:T(8,128)(2,1)} async-done(((bf16[8,60,3584]{2,1,0:T(8,128)(2,1)}), bf16[8,60,3584]{2,1,0:T(8,128)(2,1)}, u32[]{:S(2)}, u32[]{:S(2)}) %all-to-all-start.1) | async-done | bytes 3440672 | tf_op jit(solution)/shard_map/all_to_all | solution.py:53
  223.7 4.6 %reshape.204 = bf16[480,3584]{1,0:T(8,128)(2,1)} reshape(bf16[8,60,3584]{2,1,0:T(8,128)(2,1)} %all-to-all-done.1) | data formatting | bytes 6881280 | tf_op jit(solution)/shard_map/reshape | solution.py:53
  228.3 3.3 %gather_fusion = bf16[32,3584]{1,0:T(8,128)(2,1)S(1)} fusion(bf16[480,3584]{1,0:T(8,128)(2,1)} %reshape.204, s32[1024]{0:T(1024)S(1)} %get-tuple-element.40), kind=kCustom, calls=%fused_computation | custom fusion | bytes 458880 | tf_op jit(solution)/shard_map/gather | solution.py:61
  231.6 3.3 %gather_fusion.1 = bf16[32,3584]{1,0:T(8,128)(2,1)S(1)} fusion(bf16[480,3584]{1,0:T(8,128)(2,1)} %reshape.204, s32[1024]{0:T(1024)S(1)} %get-tuple-element.39), kind=kCustom, calls=%fused_computation.1 | custom fusion | bytes 458880 | tf_op jit(solution)/shard_map/gather | solution.py:61
  234.9 3.3 %gather_fusion.2 = bf16[32,3584]{1,0:T(8,128)(2,1)S(1)} fusion(bf16[480,3584]{1,0:T(8,128)(2,1)} %reshape.204, s32[1024]{0:T(1024)S(1)} %get-tuple-element.38), kind=kCustom, calls=%fused_computation.2 | custom fusion | bytes 458880 | tf_op jit(solution)/shard_map/gather | solution.py:61
  238.3 3.3 %gather_fusion.3 = bf16[32,3584]{1,0:T(8,128)(2,1)S(1)} fusion(bf16[480,3584]{1,0:T(8,128)(2,1)} %reshape.204, s32[1024]{0:T(1024)S(1)} %get-tuple-element.37), kind=kCustom, calls=%fused_computation.3 | custom fusion | bytes 458880 | tf_op jit(solution)/shard_map/gather | solution.py:61
  241.6 3.3 %gather_fusion.4 = bf16[32,3584]{1,0:T(8,128)(2,1)S(1)} fusion(bf16[480,3584]{1,0:T(8,128)(2,1)} %reshape.204, s32[1024]{0:T(1024)S(1)} %get-tuple-element.36), kind=kCustom, calls=%fused_computation.4 | custom fusion | bytes 458880 | tf_op jit(solution)/shard_map/gather | solution.py:61
  244.9 3.3 %gather_fusion.5 = bf16[32,3584]{1,0:T(8,128)(2,1)S(1)} fusion(bf16[480,3584]{1,0:T(8,128)(2,1)} %reshape.204, s32[1024]{0:T(1024)S(1)} %get-tuple-element.35), kind=kCustom, calls=%fused_computation.5 | custom fusion | bytes 458880 | tf_op jit(solution)/shard_map/gather | solution.py:61
  248.2 3.3 %gather_fusion.6 = bf16[32,3584]{1,0:T(8,128)(2,1)S(1)} fusion(bf16[480,3584]{1,0:T(8,128)(2,1)} %reshape.204, s32[1024]{0:T(1024)S(1)} %get-tuple-element.34), kind=kCustom, calls=%fused_computation.6 | custom fusion | bytes 458880 | tf_op jit(solution)/shard_map/gather | solution.py:61
  251.6 3.3 %gather_fusion.7 = bf16[32,3584]{1,0:T(8,128)(2,1)S(1)} fusion(bf16[480,3584]{1,0:T(8,128)(2,1)} %reshape.204, s32[1024]{0:T(1024)S(1)} %get-tuple-element.33), kind=kCustom, calls=%fused_computation.7 | custom fusion | bytes 458880 | tf_op jit(solution)/shard_map/gather | solution.py:61
  254.9 1.1 add_convert_fusion
  256.0 21.9 %all-reduce.2.cloned.1.call-done = bf16[32,3584]{1,0:T(8,128)(2,1)} async-done(((bf16[32,3584]{1,0:T(8,128)(2,1)}), bf16[32,3584]{1,0:T(8,128)(2,1)}) %all-reduce.2.cloned.1.call-update) | async-done | bytes 229392 | tf_op jit(solution)/shard_map/psum | solution.py:63
  277.9 1.6 copy.31
  (21 shorter events, 0.5 us)
Async XLA Ops:
  6.5 9.1 %copy-start = (bf16[32,3584]{1,0:T(8,128)(2,1)S(1)}, bf16[32,3584]{1,0:T(8,128)(2,1)}, u32[]{:S(2)}) copy-start(bf16[32,3584]{1,0:T(8,128)(2,1)} %param.7) | copy-start | bytes 688132
  136.3 5.2 %copy-start.1 = (f32[32,8]{0,1:T(8,128)S(1)}, f32[32,8]{0,1:T(8,128)}, u32[]{:S(2)}) copy-start(f32[32,8]{0,1:T(8,128)} %param.8) | copy-start | bytes 3076
  136.3 87.4 %all-to-all-start.1 = ((bf16[8,60,3584]{2,1,0:T(8,128)(2,1)}), bf16[8,60,3584]{2,1,0:T(8,128)(2,1)}, u32[]{:S(2)}, u32[]{:S(2)}) async-start(bf16[8,60,3584]{2,1,0:T(8,128)(2,1)} %reshape.203), calls=%async_computation.1 | async-start | bytes 7340032 | tf_op jit(solution)/shard_map/all_to_all | solution.py:53
  140.9 137.0 %all-reduce.2.cloned.1.call-start = ((), (), s32[]{:S(2)}) async-start(), calls=%async_computation.2 | async-start | bytes 458752 | tf_op jit(solution)/shard_map/psum | solution.py:63
Sparse Core Ops, SparseCore 0:
  256.2 21.7 all-reduce.1
where the time goes:
time: 287 us; the launch traced here: 286 us
  waiting for transfers between devices  104 us (36%)
  blocking collectives  89.2 us (31%)
  local copies, waits for them, and re-layouts  49.7 us (17%)
  matrix products  17.6 us (6%)
  between operations  13.6 us (5%)
  other arithmetic  7.44 us (3%)
  starting transfers between devices  4.85 us (2%)
    all_to_all x1, blocking collectives, body(): lax.all_to_all(outgoing, 'expert', split_axis=0, concat_axis=0, tiled=True)  89.2 us
    all_to_all x1, waiting for transfers between devices, body(): lax.all_to_all(results, 'expert', split_axis=0, concat_axis=0, tiled=True)  82.1 us
    gather x8, local copies, waits for them, and re-layouts, body(): returned[choice_rows[:, column]].astype(jnp.float32)  26.6 us
    psum x1, waiting for transfers between devices, body(): return lax.psum(partial_value.astype(jnp.bfloat16), 'attn')  21.9 us
    dot_general x1, matrix products, expert_rows(): jnp.einsum('rf,df->rd', hidden, w_down, preferred_element_type=jnp.float32)  9.75 us
  transfers between devices with their start and end apart: 2, of which 2 were waited for; matrix products, arithmetic and copies ran while one was open for 0% of the time, Pallas kernels for 0%

commit v1 on v0

v1 whole, which is shorter than its diff:
```python
import functools

import jax
import jax.numpy as jnp
from jax import lax
from jax.experimental import pallas as pl
from jax.experimental.pallas import tpu as pltpu
from jax.sharding import PartitionSpec as P

LANES = 128
VMEM = pl.BlockSpec(memory_space=pltpu.VMEM)
SMEM = pl.BlockSpec(memory_space=pltpu.SMEM)


def expert_weights(slots, gates, plan_ref, experts):
    owner = slots >> 1
    copied = jnp.zeros_like(slots)
    for d in range(experts):
        copied = jnp.where(owner == d, plan_ref[d], copied)
    chosen = jnp.where((slots & 1) == 0, owner, copied)
    return [
        jnp.sum(jnp.where(chosen == e, gates, 0.0), axis=0, keepdims=True)
        for e in range(experts)
    ]


def prepare_kernel(experts, at_ref, plan_ref, slots_ref, gates_ref, tok_ref, all_ref, mine_ref, w_ref):
    count, width = tok_ref.shape
    half = count // 2
    sums = expert_weights(slots_ref[...], gates_ref[...], plan_ref, experts)
    high = [s.astype(jnp.bfloat16).astype(jnp.float32) for s in sums]
    low = [s - h for s, h in zip(sums, high)]
    pad = jnp.zeros((LANES - 2 * experts, count), jnp.float32)
    table = jnp.concatenate(high + low + [pad], axis=0)
    table = jnp.concatenate([table, jnp.zeros((LANES, LANES - count), jnp.float32)], axis=1)
    w_ref[...] = table.T[:count]
    for place in range(2):
        start = pl.multiple_of((at_ref[0] ^ place) * half, half)
        rows = tok_ref[pl.ds(start, half), :]
        weights = w_ref[pl.ds(start, half), :].astype(jnp.bfloat16)
        here = pl.ds(place * half, half)
        all_ref[here, pl.ds(0, width)] = rows
        all_ref[here, pl.ds(width, LANES)] = weights
        if place == 0:
            mine_ref[:, pl.ds(0, width)] = rows
            mine_ref[:, pl.ds(width, LANES)] = weights


def prepare(tokens, gates, slots, plan, experts, attn_at):
    count, width = tokens.shape
    return pl.pallas_call(
        functools.partial(prepare_kernel, experts),
        out_shape=(
            jax.ShapeDtypeStruct((count, width + LANES), jnp.bfloat16),
            jax.ShapeDtypeStruct((count // 2, width + LANES), jnp.bfloat16),
        ),
        in_specs=[SMEM, SMEM, VMEM, VMEM, VMEM],
        out_specs=(VMEM, VMEM),
        scratch_shapes=[pltpu.VMEM((count, LANES), jnp.float32)],
        name="prepare",
    )(attn_at.reshape(1), plan, slots.T, gates.T, tokens)


def ffn_kernel(experts, blocks, at_ref, *refs):
    x_refs = refs[:blocks]
    gate_ref, up_ref, down_ref, keep_ref, send_ref, x_ref, h_ref, w_ref = refs[blocks:]
    width, units = gate_ref.shape
    row = 0
    for ref in x_refs:
        size = ref.shape[0]
        x_ref[pl.ds(row, size), :] = ref[:, pl.ds(0, width)]
        w_ref[pl.ds(row, size), :] = ref[:, pl.ds(width, LANES)].astype(jnp.float32)
        row += size
    lane = lax.broadcasted_iota(jnp.int32, (1, LANES), 1)
    own = (lane == at_ref[0]) | (lane == at_ref[0] + experts)
    weight = jnp.sum(jnp.where(own, w_ref[...], 0.0), axis=1, keepdims=True)
    w_ref[...] = jnp.broadcast_to(weight, w_ref.shape)
    tile = min(256, units)
    for n in range(0, units, tile):
        cols = pl.ds(n, tile)
        gate = jnp.dot(x_ref[...], gate_ref[:, cols], preferred_element_type=jnp.float32)
        up = jnp.dot(x_ref[...], up_ref[:, cols], preferred_element_type=jnp.float32)
        h_ref[:, cols] = (gate / (1.0 + jnp.exp(-gate)) * up).astype(jnp.bfloat16)
    half = row // 2
    wide = 512

    def down(j, carry):
        cols = pl.ds(pl.multiple_of(j * wide, wide), wide)
        y = lax.dot_general(
            h_ref[...], down_ref[cols, :], (((1,), (1,)), ((), ())), preferred_element_type=jnp.float32
        )
        y = (y * w_ref[:, pl.ds(0, 1)]).astype(jnp.bfloat16)
        keep_ref[:, cols] = y[:half]
        send_ref[:, cols] = y[half:]
        return carry

    lax.fori_loop(0, width // wide, down, 0)


def ffn(x_blocks, w_gate, w_up, w_down, expert_at, experts):
    width, units = w_gate.shape
    rows = sum(b.shape[0] for b in x_blocks)
    out = jax.ShapeDtypeStruct((rows // 2, width), jnp.bfloat16)
    return pl.pallas_call(
        functools.partial(ffn_kernel, experts, len(x_blocks)),
        out_shape=(out, out),
        in_specs=[SMEM] + [VMEM] * (len(x_blocks) + 3),
        out_specs=(VMEM, VMEM),
        scratch_shapes=[
            pltpu.VMEM((rows, width), jnp.bfloat16),
            pltpu.VMEM((rows, units), jnp.bfloat16),
            pltpu.VMEM((rows, LANES), jnp.float32),
        ],
        cost_estimate=pl.CostEstimate(
            flops=6 * rows * width * units,
            bytes_accessed=6 * width * units + 8 * rows * width,
            transcendentals=rows * units,
        ),
        name="ffn",
    )(expert_at.reshape(1), *x_blocks, w_gate, w_up, w_down)


def add(*terms):
    total = terms[0].astype(jnp.float32)
    for term in terms[1:]:
        total = total + term.astype(jnp.float32)
    return total.astype(jnp.bfloat16)


def body_line(tokens, gates, slots, plan, gate_proj, up_proj, down_proj):
    experts = lax.axis_size("expert")
    expert_at = lax.axis_index("expert").astype(jnp.int32)
    attn_at = lax.axis_index("attn").astype(jnp.int32)
    half = tokens.shape[0] // 2

    def swap(value, bit):
        return lax.ppermute(value, "expert", [(i, i ^ bit) for i in range(experts)])

    def core(value):
        return swap(value, 1)

    def pair(value):
        return lax.ppermute(value, "attn", [(0, 1), (1, 0)])

    own, mine = prepare(tokens, gates, slots, plan, experts, attn_at)
    weights = (gate_proj[0], up_proj[0], down_proj[0])

    own_core = core(own)
    far = [swap(mine, 2 * k) for k in (3, 2)]
    near = swap(own, 2)
    near_core = core(near)
    far_rows = []
    for block in far:
        other = pair(block)
        far_rows.append(([block, other], [core(block), core(other)]))

    keep, send = ffn([own, near, own_core, near_core], *weights, expert_at, experts)
    count = 2 * half
    got = core(send)
    near_sum = swap(add(keep[count:], got[count:]), 2)
    both = add(keep[:count], got[:count], near_sum)
    terms = [both[:half], pair(both[half:])]
    for k, (kept, sent) in zip((3, 2), far_rows):
        keep, send = ffn(kept + sent, *weights, expert_at, experts)
        got = core(send)
        total = add(keep, got)
        part = add(total[:half], pair(total[half:]))
        terms.append(swap(part, 2 * k))
    final = add(*terms)
    other = pair(final)
    return jnp.where(
        attn_at == 0,
        jnp.concatenate([final, other], axis=0),
        jnp.concatenate([other, final], axis=0),
    )


def body_any(tokens, gates, slots, plan, gate_proj, up_proj, down_proj):
    experts = lax.axis_size("expert")
    expert_at = lax.axis_index("expert").astype(jnp.int32)
    owner = slots >> 1
    chosen = jnp.where((slots & 1) == 0, owner, plan[owner])
    hit = chosen[:, :, None] == jnp.arange(experts, dtype=jnp.int32)
    sums = jnp.sum(jnp.where(hit, gates[:, :, None], 0.0), axis=1)
    rows = lax.all_gather(tokens, "expert", axis=0, tiled=True)
    weight = lax.all_gather(sums, "expert", axis=0, tiled=True)
    weight = jnp.sum(
        jnp.where(jnp.arange(experts, dtype=jnp.int32) == expert_at, weight, 0.0), axis=1
    )
    gate = jnp.dot(rows, gate_proj[0], preferred_element_type=jnp.float32)
    up = jnp.dot(rows, up_proj[0], preferred_element_type=jnp.float32)
    hidden = (jax.nn.silu(gate) * up).astype(jnp.bfloat16)
    down = jnp.einsum("rf,df->rd", hidden, down_proj[0], preferred_element_type=jnp.float32)
    part = (down * weight[:, None]).astype(jnp.bfloat16)
    mine = lax.psum_scatter(part, "expert", scatter_dimension=0, tiled=True)
    return lax.psum(mine, "attn")


def solution(mesh):
    sizes = dict(mesh.shape)
    line = sizes["attn"] == 2 and sizes["expert"] == 8
    return jax.shard_map(
        body_line if line else body_any,
        mesh=mesh,
        in_specs=(
            P(("groups", "expert"), None),
            P(("groups", "expert"), None),
            P(("groups", "expert"), None),
            P("groups"),
            P("expert", None, "attn"),
            P("expert", None, "attn"),
            P("expert", None, "attn"),
        ),
        out_specs=P(("groups", "expert"), None),
        check_vma=False,
    )
```

time: 287 us -> 84.2 us (0.29)
  blocking collectives: 89.2 us -> 0 us
  waiting for transfers between devices: 104 us -> 29.1 us
  local copies, waits for them, and re-layouts: 49.7 us -> 3.35 us
  Pallas kernels: 0 us -> 27.8 us
  matrix products: 17.6 us -> 0 us
  starting transfers between devices: 4.85 us -> 20.7 us
  between operations: 13.6 us -> 0.13 us
  other arithmetic: 7.44 us -> 2.98 us
    all_to_all x1 -> x0, blocking collectives: 89.2 us -> none  [body(): lax.all_to_all(outgoing, 'expert', split_axis=0, concat_axis=0, tiled=True)]
    all_to_all x1 -> x0, waiting for transfers between devices: 82.1 us -> none  [body(): lax.all_to_all(results, 'expert', split_axis=0, concat_axis=0, tiled=True)]
    ppermute x0 -> x21, waiting for transfers between devices: none -> 29.1 us  [the longest x15 15.3 us: swap(): return lax.ppermute(value, 'expert', [(i, i ^ bit) for i in range(experts)])]
    gather x10 -> x0, local copies, waits for them, and re-layouts: 28.3 us -> none  [the longest x8 26.6 us: body(): returned[choice_rows[:, column]].astype(jnp.float32)]
    pallas_call x0 -> x4, Pallas kernels: none -> 27.8 us  [the longest x3 26 us: ffn(): pl.pallas_call(functools.partial(ffn_kernel, experts, len(x_blocks)), out...]
    psum x1 -> x0, waiting for transfers between devices: 21.9 us -> none  [body(): return lax.psum(partial_value.astype(jnp.bfloat16), 'attn')]
    ppermute x0 -> x21, starting transfers between devices: none -> 20.7 us  [the longest x15 12.3 us: swap(): return lax.ppermute(value, 'expert', [(i, i ^ bit) for i in range(experts)])]
    reshape x7 -> x0, local copies, waits for them, and re-layouts: 18.7 us -> none  [the longest x1 4.62 us: body(): results = results.reshape(experts, per_owner, model_width)]
  transfers between devices with their start and end apart: 2 -> 21, of which waited for: 2 -> 7; matrix products, arithmetic and copies ran while one was open for 0% -> 3% of each run, Pallas kernels for 0% -> 31%
where the time goes in v1:
time: 84.2 us; the launch traced here: 84.1 us
  waiting for transfers between devices  29.1 us (35%)
  Pallas kernels  27.8 us (33%)
  starting transfers between devices  20.7 us (25%)
  local copies, waits for them, and re-layouts  3.35 us (4%)
  other arithmetic  2.98 us (4%)
    pallas_call x3, Pallas kernels, ffn(): pl.pallas_call(functools.partial(ffn_kernel, experts, len(x_blocks)), out...  26 us
    ppermute x15, waiting for transfers between devices, swap(): return lax.ppermute(value, 'expert', [(i, i ^ bit) for i in range(experts)])  15.3 us
    ppermute x6, waiting for transfers between devices, pair(): return lax.ppermute(value, 'attn', [(0, 1), (1, 0)])  13.8 us
    ppermute x15, starting transfers between devices, swap(): return lax.ppermute(value, 'expert', [(i, i ^ bit) for i in range(experts)])  12.3 us
    ppermute x6, starting transfers between devices, pair(): return lax.ppermute(value, 'attn', [(0, 1), (1, 0)])  8.42 us
    unnamed x26, local copies, waits for them, and re-layouts  3.32 us
    convert_element_type x7, other arithmetic, add(): return total.astype(jnp.bfloat16)  2.26 us
    pallas_call x1, Pallas kernels, prepare(): pl.pallas_call(functools.partial(prepare_kernel, experts), out_shape=(jax...  1.82 us
  transfers between devices with their start and end apart: 21, of which 7 were waited for; matrix products, arithmetic and copies ran while one was open for 3% of the time, Pallas kernels for 31%

profile of v1, /device:TPU:0, one launch (start us, length us, event | category | flops | bytes accessed | tf_op | source)
XLA Modules:
  0.0 84.1 jit_solution(14410927418231757062)
XLA Ops:
  0.0 1.8 %prepare.1 = (bf16[32,3712]{1,0:T(8,128)(2,1)}, bf16[16,3712]{1,0:T(8,128)(2,1)}) custom-call(s32[1]{0:T(128)} %bitcast.1.at_ref, s32[8]{0:T(128)} %plan_ref.1, s32[8,32]{1,0:T(8,128)} %bitcast.16, f32[8,32]{1,0:T(8,128)} %bitcast.17, bf16[32,3584]{1,0:T(8,128)(2,1)} %tok_ref.1), custom_call_target="tpu_custom_call" | custom-call | tf_op jit(solution)/shard_map/prepare/pallas_call | solution.py:51
  1.8 5.1 %collective-permute-start.6 = (bf16[16,3712]{1,0:T(8,128)(2,1)}, bf16[16,3712]{1,0:T(8,128)(2,1)S(1)}, u32[]{:S(2)}, u32[]{:S(2)}) collective-permute-start(bf16[16,3712]{1,0:T(8,128)(2,1)} %get-tuple-element.16), channel_id=1, source_target_pairs={{0,12},{2,14},{4,8},{6,10},{8,4},{10,6},{12,0},{14,2},{1,13},{3,15... | collective-permute-start | bytes 356360 | tf_op jit(solution)/shard_map/ppermute | solution.py:137
  6.9 0.6 collective-permute-start.13
  7.5 3.8 %collective-permute-done.6.refs_0_ = bf16[16,3712]{1,0:T(8,128)(2,1)S(1)} collective-permute-done((bf16[16,3712]{1,0:T(8,128)(2,1)}, bf16[16,3712]{1,0:T(8,128)(2,1)S(1)}, u32[]{:S(2)}, u32[]{:S(2)}) %collective-permute-start.6) | collective-permute-done | bytes 118816 | tf_op jit(solution)/shard_map/ppermute | solution.py:137
  11.2 1.7 %collective-permute-start.7 = (bf16[16,3712]{1,0:T(8,128)(2,1)S(1)}, bf16[16,3712]{1,0:T(8,128)(2,1)S(1)}, u32[]{:S(2)}, u32[]{:S(2)}) collective-permute-start(bf16[16,3712]{1,0:T(8,128)(2,1)S(1)} %collective-permute-done.6.refs_0_), channel_id=1, source_target_pairs={{0,1},{1,0},{2,3},{3,2},{4,5},{5,4},{6,7},{7,6},{8,9},{9,8},{10,11... | collective-permute-start | bytes 356360 | tf_op jit(solution)/shard_map/ppermute | solution.py:143
  12.9 4.5 %collective-permute-done.13.refs_0_ = bf16[16,3712]{1,0:T(8,128)(2,1)S(1)} collective-permute-done((bf16[16,3712]{1,0:T(8,128)(2,1)}, bf16[16,3712]{1,0:T(8,128)(2,1)S(1)}, u32[]{:S(2)}, u32[]{:S(2)}) %collective-permute-start.13) | collective-permute-done | bytes 118816 | tf_op jit(solution)/shard_map/ppermute | solution.py:137
  17.4 1.5 %collective-permute-start.14 = (bf16[16,3712]{1,0:T(8,128)(2,1)S(1)}, bf16[16,3712]{1,0:T(8,128)(2,1)S(1)}, u32[]{:S(2)}, u32[]{:S(2)}) collective-permute-start(bf16[16,3712]{1,0:T(8,128)(2,1)S(1)} %collective-permute-done.13.refs_0_), channel_id=1, source_target_pairs={{0,1},{1,0},{2,3},{3,2},{4,5},{5,4},{6,7},{7,6},{8,9},{9,8},{10,11... | collective-permute-start | bytes 356360 | tf_op jit(solution)/shard_map/ppermute | solution.py:143
  18.9 0.5 collective-permute-start.1
  19.9 2.3 %collective-permute-done.14.refs_1_ = bf16[16,3712]{1,0:T(8,128)(2,1)S(1)} collective-permute-done((bf16[16,3712]{1,0:T(8,128)(2,1)S(1)}, bf16[16,3712]{1,0:T(8,128)(2,1)S(1)}, u32[]{:S(2)}, u32[]{:S(2)}) %collective-permute-start.14) | collective-permute-done | bytes 118816 | tf_op jit(solution)/shard_map/ppermute | solution.py:143
  22.3 0.6 copy-done.10
  22.9 8.6 %ffn.4 = (bf16[32,3584]{1,0:T(8,128)(2,1)}, bf16[32,3584]{1,0:T(8,128)(2,1)}) custom-call(s32[1]{0:T(128)} %bitcast.at_ref, bf16[16,3712]{1,0:T(8,128)(2,1)} %copy-done.6, bf16[16,3712]{1,0:T(8,128)(2,1)} %copy-done.8, bf16[16,3712]{1,0:T(8,128)(2,1)} %copy-done.9, bf16[16,3712]{1,0:T(8,128)(2,1)} %copy-done.10, bf16[3584,512]{1,0:T(8,128)(2,1)} %bitcast.7, ...), custom_call_target="tpu_custom_call" | custom-call | flops 704643072 | bytes 12845056 | tf_op jit(solution)/shard_map/ffn/pallas_call | solution.py:104
  31.5 0.5 collective-permute-start.10
  32.0 0.6 copy-done.11
  32.7 0.6 copy-done.12
  33.3 8.6 %ffn.5 = (bf16[32,3584]{1,0:T(8,128)(2,1)}, bf16[32,3584]{1,0:T(8,128)(2,1)}) custom-call(s32[1]{0:T(128)} %bitcast.at_ref, bf16[16,3712]{1,0:T(8,128)(2,1)} %copy-done.5, bf16[16,3712]{1,0:T(8,128)(2,1)} %copy-done.7, bf16[16,3712]{1,0:T(8,128)(2,1)} %copy-done.11, bf16[16,3712]{1,0:T(8,128)(2,1)} %copy-done.12, bf16[3584,512]{1,0:T(8,128)(2,1)} %bitcast.8, ...), custom_call_target="tpu_custom_call" | custom-call | flops 704643072 | bytes 12845056 | tf_op jit(solution)/shard_map/ffn/pallas_call | solution.py:104
  42.0 0.7 copy-done.1
  42.6 0.7 copy-done.2
  43.3 8.8 %ffn.3 = (bf16[64,3584]{1,0:T(8,128)(2,1)}, bf16[64,3584]{1,0:T(8,128)(2,1)}) custom-call(s32[1]{0:T(128)} %bitcast.at_ref, bf16[32,3712]{1,0:T(8,128)(2,1)} %get-tuple-element.13.refs_0_, bf16[32,3712]{1,0:T(8,128)(2,1)} %copy-done, bf16[32,3712]{1,0:T(8,128)(2,1)} %copy-done.1, bf16[32,3712]{1,0:T(8,128)(2,1)} %copy-done.2, bf16[3584,512]{1,0:T(8,128)(2,1)} %bitcast.9, ...), custom_call_target="tpu_custom_call" | custom-call | flops 1409286144 | bytes 14680064 | tf_op jit(solution)/shard_map/ffn/pallas_call | solution.py:104
  52.2 0.5 collective-permute-start.3
  52.7 1.6 %collective-permute-start.11 = (bf16[16,3584]{1,0:T(8,128)(2,1)S(1)}, bf16[16,3584]{1,0:T(8,128)(2,1)S(1)}, u32[]{:S(2)}, u32[]{:S(2)}) collective-permute-start(bf16[16,3584]{1,0:T(8,128)(2,1)S(1)} %slice.45), channel_id=1, source_target_pairs={{0,1},{1,0},{2,3},{3,2},{4,5},{5,4},{6,7},{7,6},{8,9},{9,8},{10,11... | collective-permute-start | bytes 344072 | tf_op jit(solution)/shard_map/ppermute | solution.py:143
  54.4 0.6 collective-permute-start.18
  55.0 3.8 %collective-permute-done.11 = bf16[16,3584]{1,0:T(8,128)(2,1)S(1)} collective-permute-done((bf16[16,3584]{1,0:T(8,128)(2,1)S(1)}, bf16[16,3584]{1,0:T(8,128)(2,1)S(1)}, u32[]{:S(2)}, u32[]{:S(2)}) %collective-permute-start.11) | collective-permute-done | bytes 114720 | tf_op jit(solution)/shard_map/ppermute | solution.py:143
  59.2 1.0 %add_convert_fusion.3 = bf16[32,3584]{1,0:T(8,128)(2,1)S(1)} fusion(bf16[64,3584]{1,0:T(8,128)(2,1)S(1)} %collective-permute-done.3, bf16[64,3584]{1,0:T(8,128)(2,1)} %get-tuple-element.14), kind=kLoop, calls=%fused_computation.3 | loop fusion | flops 458752 | bytes 688128 | tf_op jit(solution)/shard_map/convert_element_type | solution.py:127
  60.2 3.6 %collective-permute-start.4 = (bf16[32,3584]{1,0:T(8,128)(2,1)S(1)}, bf16[32,3584]{1,0:T(8,128)(2,1)S(1)}, u32[]{:S(2)}, u32[]{:S(2)}) collective-permute-start(bf16[32,3584]{1,0:T(8,128)(2,1)S(1)} %add_convert_fusion.3), channel_id=1, source_target_pairs={{0,4},{2,6},{4,0},{6,2},{8,12},{10,14},{12,8},{14,10},{1,5},{3,7},... | collective-permute-start | bytes 688136 | tf_op jit(solution)/shard_map/ppermute | solution.py:137
  63.9 0.6 collective-permute-start.19
  64.5 7.0 %collective-permute-done.4 = bf16[32,3584]{1,0:T(8,128)(2,1)S(1)} collective-permute-done((bf16[32,3584]{1,0:T(8,128)(2,1)S(1)}, bf16[32,3584]{1,0:T(8,128)(2,1)S(1)}, u32[]{:S(2)}, u32[]{:S(2)}) %collective-permute-start.4) | collective-permute-done | bytes 229408 | tf_op jit(solution)/shard_map/ppermute | solution.py:137
  71.5 1.0 %add_convert_fusion.2 = bf16[32,3584]{1,0:T(8,128)(2,1)S(1)} fusion(bf16[32,3584]{1,0:T(8,128)(2,1)S(1)} %collective-permute-done.4, bf16[64,3584]{1,0:T(8,128)(2,1)S(1)} %collective-permute-done.3, bf16[64,3584]{1,0:T(8,128)(2,1)} %get-tuple-element.14), kind=kLoop, calls=%fused_computation.2 | loop fusion | flops 688128 | bytes 917504 | tf_op jit(solution)/shard_map/convert_element_type | solution.py:127
  72.5 1.6 %collective-permute-start.5 = (bf16[16,3584]{1,0:T(8,128)(2,1)S(1)}, bf16[16,3584]{1,0:T(8,128)(2,1)S(1)}, u32[]{:S(2)}, u32[]{:S(2)}) collective-permute-start(bf16[16,3584]{1,0:T(8,128)(2,1)S(1)} %slice.43), channel_id=1, source_target_pairs={{0,1},{1,0},{2,3},{3,2},{4,5},{5,4},{6,7},{7,6},{8,9},{9,8},{10,11... | collective-permute-start | bytes 344072 | tf_op jit(solution)/shard_map/ppermute | solution.py:143
  74.1 4.3 %collective-permute-done.5 = bf16[16,3584]{1,0:T(8,128)(2,1)S(1)} collective-permute-done((bf16[16,3584]{1,0:T(8,128)(2,1)S(1)}, bf16[16,3584]{1,0:T(8,128)(2,1)S(1)}, u32[]{:S(2)}, u32[]{:S(2)}) %collective-permute-start.5) | collective-permute-done | bytes 114720 | tf_op jit(solution)/shard_map/ppermute | solution.py:143
  78.5 1.6 %collective-permute-start.20 = (bf16[16,3584]{1,0:T(8,128)(2,1)S(1)}, bf16[16,3584]{1,0:T(8,128)(2,1)S(1)}, u32[]{:S(2)}, u32[]{:S(2)}) collective-permute-start(bf16[16,3584]{1,0:T(8,128)(2,1)S(1)} %add_convert_fusion.4), channel_id=1, source_target_pairs={{0,1},{1,0},{2,3},{3,2},{4,5},{5,4},{6,7},{7,6},{8,9},{9,8},{10,11... | collective-permute-start | bytes 344072 | tf_op jit(solution)/shard_map/ppermute | solution.py:143
  80.0 3.3 %collective-permute-done.20 = bf16[16,3584]{1,0:T(8,128)(2,1)S(1)} collective-permute-done((bf16[16,3584]{1,0:T(8,128)(2,1)S(1)}, bf16[16,3584]{1,0:T(8,128)(2,1)S(1)}, u32[]{:S(2)}, u32[]{:S(2)}) %collective-permute-start.20) | collective-permute-done | bytes 114720 | tf_op jit(solution)/shard_map/ppermute | solution.py:143
  83.3 0.7 maximum_select_fusion
  (51 shorter events, 1.2 us)
Async XLA Ops:
  1.8 9.4 %collective-permute-start.6 = (bf16[16,3712]{1,0:T(8,128)(2,1)}, bf16[16,3712]{1,0:T(8,128)(2,1)S(1)}, u32[]{:S(2)}, u32[]{:S(2)}) collective-permute-start(bf16[16,3712]{1,0:T(8,128)(2,1)} %get-tuple-element.16), channel_id=1, source_target_pairs={{0,12},{2,14},{4,8},{6,10},{8,4},{10,6},{12,0},{14,2},{1,13},{3,15... | collective-permute-start | bytes 356360 | tf_op jit(solution)/shard_map/ppermute | solution.py:137
  6.9 12.5 %collective-permute-start = (bf16[32,3712]{1,0:T(8,128)(2,1)}, bf16[32,3712]{1,0:T(8,128)(2,1)S(1)}, u32[]{:S(2)}, u32[]{:S(2)}) collective-permute-start(bf16[32,3712]{1,0:T(8,128)(2,1)} %get-tuple-element.13.refs_0_), channel_id=1, source_target_pairs={{0,4},{2,6},{4,0},{6,2},{8,12},{10,14},{12,8},{14,10},{1,5},{3,7},... | collective-permute-start | bytes 712712 | tf_op jit(solution)/shard_map/ppermute | solution.py:137
  6.9 10.5 %collective-permute-start.13 = (bf16[16,3712]{1,0:T(8,128)(2,1)}, bf16[16,3712]{1,0:T(8,128)(2,1)S(1)}, u32[]{:S(2)}, u32[]{:S(2)}) collective-permute-start(bf16[16,3712]{1,0:T(8,128)(2,1)} %get-tuple-element.16), channel_id=1, source_target_pairs={{0,8},{2,10},{4,12},{6,14},{8,0},{10,2},{12,4},{14,6},{1,9},{3,11}... | collective-permute-start | bytes 356360 | tf_op jit(solution)/shard_map/ppermute | solution.py:137
  11.2 11.0 %copy-start.6 = (bf16[16,3712]{1,0:T(8,128)(2,1)}, bf16[16,3712]{1,0:T(8,128)(2,1)S(1)}, u32[]{:S(2)}) copy-start(bf16[16,3712]{1,0:T(8,128)(2,1)S(1)} %collective-permute-done.6.refs_0_) | copy-start | bytes 356356
  11.2 7.6 %collective-permute-start.7 = (bf16[16,3712]{1,0:T(8,128)(2,1)S(1)}, bf16[16,3712]{1,0:T(8,128)(2,1)S(1)}, u32[]{:S(2)}, u32[]{:S(2)}) collective-permute-start(bf16[16,3712]{1,0:T(8,128)(2,1)S(1)} %collective-permute-done.6.refs_0_), channel_id=1, source_target_pairs={{0,1},{1,0},{2,3},{3,2},{4,5},{5,4},{6,7},{7,6},{8,9},{9,8},{10,11... | collective-permute-start | bytes 356360 | tf_op jit(solution)/shard_map/ppermute | solution.py:143
  12.9 6.6 %collective-permute-start.8 = (bf16[16,3712]{1,0:T(8,128)(2,1)S(1)}, bf16[16,3712]{1,0:T(8,128)(2,1)S(1)}, u32[]{:S(2)}, u32[]{:S(2)}) collective-permute-start(bf16[16,3712]{1,0:T(8,128)(2,1)S(1)} %collective-permute-done.6.refs_0_), channel_id=1, source_target_pairs={{0,2},{2,0},{4,6},{6,4},{8,10},{10,8},{12,14},{14,12},{1,3},{3,1},... | collective-permute-start | bytes 356360 | tf_op jit(solution)/shard_map/ppermute | solution.py:137
  17.4 14.1 %copy-start.5 = (bf16[16,3712]{1,0:T(8,128)(2,1)}, bf16[16,3712]{1,0:T(8,128)(2,1)S(1)}, u32[]{:S(2)}) copy-start(bf16[16,3712]{1,0:T(8,128)(2,1)S(1)} %collective-permute-done.13.refs_0_) | copy-start | bytes 356356
  17.4 4.8 %collective-permute-start.14 = (bf16[16,3712]{1,0:T(8,128)(2,1)S(1)}, bf16[16,3712]{1,0:T(8,128)(2,1)S(1)}, u32[]{:S(2)}, u32[]{:S(2)}) collective-permute-start(bf16[16,3712]{1,0:T(8,128)(2,1)S(1)} %collective-permute-done.13.refs_0_), channel_id=1, source_target_pairs={{0,1},{1,0},{2,3},{3,2},{4,5},{5,4},{6,7},{7,6},{8,9},{9,8},{10,11... | collective-permute-start | bytes 356360 | tf_op jit(solution)/shard_map/ppermute | solution.py:143
  18.9 3.4 %copy-start.8 = (bf16[16,3712]{1,0:T(8,128)(2,1)}, bf16[16,3712]{1,0:T(8,128)(2,1)S(1)}, u32[]{:S(2)}) copy-start(bf16[16,3712]{1,0:T(8,128)(2,1)S(1)} %collective-permute-done.7.refs_1_) | copy-start | bytes 356356
  18.9 3.3 %collective-permute-start.9 = (bf16[16,3712]{1,0:T(8,128)(2,1)S(1)}, bf16[16,3712]{1,0:T(8,128)(2,1)S(1)}, u32[]{:S(2)}, u32[]{:S(2)}) collective-permute-start(bf16[16,3712]{1,0:T(8,128)(2,1)S(1)} %collective-permute-done.7.refs_1_), channel_id=1, source_target_pairs={{0,2},{2,0},{4,6},{6,4},{8,10},{10,8},{12,14},{14,12},{1,3},{3,1},... | collective-permute-start | bytes 356360 | tf_op jit(solution)/shard_map/ppermute | solution.py:137
  18.9 23.0 %collective-permute-start.1 = (bf16[32,3712]{1,0:T(8,128)(2,1)}, bf16[32,3712]{1,0:T(8,128)(2,1)S(1)}, u32[]{:S(2)}, u32[]{:S(2)}) collective-permute-start(bf16[32,3712]{1,0:T(8,128)(2,1)} %get-tuple-element.13.refs_0_), channel_id=1, source_target_pairs={{0,2},{2,0},{4,6},{6,4},{8,10},{10,8},{12,14},{14,12},{1,3},{3,1},... | collective-permute-start | bytes 712712 | tf_op jit(solution)/shard_map/ppermute | solution.py:137
  19.4 12.1 %copy-start = (bf16[32,3712]{1,0:T(8,128)(2,1)}, bf16[32,3712]{1,0:T(8,128)(2,1)S(1)}, u32[]{:S(2)}) copy-start(bf16[32,3712]{1,0:T(8,128)(2,1)S(1)} %collective-permute-done.refs_1_) | copy-start | bytes 712708
  19.4 22.5 %collective-permute-start.2 = (bf16[32,3712]{1,0:T(8,128)(2,1)S(1)}, bf16[32,3712]{1,0:T(8,128)(2,1)S(1)}, u32[]{:S(2)}, u32[]{:S(2)}) collective-permute-start(bf16[32,3712]{1,0:T(8,128)(2,1)S(1)} %collective-permute-done.refs_1_), channel_id=1, source_target_pairs={{0,2},{2,0},{4,6},{6,4},{8,10},{10,8},{12,14},{14,12},{1,3},{3,1},... | collective-permute-start | bytes 712712 | tf_op jit(solution)/shard_map/ppermute | solution.py:137
  19.5 2.8 %copy-start.9 = (bf16[16,3712]{1,0:T(8,128)(2,1)}, bf16[16,3712]{1,0:T(8,128)(2,1)S(1)}, u32[]{:S(2)}) copy-start(bf16[16,3712]{1,0:T(8,128)(2,1)S(1)} %collective-permute-done.8.refs_2_) | copy-start | bytes 356356
  19.5 12.5 %collective-permute-start.15 = (bf16[16,3712]{1,0:T(8,128)(2,1)S(1)}, bf16[16,3712]{1,0:T(8,128)(2,1)S(1)}, u32[]{:S(2)}, u32[]{:S(2)}) collective-permute-start(bf16[16,3712]{1,0:T(8,128)(2,1)S(1)} %collective-permute-done.13.refs_0_), channel_id=1, source_target_pairs={{0,2},{2,0},{4,6},{6,4},{8,10},{10,8},{12,14},{14,12},{1,3},{3,1},... | collective-permute-start | bytes 356360 | tf_op jit(solution)/shard_map/ppermute | solution.py:137
  22.2 9.3 %copy-start.7 = (bf16[16,3712]{1,0:T(8,128)(2,1)}, bf16[16,3712]{1,0:T(8,128)(2,1)S(1)}, u32[]{:S(2)}) copy-start(bf16[16,3712]{1,0:T(8,128)(2,1)S(1)} %collective-permute-done.14.refs_1_) | copy-start | bytes 356356
  22.2 9.8 %collective-permute-start.16 = (bf16[16,3712]{1,0:T(8,128)(2,1)S(1)}, bf16[16,3712]{1,0:T(8,128)(2,1)S(1)}, u32[]{:S(2)}, u32[]{:S(2)}) collective-permute-start(bf16[16,3712]{1,0:T(8,128)(2,1)S(1)} %collective-permute-done.14.refs_1_), channel_id=1, source_target_pairs={{0,2},{2,0},{4,6},{6,4},{8,10},{10,8},{12,14},{14,12},{1,3},{3,1},... | collective-permute-start | bytes 356360 | tf_op jit(solution)/shard_map/ppermute | solution.py:137
  22.2 0.7 copy-start.10
  31.5 21.2 %collective-permute-start.10 = (bf16[32,3584]{1,0:T(8,128)(2,1)}, bf16[32,3584]{1,0:T(8,128)(2,1)S(1)}, u32[]{:S(2)}, u32[]{:S(2)}) collective-permute-start(bf16[32,3584]{1,0:T(8,128)(2,1)} %get-tuple-element.18), channel_id=1, source_target_pairs={{0,2},{2,0},{4,6},{6,4},{8,10},{10,8},{12,14},{14,12},{1,3},{3,1},... | collective-permute-start | bytes 688136 | tf_op jit(solution)/shard_map/ppermute | solution.py:137
  41.9 10.8 %copy-start.3 = (bf16[32,3584]{1,0:T(8,128)(2,1)S(1)}, bf16[32,3584]{1,0:T(8,128)(2,1)}, u32[]{:S(2)}) copy-start(bf16[32,3584]{1,0:T(8,128)(2,1)} %get-tuple-element.17) | copy-start | bytes 688132
  41.9 12.4 %copy-start.4 = (bf16[32,3584]{1,0:T(8,128)(2,1)S(1)}, bf16[32,3584]{1,0:T(8,128)(2,1)}, u32[]{:S(2)}) copy-start(bf16[32,3584]{1,0:T(8,128)(2,1)} %get-tuple-element.19) | copy-start | bytes 688132
  41.9 12.4 %collective-permute-start.17 = (bf16[32,3584]{1,0:T(8,128)(2,1)}, bf16[32,3584]{1,0:T(8,128)(2,1)S(1)}, u32[]{:S(2)}, u32[]{:S(2)}) collective-permute-start(bf16[32,3584]{1,0:T(8,128)(2,1)} %get-tuple-element.20), channel_id=1, source_target_pairs={{0,2},{2,0},{4,6},{6,4},{8,10},{10,8},{12,14},{14,12},{1,3},{3,1},... | collective-permute-start | bytes 688136 | tf_op jit(solution)/shard_map/ppermute | solution.py:137
  41.9 0.7 copy-start.1
  42.6 0.7 copy-start.2
  52.2 7.0 %collective-permute-start.3 = (bf16[64,3584]{1,0:T(8,128)(2,1)}, bf16[64,3584]{1,0:T(8,128)(2,1)S(1)}, u32[]{:S(2)}, u32[]{:S(2)}) collective-permute-start(bf16[64,3584]{1,0:T(8,128)(2,1)} %get-tuple-element.15), channel_id=1, source_target_pairs={{0,2},{2,0},{4,6},{6,4},{8,10},{10,8},{12,14},{14,12},{1,3},{3,1},... | collective-permute-start | bytes 1376264 | tf_op jit(solution)/shard_map/ppermute | solution.py:137
  52.7 6.1 %collective-permute-start.11 = (bf16[16,3584]{1,0:T(8,128)(2,1)S(1)}, bf16[16,3584]{1,0:T(8,128)(2,1)S(1)}, u32[]{:S(2)}, u32[]{:S(2)}) collective-permute-start(bf16[16,3584]{1,0:T(8,128)(2,1)S(1)} %slice.45), channel_id=1, source_target_pairs={{0,1},{1,0},{2,3},{3,2},{4,5},{5,4},{6,7},{7,6},{8,9},{9,8},{10,11... | collective-permute-start | bytes 344072 | tf_op jit(solution)/shard_map/ppermute | solution.py:143
  54.4 9.5 %collective-permute-start.18 = (bf16[16,3584]{1,0:T(8,128)(2,1)S(1)}, bf16[16,3584]{1,0:T(8,128)(2,1)S(1)}, u32[]{:S(2)}, u32[]{:S(2)}) collective-permute-start(bf16[16,3584]{1,0:T(8,128)(2,1)S(1)} %slice.47), channel_id=1, source_target_pairs={{0,1},{1,0},{2,3},{3,2},{4,5},{5,4},{6,7},{7,6},{8,9},{9,8},{10,11... | collective-permute-start | bytes 344072 | tf_op jit(solution)/shard_map/ppermute | solution.py:143
  58.8 15.2 %collective-permute-start.12 = (bf16[16,3584]{1,0:T(8,128)(2,1)S(1)}, bf16[16,3584]{1,0:T(8,128)(2,1)S(1)}, u32[]{:S(2)}, u32[]{:S(2)}) collective-permute-start(bf16[16,3584]{1,0:T(8,128)(2,1)S(1)} %add_convert_fusion.6), channel_id=1, source_target_pairs={{0,12},{2,14},{4,8},{6,10},{8,4},{10,6},{12,0},{14,2},{1,13},{3,15... | collective-permute-start | bytes 344072 | tf_op jit(solution)/shard_map/ppermute | solution.py:137
  60.2 11.3 %collective-permute-start.4 = (bf16[32,3584]{1,0:T(8,128)(2,1)S(1)}, bf16[32,3584]{1,0:T(8,128)(2,1)S(1)}, u32[]{:S(2)}, u32[]{:S(2)}) collective-permute-start(bf16[32,3584]{1,0:T(8,128)(2,1)S(1)} %add_convert_fusion.3), channel_id=1, source_target_pairs={{0,4},{2,6},{4,0},{6,2},{8,12},{10,14},{12,8},{14,10},{1,5},{3,7},... | collective-permute-start | bytes 688136 | tf_op jit(solution)/shard_map/ppermute | solution.py:137
  63.9 10.2 %collective-permute-start.19 = (bf16[16,3584]{1,0:T(8,128)(2,1)S(1)}, bf16[16,3584]{1,0:T(8,128)(2,1)S(1)}, u32[]{:S(2)}, u32[]{:S(2)}) collective-permute-start(bf16[16,3584]{1,0:T(8,128)(2,1)S(1)} %add_convert_fusion.5), channel_id=1, source_target_pairs={{0,8},{2,10},{4,12},{6,14},{8,0},{10,2},{12,4},{14,6},{1,9},{3,11}... | collective-permute-start | bytes 344072 | tf_op jit(solution)/shard_map/ppermute | solution.py:137
  72.5 5.9 %collective-permute-start.5 = (bf16[16,3584]{1,0:T(8,128)(2,1)S(1)}, bf16[16,3584]{1,0:T(8,128)(2,1)S(1)}, u32[]{:S(2)}, u32[]{:S(2)}) collective-permute-start(bf16[16,3584]{1,0:T(8,128)(2,1)S(1)} %slice.43), channel_id=1, source_target_pairs={{0,1},{1,0},{2,3},{3,2},{4,5},{5,4},{6,7},{7,6},{8,9},{9,8},{10,11... | collective-permute-start | bytes 344072 | tf_op jit(solution)/shard_map/ppermute | solution.py:143
  78.5 4.9 %collective-permute-start.20 = (bf16[16,3584]{1,0:T(8,128)(2,1)S(1)}, bf16[16,3584]{1,0:T(8,128)(2,1)S(1)}, u32[]{:S(2)}, u32[]{:S(2)}) collective-permute-start(bf16[16,3584]{1,0:T(8,128)(2,1)S(1)} %add_convert_fusion.4), channel_id=1, source_target_pairs={{0,1},{1,0},{2,3},{3,2},{4,5},{5,4},{6,7},{7,6},{8,9},{9,8},{10,11... | collective-permute-start | bytes 344072 | tf_op jit(solution)/shard_map/ppermute | solution.py:143
  (2 other events, 1.3 us)

commit v2 on v1

--- a/solution.py
+++ b/solution.py
@@ -8,6 +8,7 @@
 from jax.sharding import PartitionSpec as P
 
 LANES = 128
+SMALL = 4 << 20
 VMEM = pl.BlockSpec(memory_space=pltpu.VMEM)
 SMEM = pl.BlockSpec(memory_space=pltpu.SMEM)
 
@@ -24,9 +25,29 @@
     ]
 
 
-def prepare_kernel(experts, at_ref, plan_ref, slots_ref, gates_ref, tok_ref, all_ref, mine_ref, w_ref):
-    count, width = tok_ref.shape
+def prepare_kernel(
+    experts, at_ref, expert_ref, plan_hbm, slots_hbm, gates_hbm, tok_hbm, all_ref, mine_ref,
+    plan_ref, slots_ref, gates_ref, w_ref, sems
+):
+    count, width = tok_hbm.shape
     half = count // 2
+    copies = [
+        pltpu.make_async_copy(plan_hbm, plan_ref, sems.at[0]),
+        pltpu.make_async_copy(slots_hbm, slots_ref, sems.at[1]),
+        pltpu.make_async_copy(gates_hbm, gates_ref, sems.at[2]),
+    ]
+    starts = [pl.multiple_of((at_ref[0] ^ place) * half, half) for place in range(2)]
+    targets = [
+        (starts[0], mine_ref.at[:, pl.ds(0, width)]),
+        (starts[0], all_ref.at[pl.ds(0, half), pl.ds(0, width)]),
+        (starts[1], all_ref.at[pl.ds(half, half), pl.ds(0, width)]),
+    ]
+    for i, (start, target) in enumerate(targets):
+        copies.append(pltpu.make_async_copy(tok_hbm.at[pl.ds(start, half), :], target, sems.at[3 + i]))
+    for copy in copies:
+        copy.start()
+    for copy in copies[:3]:
+        copy.wait()
     sums = expert_weights(slots_ref[...], gates_ref[...], plan_ref, experts)
     high = [s.astype(jnp.bfloat16).astype(jnp.float32) for s in sums]
     low = [s - h for s, h in zip(sums, high)]
@@ -35,30 +56,64 @@
     table = jnp.concatenate([table, jnp.zeros((LANES, LANES - count), jnp.float32)], axis=1)
     w_ref[...] = table.T[:count]
     for place in range(2):
-        start = pl.multiple_of((at_ref[0] ^ place) * half, half)
-        rows = tok_ref[pl.ds(start, half), :]
-        weights = w_ref[pl.ds(start, half), :].astype(jnp.bfloat16)
-        here = pl.ds(place * half, half)
-        all_ref[here, pl.ds(0, width)] = rows
-        all_ref[here, pl.ds(width, LANES)] = weights
+        weights = w_ref[pl.ds(starts[place], half), :].astype(jnp.bfloat16)
+        all_ref[pl.ds(place * half, half), pl.ds(width, LANES)] = weights
         if place == 0:
-            mine_ref[:, pl.ds(0, width)] = rows
             mine_ref[:, pl.ds(width, LANES)] = weights
-
-
-def prepare(tokens, gates, slots, plan, experts, attn_at):
+    for copy in copies[3:]:
+        copy.wait()
+
+
+def prepare(tokens, gates, slots, plan, experts, attn_at, expert_at):
     count, width = tokens.shape
+    top = slots.shape[1]
+    given = [pltpu.with_memory_space_constraint(v, pltpu.HBM) for v in (plan, slots.T, gates.T, tokens)]
     return pl.pallas_call(
         functools.partial(prepare_kernel, experts),
         out_shape=(
             jax.ShapeDtypeStruct((count, width + LANES), jnp.bfloat16),
             jax.ShapeDtypeStruct((count // 2, width + LANES), jnp.bfloat16),
         ),
-        in_specs=[SMEM, SMEM, VMEM, VMEM, VMEM],
+        in_specs=[SMEM] * 2 + [pl.BlockSpec(memory_space=pltpu.HBM)] * 4,
         out_specs=(VMEM, VMEM),
-        scratch_shapes=[pltpu.VMEM((count, LANES), jnp.float32)],
+        scratch_shapes=[
+            pltpu.SMEM((experts,), jnp.int32),
+            pltpu.VMEM((top, count), jnp.int32),
+            pltpu.VMEM((top, count), jnp.float32),
+            pltpu.VMEM((count, LANES), jnp.float32),
+            pltpu.SemaphoreType.DMA((6,)),
+        ],
+        compiler_params=pltpu.CompilerParams(vmem_limit_bytes=SMALL),
         name="prepare",
-    )(attn_at.reshape(1), plan, slots.T, gates.T, tokens)
+    )(attn_at.reshape(1), expert_at.reshape(1), *given)
+
+
+def load_kernel(*refs):
+    count = len(refs) // 2
+    sources, targets, sems = refs[:count], refs[count : 2 * count], refs[-1]
+    copies = [
+        pltpu.make_async_copy(source, target, sems.at[i])
+        for i, (source, target) in enumerate(zip(sources, targets))
+    ]
+    for copy in copies:
+        copy.start()
+    for copy in copies:
+        copy.wait()
+
+
+def load(*arrays):
+    return pl.pallas_call(
+        load_kernel,
+        out_shape=tuple(jax.ShapeDtypeStruct(a.shape, a.dtype) for a in arrays),
+        in_specs=[pl.BlockSpec(memory_space=pltpu.HBM)] * len(arrays),
+        out_specs=(VMEM,) * len(arrays),
+        scratch_shapes=[pltpu.SemaphoreType.DMA((len(arrays),))],
+        compiler_params=pltpu.CompilerParams(vmem_limit_bytes=SMALL),
+        cost_estimate=pl.CostEstimate(
+            flops=0, transcendentals=0, bytes_accessed=sum(2 * a.size * a.dtype.itemsize for a in arrays)
+        ),
+        name="load",
+    )(*[pltpu.with_memory_space_constraint(a, pltpu.HBM) for a in arrays])
 
 
 def ffn_kernel(experts, blocks, at_ref, *refs):
@@ -116,6 +171,7 @@
             bytes_accessed=6 * width * units + 8 * rows * width,
             transcendentals=rows * units,
         ),
+        compiler_params=pltpu.CompilerParams(vmem_limit_bytes=2 * SMALL),
         name="ffn",
     )(expert_at.reshape(1), *x_blocks, w_gate, w_up, w_down)
 
@@ -128,10 +184,15 @@
 
 
 def body_line(tokens, gates, slots, plan, gate_proj, up_proj, down_proj):
+    return line(tokens, gates, slots, plan, gate_proj, up_proj, down_proj)
+
+
+def line(tokens, gates, slots, plan, gate_proj, up_proj, down_proj):
     experts = lax.axis_size("expert")
     expert_at = lax.axis_index("expert").astype(jnp.int32)
     attn_at = lax.axis_index("attn").astype(jnp.int32)
-    half = tokens.shape[0] // 2
+    count = tokens.shape[0]
+    half = count // 2
 
     def swap(value, bit):
         return lax.ppermute(value, "expert", [(i, i ^ bit) for i in range(experts)])
@@ -142,31 +203,39 @@
     def pair(value):
         return lax.ppermute(value, "attn", [(0, 1), (1, 0)])
 
-    own, mine = prepare(tokens, gates, slots, plan, experts, attn_at)
-    weights = (gate_proj[0], up_proj[0], down_proj[0])
-
+    def run(*blocks):
+        return ffn(blocks, *weights, expert_at, experts)
+
+    own, mine = prepare(tokens, gates, slots, plan, experts, attn_at, expert_at)
+    far = swap(mine, 4)
+    near = swap(own, 2)
     own_core = core(own)
-    far = [swap(mine, 2 * k) for k in (3, 2)]
-    near = swap(own, 2)
+    weights = load(gate_proj[0], up_proj[0], down_proj[0])
+
+    relay = swap(far, 2)
+    far_pair = pair(far)
+    far_core = core(far)
     near_core = core(near)
-    far_rows = []
-    for block in far:
-        other = pair(block)
-        far_rows.append(([block, other], [core(block), core(other)]))
-
-    keep, send = ffn([own, near, own_core, near_core], *weights, expert_at, experts)
-    count = 2 * half
+    keep, send = run(own, near, own_core, near_core)
     got = core(send)
+    relay_pair = pair(relay)
+    relay_core = core(relay)
+    far_pair_core = core(far_pair)
+    far_keep, far_send = run(far, far_pair, far_core, far_pair_core)
+    far_got = core(far_send)
     near_sum = swap(add(keep[count:], got[count:]), 2)
+    relay_pair_core = core(relay_pair)
+    far_total = add(far_keep, far_got)
+    far_other = pair(far_total[half:])
+    relay_keep, relay_send = run(relay, relay_pair, relay_core, relay_pair_core)
+    relay_got = core(relay_send)
+    relay_total = add(relay_keep, relay_got)
+    relay_other = pair(relay_total[half:])
+    relay_sum = swap(add(relay_total[:half], relay_other), 2)
+    far_sum = swap(add(far_total[:half], far_other, relay_sum), 4)
     both = add(keep[:count], got[:count], near_sum)
-    terms = [both[:half], pair(both[half:])]
-    for k, (kept, sent) in zip((3, 2), far_rows):
-        keep, send = ffn(kept + sent, *weights, expert_at, experts)
-        got = core(send)
-        total = add(keep, got)
-        part = add(total[:half], pair(total[half:]))
-        terms.append(swap(part, 2 * k))
-    final = add(*terms)
+    near_other = pair(both[half:])
+    final = add(both[:half], near_other, far_sum)
     other = pair(final)
     return jnp.where(
         attn_at == 0,
@@ -198,9 +267,9 @@
 
 def solution(mesh):
     sizes = dict(mesh.shape)
-    line = sizes["attn"] == 2 and sizes["expert"] == 8
+    line_form = sizes["attn"] == 2 and sizes["expert"] == 8
     return jax.shard_map(
-        body_line if line else body_any,
+        body_line if line_form else body_any,
         mesh=mesh,
         in_specs=(
             P(("groups", "expert"), None),

time: 84.2 us -> 66.5 us (0.79)
  Pallas kernels: 27.8 us -> 15.5 us
  local copies, waits for them, and re-layouts: 3.35 us -> 0.03 us
  other arithmetic: 2.98 us -> 1.1 us
  starting transfers between devices: 20.7 us -> 19.1 us
  waiting for transfers between devices: 29.1 us -> 30.5 us
    pallas_call x3, Pallas kernels: 26 us -> 10.2 us  [ffn(): pl.pallas_call(functools.partial(ffn_kernel, experts, len(x_blocks)), out...]
    pallas_call x0 -> x1, Pallas kernels: none -> 4.23 us  [load(): pl.pallas_call(load_kernel, out_shape=tuple((jax.ShapeDtypeStruct(a.shape...]
    unnamed x26 -> x0, local copies, waits for them, and re-layouts: 3.32 us -> none
    ppermute x15, waiting for transfers between devices: 15.3 us -> 17.9 us  [swap(): return lax.ppermute(value, 'expert', [(i, i ^ bit) for i in range(experts)])]
    convert_element_type x7, other arithmetic: 2.26 us -> 0.37 us  [add(): return total.astype(jnp.bfloat16)]
    ppermute x6, starting transfers between devices: 8.42 us -> 6.87 us  [pair(): return lax.ppermute(value, 'attn', [(0, 1), (1, 0)])]
    ppermute x6, waiting for transfers between devices: 13.8 us -> 12.6 us  [pair(): return lax.ppermute(value, 'attn', [(0, 1), (1, 0)])]
  transfers between devices with their start and end apart: 21 -> 21, of which waited for: 7 -> 10; matrix products, arithmetic and copies ran while one was open for 3% -> 1% of each run, Pallas kernels for 31% -> 22%
where the time goes in v2:
time: 66.5 us; the launch traced here: 66.4 us
  waiting for transfers between devices  30.5 us (46%)
  starting transfers between devices  19.1 us (29%)
  Pallas kernels  15.5 us (23%)
  other arithmetic  1.1 us (2%)
    ppermute x15, waiting for transfers between devices, swap(): return lax.ppermute(value, 'expert', [(i, i ^ bit) for i in range(experts)])  17.9 us
    ppermute x6, waiting for transfers between devices, pair(): return lax.ppermute(value, 'attn', [(0, 1), (1, 0)])  12.6 us
    ppermute x15, starting transfers between devices, swap(): return lax.ppermute(value, 'expert', [(i, i ^ bit) for i in range(experts)])  12.3 us
    pallas_call x3, Pallas kernels, ffn(): pl.pallas_call(functools.partial(ffn_kernel, experts, len(x_blocks)), out...  10.2 us
    ppermute x6, starting transfers between devices, pair(): return lax.ppermute(value, 'attn', [(0, 1), (1, 0)])  6.87 us
    pallas_call x1, Pallas kernels, load(): pl.pallas_call(load_kernel, out_shape=tuple((jax.ShapeDtypeStruct(a.shape...  4.23 us
  transfers between devices with their start and end apart: 21, of which 10 were waited for; matrix products, arithmetic and copies ran while one was open for 1% of the time, Pallas kernels for 22%

profile of v2, /device:TPU:0, one launch (start us, length us, event | category | flops | bytes accessed | tf_op | source)
XLA Modules:
  0.0 66.4 jit_solution(344923805339691331)
XLA Ops:
  0.0 1.1 %prepare.1 = (bf16[32,3712]{1,0:T(8,128)(2,1)S(1)}, bf16[16,3712]{1,0:T(8,128)(2,1)S(1)}) custom-call(s32[1]{0:T(128)} %bitcast.1.at_ref, s32[1]{0:T(128)} %bitcast.expert_ref.at_ref, s32[8]{0:T(128)} %plan_hbm.1, s32[8,32]{1,0:T(8,128)} %bitcast.10, f32[8,32]{1,0:T(8,128)} %bitcast.11, bf16[32,3584]{1,0:T(8,128)(2,1)} %tok_hbm.1), custom_call_target="tpu_custom_call" | custom-call | tf_op jit(solution)/shard_map/prepare/pallas_call | solution.py:71
  1.1 4.1 %collective-permute-start.6 = (bf16[16,3712]{1,0:T(8,128)(2,1)S(1)}, bf16[16,3712]{1,0:T(8,128)(2,1)S(1)}, u32[]{:S(2)}, u32[]{:S(2)}) collective-permute-start(bf16[16,3712]{1,0:T(8,128)(2,1)S(1)} %get-tuple-element.22), channel_id=1, source_target_pairs={{0,8},{2,10},{4,12},{6,14},{8,0},{10,2},{12,4},{14,6},{1,9},{3,11}... | collective-permute-start | bytes 356360 | tf_op jit(solution)/shard_map/ppermute | solution.py:198
  5.2 5.8 %collective-permute-done.6.refs_0_ = bf16[16,3712]{1,0:T(8,128)(2,1)S(1)} collective-permute-done((bf16[16,3712]{1,0:T(8,128)(2,1)S(1)}, bf16[16,3712]{1,0:T(8,128)(2,1)S(1)}, u32[]{:S(2)}, u32[]{:S(2)}) %collective-permute-start.6) | collective-permute-done | bytes 118816 | tf_op jit(solution)/shard_map/ppermute | solution.py:198
  11.0 0.7 %collective-permute-start.12 = (bf16[16,3712]{1,0:T(8,128)(2,1)S(1)}, bf16[16,3712]{1,0:T(8,128)(2,1)S(1)}, u32[]{:S(2)}, u32[]{:S(2)}) collective-permute-start(bf16[16,3712]{1,0:T(8,128)(2,1)S(1)} %collective-permute-done.6.refs_0_), channel_id=1, source_target_pairs={{0,4},{2,6},{4,0},{6,2},{8,12},{10,14},{12,8},{14,10},{1,5},{3,7},... | collective-permute-start | bytes 356360 | tf_op jit(solution)/shard_map/ppermute | solution.py:198
  11.7 1.3 %collective-permute-start = (bf16[32,3712]{1,0:T(8,128)(2,1)S(1)}, bf16[32,3712]{1,0:T(8,128)(2,1)S(1)}, u32[]{:S(2)}, u32[]{:S(2)}) collective-permute-start(bf16[32,3712]{1,0:T(8,128)(2,1)S(1)} %get-tuple-element.16.refs_0_), channel_id=1, source_target_pairs={{0,4},{2,6},{4,0},{6,2},{8,12},{10,14},{12,8},{14,10},{1,5},{3,7},... | collective-permute-start | bytes 712712 | tf_op jit(solution)/shard_map/ppermute | solution.py:198
  13.0 4.1 %collective-permute-done.12.refs_0_ = bf16[16,3712]{1,0:T(8,128)(2,1)S(1)} collective-permute-done((bf16[16,3712]{1,0:T(8,128)(2,1)S(1)}, bf16[16,3712]{1,0:T(8,128)(2,1)S(1)}, u32[]{:S(2)}, u32[]{:S(2)}) %collective-permute-start.12) | collective-permute-done | bytes 118816 | tf_op jit(solution)/shard_map/ppermute | solution.py:198
  17.1 1.5 %collective-permute-start.13 = (bf16[16,3712]{1,0:T(8,128)(2,1)S(1)}, bf16[16,3712]{1,0:T(8,128)(2,1)S(1)}, u32[]{:S(2)}, u32[]{:S(2)}) collective-permute-start(bf16[16,3712]{1,0:T(8,128)(2,1)S(1)} %collective-permute-done.12.refs_0_), channel_id=1, source_target_pairs={{0,1},{1,0},{2,3},{3,2},{4,5},{5,4},{6,7},{7,6},{8,9},{9,8},{10,11... | collective-permute-start | bytes 356360 | tf_op jit(solution)/shard_map/ppermute | solution.py:204
  18.7 0.5 collective-permute-start.7
  19.1 2.8 %collective-permute-done.13.refs_1_ = bf16[16,3712]{1,0:T(8,128)(2,1)S(1)} collective-permute-done((bf16[16,3712]{1,0:T(8,128)(2,1)S(1)}, bf16[16,3712]{1,0:T(8,128)(2,1)S(1)}, u32[]{:S(2)}, u32[]{:S(2)}) %collective-permute-start.13) | collective-permute-done | bytes 118816 | tf_op jit(solution)/shard_map/ppermute | solution.py:204
  22.0 0.5 collective-permute-start.1
  22.5 1.0 %collective-permute-done.7.refs_1_ = bf16[16,3712]{1,0:T(8,128)(2,1)S(1)} collective-permute-done((bf16[16,3712]{1,0:T(8,128)(2,1)S(1)}, bf16[16,3712]{1,0:T(8,128)(2,1)S(1)}, u32[]{:S(2)}, u32[]{:S(2)}) %collective-permute-start.7) | collective-permute-done | bytes 118816 | tf_op jit(solution)/shard_map/ppermute | solution.py:204
  23.5 0.5 collective-permute-start.9
  24.0 4.2 %load.1 = (bf16[3584,512]{1,0:T(8,128)(2,1)S(1)}, bf16[3584,512]{1,0:T(8,128)(2,1)S(1)}, bf16[3584,512]{1,0:T(8,128)(2,1)S(1)}) custom-call(bf16[3584,512]{1,0:T(8,128)(2,1)} %bitcast.7, bf16[3584,512]{1,0:T(8,128)(2,1)} %bitcast.8, bf16[3584,512]{1,0:T(8,128)(2,1)} %bitcast.9), custom_call_target="tpu_custom_call" | custom-call | bytes 22020096 | tf_op jit(solution)/shard_map/load/pallas_call | solution.py:105
  28.3 3.4 %ffn.5 = (bf16[32,3584]{1,0:T(8,128)(2,1)S(1)}, bf16[32,3584]{1,0:T(8,128)(2,1)S(1)}) custom-call(s32[1]{0:T(128)} %bitcast.expert_ref.at_ref, bf16[16,3712]{1,0:T(8,128)(2,1)S(1)} %collective-permute-done.12.refs_0_, bf16[16,3712]{1,0:T(8,128)(2,1)S(1)} %collective-permute-done.13.refs_1_, bf16[16,3712]{1,0:T(8,128)(2,1)S(1)} %collective-permute-done.14.refs_2_, ...), custom_call_target="tpu_custom_call" | custom-call | flops 704643072 | bytes 12845056 | tf_op jit(solution)/shard_map/ffn/pallas_call | solution.py:159
  31.8 3.4 %ffn.4 = (bf16[32,3584]{1,0:T(8,128)(2,1)S(1)}, bf16[32,3584]{1,0:T(8,128)(2,1)S(1)}) custom-call(s32[1]{0:T(128)} %bitcast.expert_ref.at_ref, bf16[16,3712]{1,0:T(8,128)(2,1)S(1)} %collective-permute-done.6.refs_0_, bf16[16,3712]{1,0:T(8,128)(2,1)S(1)} %collective-permute-done.7.refs_1_, bf16[16,3712]{1,0:T(8,128)(2,1)S(1)} %collective-permute-done.8.refs_2_, ...), custom_call_target="tpu_custom_call" | custom-call | flops 704643072 | bytes 12845056 | tf_op jit(solution)/shard_map/ffn/pallas_call | solution.py:159
  35.2 0.5 collective-permute-start.10
  35.8 3.3 %ffn.3 = (bf16[64,3584]{1,0:T(8,128)(2,1)S(1)}, bf16[64,3584]{1,0:T(8,128)(2,1)S(1)}) custom-call(s32[1]{0:T(128)} %bitcast.expert_ref.at_ref, bf16[32,3712]{1,0:T(8,128)(2,1)S(1)} %get-tuple-element.16.refs_0_, bf16[32,3712]{1,0:T(8,128)(2,1)S(1)} %collective-permute-done.refs_1_, bf16[32,3712]{1,0:T(8,128)(2,1)S(1)} %collective-permute-done.1.refs_2_, ...), custom_call_target="tpu_custom_call" | custom-call | flops 1409286144 | bytes 14680064 | tf_op jit(solution)/shard_map/ffn/pallas_call | solution.py:159
  39.1 0.1 collective-permute-start.3
  39.3 1.3 %collective-permute-start.17 = (bf16[16,3584]{1,0:T(8,128)(2,1)S(1)}, bf16[16,3584]{1,0:T(8,128)(2,1)S(1)}, u32[]{:S(2)}, u32[]{:S(2)}) collective-permute-start(bf16[16,3584]{1,0:T(8,128)(2,1)S(1)} %slice.47), channel_id=1, source_target_pairs={{0,1},{1,0},{2,3},{3,2},{4,5},{5,4},{6,7},{7,6},{8,9},{9,8},{10,11... | collective-permute-start | bytes 344072 | tf_op jit(solution)/shard_map/ppermute | solution.py:204
  40.7 0.8 %collective-permute-start.11 = (bf16[16,3584]{1,0:T(8,128)(2,1)S(1)}, bf16[16,3584]{1,0:T(8,128)(2,1)S(1)}, u32[]{:S(2)}, u32[]{:S(2)}) collective-permute-start(bf16[16,3584]{1,0:T(8,128)(2,1)S(1)} %slice.45), channel_id=1, source_target_pairs={{0,1},{1,0},{2,3},{3,2},{4,5},{5,4},{6,7},{7,6},{8,9},{9,8},{10,11... | collective-permute-start | bytes 344072 | tf_op jit(solution)/shard_map/ppermute | solution.py:204
  41.5 3.8 %collective-permute-done.17 = bf16[16,3584]{1,0:T(8,128)(2,1)S(1)} collective-permute-done((bf16[16,3584]{1,0:T(8,128)(2,1)S(1)}, bf16[16,3584]{1,0:T(8,128)(2,1)S(1)}, u32[]{:S(2)}, u32[]{:S(2)}) %collective-permute-start.17) | collective-permute-done | bytes 114720 | tf_op jit(solution)/shard_map/ppermute | solution.py:204
  45.4 0.7 %collective-permute-start.18 = (bf16[16,3584]{1,0:T(8,128)(2,1)S(1)}, bf16[16,3584]{1,0:T(8,128)(2,1)S(1)}, u32[]{:S(2)}, u32[]{:S(2)}) collective-permute-start(bf16[16,3584]{1,0:T(8,128)(2,1)S(1)} %add_convert_fusion.6), channel_id=1, source_target_pairs={{0,4},{2,6},{4,0},{6,2},{8,12},{10,14},{12,8},{14,10},{1,5},{3,7},... | collective-permute-start | bytes 344072 | tf_op jit(solution)/shard_map/ppermute | solution.py:198
  46.2 1.4 %collective-permute-start.4 = (bf16[32,3584]{1,0:T(8,128)(2,1)S(1)}, bf16[32,3584]{1,0:T(8,128)(2,1)S(1)}, u32[]{:S(2)}, u32[]{:S(2)}) collective-permute-start(bf16[32,3584]{1,0:T(8,128)(2,1)S(1)} %add_convert_fusion.3), channel_id=1, source_target_pairs={{0,4},{2,6},{4,0},{6,2},{8,12},{10,14},{12,8},{14,10},{1,5},{3,7},... | collective-permute-start | bytes 688136 | tf_op jit(solution)/shard_map/ppermute | solution.py:198
  47.6 3.9 %collective-permute-done.18 = bf16[16,3584]{1,0:T(8,128)(2,1)S(1)} collective-permute-done((bf16[16,3584]{1,0:T(8,128)(2,1)S(1)}, bf16[16,3584]{1,0:T(8,128)(2,1)S(1)}, u32[]{:S(2)}, u32[]{:S(2)}) %collective-permute-start.18) | collective-permute-done | bytes 114720 | tf_op jit(solution)/shard_map/ppermute | solution.py:198
  51.5 2.2 %collective-permute-start.19 = (bf16[16,3584]{1,0:T(8,128)(2,1)S(1)}, bf16[16,3584]{1,0:T(8,128)(2,1)S(1)}, u32[]{:S(2)}, u32[]{:S(2)}) collective-permute-start(bf16[16,3584]{1,0:T(8,128)(2,1)S(1)} %add_convert_fusion.5), channel_id=1, source_target_pairs={{0,8},{2,10},{4,12},{6,14},{8,0},{10,2},{12,4},{14,6},{1,9},{3,11}... | collective-permute-start | bytes 344072 | tf_op jit(solution)/shard_map/ppermute | solution.py:198
  53.8 2.0 %collective-permute-done.4 = bf16[32,3584]{1,0:T(8,128)(2,1)S(1)} collective-permute-done((bf16[32,3584]{1,0:T(8,128)(2,1)S(1)}, bf16[32,3584]{1,0:T(8,128)(2,1)S(1)}, u32[]{:S(2)}, u32[]{:S(2)}) %collective-permute-start.4) | collective-permute-done | bytes 229408 | tf_op jit(solution)/shard_map/ppermute | solution.py:198
  55.9 1.3 %collective-permute-start.5 = (bf16[16,3584]{1,0:T(8,128)(2,1)S(1)}, bf16[16,3584]{1,0:T(8,128)(2,1)S(1)}, u32[]{:S(2)}, u32[]{:S(2)}) collective-permute-start(bf16[16,3584]{1,0:T(8,128)(2,1)S(1)} %slice.43), channel_id=1, source_target_pairs={{0,1},{1,0},{2,3},{3,2},{4,5},{5,4},{6,7},{7,6},{8,9},{9,8},{10,11... | collective-permute-start | bytes 344072 | tf_op jit(solution)/shard_map/ppermute | solution.py:204
  57.2 2.1 %collective-permute-done.19 = bf16[16,3584]{1,0:T(8,128)(2,1)S(1)} collective-permute-done((bf16[16,3584]{1,0:T(8,128)(2,1)S(1)}, bf16[16,3584]{1,0:T(8,128)(2,1)S(1)}, u32[]{:S(2)}, u32[]{:S(2)}) %collective-permute-start.19) | collective-permute-done | bytes 114720 | tf_op jit(solution)/shard_map/ppermute | solution.py:198
  59.4 1.4 %collective-permute-done.5 = bf16[16,3584]{1,0:T(8,128)(2,1)S(1)} collective-permute-done((bf16[16,3584]{1,0:T(8,128)(2,1)S(1)}, bf16[16,3584]{1,0:T(8,128)(2,1)S(1)}, u32[]{:S(2)}, u32[]{:S(2)}) %collective-permute-start.5) | collective-permute-done | bytes 114720 | tf_op jit(solution)/shard_map/ppermute | solution.py:204
  60.8 1.3 %collective-permute-start.20 = (bf16[16,3584]{1,0:T(8,128)(2,1)S(1)}, bf16[16,3584]{1,0:T(8,128)(2,1)S(1)}, u32[]{:S(2)}, u32[]{:S(2)}) collective-permute-start(bf16[16,3584]{1,0:T(8,128)(2,1)S(1)} %add_convert_fusion.4), channel_id=1, source_target_pairs={{0,1},{1,0},{2,3},{3,2},{4,5},{5,4},{6,7},{7,6},{8,9},{9,8},{10,11... | collective-permute-start | bytes 344072 | tf_op jit(solution)/shard_map/ppermute | solution.py:204
  62.2 3.5 %collective-permute-done.20 = bf16[16,3584]{1,0:T(8,128)(2,1)S(1)} collective-permute-done((bf16[16,3584]{1,0:T(8,128)(2,1)S(1)}, bf16[16,3584]{1,0:T(8,128)(2,1)S(1)}, u32[]{:S(2)}, u32[]{:S(2)}) %collective-permute-start.20) | collective-permute-done | bytes 114720 | tf_op jit(solution)/shard_map/ppermute | solution.py:204
  65.7 0.7 %maximum_select_fusion = bf16[32,3584]{1,0:T(8,128)(2,1)} fusion(bf16[16,3584]{1,0:T(8,128)(2,1)S(1)} %collective-permute-done.20, bf16[16,3584]{1,0:T(8,128)(2,1)S(1)} %add_convert_fusion.4, pred[]{:T(512)S(6)} %eq.3), kind=kLoop, calls=%fused_computation.4 | loop fusion | flops 1032192 | bytes 458753 | tf_op jit(solution)/shard_map/jit(_where)/select_n | solution.py:240
  (26 shorter events, 0.5 us)
Async XLA Ops:
  1.1 9.9 %collective-permute-start.6 = (bf16[16,3712]{1,0:T(8,128)(2,1)S(1)}, bf16[16,3712]{1,0:T(8,128)(2,1)S(1)}, u32[]{:S(2)}, u32[]{:S(2)}) collective-permute-start(bf16[16,3712]{1,0:T(8,128)(2,1)S(1)} %get-tuple-element.22), channel_id=1, source_target_pairs={{0,8},{2,10},{4,12},{6,14},{8,0},{10,2},{12,4},{14,6},{1,9},{3,11}... | collective-permute-start | bytes 356360 | tf_op jit(solution)/shard_map/ppermute | solution.py:198
  11.0 6.1 %collective-permute-start.12 = (bf16[16,3712]{1,0:T(8,128)(2,1)S(1)}, bf16[16,3712]{1,0:T(8,128)(2,1)S(1)}, u32[]{:S(2)}, u32[]{:S(2)}) collective-permute-start(bf16[16,3712]{1,0:T(8,128)(2,1)S(1)} %collective-permute-done.6.refs_0_), channel_id=1, source_target_pairs={{0,4},{2,6},{4,0},{6,2},{8,12},{10,14},{12,8},{14,10},{1,5},{3,7},... | collective-permute-start | bytes 356360 | tf_op jit(solution)/shard_map/ppermute | solution.py:198
  11.7 10.7 %collective-permute-start = (bf16[32,3712]{1,0:T(8,128)(2,1)S(1)}, bf16[32,3712]{1,0:T(8,128)(2,1)S(1)}, u32[]{:S(2)}, u32[]{:S(2)}) collective-permute-start(bf16[32,3712]{1,0:T(8,128)(2,1)S(1)} %get-tuple-element.16.refs_0_), channel_id=1, source_target_pairs={{0,4},{2,6},{4,0},{6,2},{8,12},{10,14},{12,8},{14,10},{1,5},{3,7},... | collective-permute-start | bytes 712712 | tf_op jit(solution)/shard_map/ppermute | solution.py:198
  17.1 4.8 %collective-permute-start.13 = (bf16[16,3712]{1,0:T(8,128)(2,1)S(1)}, bf16[16,3712]{1,0:T(8,128)(2,1)S(1)}, u32[]{:S(2)}, u32[]{:S(2)}) collective-permute-start(bf16[16,3712]{1,0:T(8,128)(2,1)S(1)} %collective-permute-done.12.refs_0_), channel_id=1, source_target_pairs={{0,1},{1,0},{2,3},{3,2},{4,5},{5,4},{6,7},{7,6},{8,9},{9,8},{10,11... | collective-permute-start | bytes 356360 | tf_op jit(solution)/shard_map/ppermute | solution.py:204
  18.7 4.8 %collective-permute-start.7 = (bf16[16,3712]{1,0:T(8,128)(2,1)S(1)}, bf16[16,3712]{1,0:T(8,128)(2,1)S(1)}, u32[]{:S(2)}, u32[]{:S(2)}) collective-permute-start(bf16[16,3712]{1,0:T(8,128)(2,1)S(1)} %collective-permute-done.6.refs_0_), channel_id=1, source_target_pairs={{0,1},{1,0},{2,3},{3,2},{4,5},{5,4},{6,7},{7,6},{8,9},{9,8},{10,11... | collective-permute-start | bytes 356360 | tf_op jit(solution)/shard_map/ppermute | solution.py:204
  19.1 4.4 %collective-permute-start.14 = (bf16[16,3712]{1,0:T(8,128)(2,1)S(1)}, bf16[16,3712]{1,0:T(8,128)(2,1)S(1)}, u32[]{:S(2)}, u32[]{:S(2)}) collective-permute-start(bf16[16,3712]{1,0:T(8,128)(2,1)S(1)} %collective-permute-done.12.refs_0_), channel_id=1, source_target_pairs={{0,2},{2,0},{4,6},{6,4},{8,10},{10,8},{12,14},{14,12},{1,3},{3,1},... | collective-permute-start | bytes 356360 | tf_op jit(solution)/shard_map/ppermute | solution.py:198
  22.0 6.3 %collective-permute-start.15 = (bf16[16,3712]{1,0:T(8,128)(2,1)S(1)}, bf16[16,3712]{1,0:T(8,128)(2,1)S(1)}, u32[]{:S(2)}, u32[]{:S(2)}) collective-permute-start(bf16[16,3712]{1,0:T(8,128)(2,1)S(1)} %collective-permute-done.13.refs_1_), channel_id=1, source_target_pairs={{0,2},{2,0},{4,6},{6,4},{8,10},{10,8},{12,14},{14,12},{1,3},{3,1},... | collective-permute-start | bytes 356360 | tf_op jit(solution)/shard_map/ppermute | solution.py:198
  22.0 13.8 %collective-permute-start.1 = (bf16[32,3712]{1,0:T(8,128)(2,1)S(1)}, bf16[32,3712]{1,0:T(8,128)(2,1)S(1)}, u32[]{:S(2)}, u32[]{:S(2)}) collective-permute-start(bf16[32,3712]{1,0:T(8,128)(2,1)S(1)} %get-tuple-element.16.refs_0_), channel_id=1, source_target_pairs={{0,2},{2,0},{4,6},{6,4},{8,10},{10,8},{12,14},{14,12},{1,3},{3,1},... | collective-permute-start | bytes 712712 | tf_op jit(solution)/shard_map/ppermute | solution.py:198
  22.5 13.3 %collective-permute-start.2 = (bf16[32,3712]{1,0:T(8,128)(2,1)S(1)}, bf16[32,3712]{1,0:T(8,128)(2,1)S(1)}, u32[]{:S(2)}, u32[]{:S(2)}) collective-permute-start(bf16[32,3712]{1,0:T(8,128)(2,1)S(1)} %collective-permute-done.refs_1_), channel_id=1, source_target_pairs={{0,2},{2,0},{4,6},{6,4},{8,10},{10,8},{12,14},{14,12},{1,3},{3,1},... | collective-permute-start | bytes 712712 | tf_op jit(solution)/shard_map/ppermute | solution.py:198
  23.5 8.3 %collective-permute-start.8 = (bf16[16,3712]{1,0:T(8,128)(2,1)S(1)}, bf16[16,3712]{1,0:T(8,128)(2,1)S(1)}, u32[]{:S(2)}, u32[]{:S(2)}) collective-permute-start(bf16[16,3712]{1,0:T(8,128)(2,1)S(1)} %collective-permute-done.6.refs_0_), channel_id=1, source_target_pairs={{0,2},{2,0},{4,6},{6,4},{8,10},{10,8},{12,14},{14,12},{1,3},{3,1},... | collective-permute-start | bytes 356360 | tf_op jit(solution)/shard_map/ppermute | solution.py:198
  23.5 8.3 %collective-permute-start.9 = (bf16[16,3712]{1,0:T(8,128)(2,1)S(1)}, bf16[16,3712]{1,0:T(8,128)(2,1)S(1)}, u32[]{:S(2)}, u32[]{:S(2)}) collective-permute-start(bf16[16,3712]{1,0:T(8,128)(2,1)S(1)} %collective-permute-done.7.refs_1_), channel_id=1, source_target_pairs={{0,2},{2,0},{4,6},{6,4},{8,10},{10,8},{12,14},{14,12},{1,3},{3,1},... | collective-permute-start | bytes 356360 | tf_op jit(solution)/shard_map/ppermute | solution.py:198
  31.7 7.5 %collective-permute-start.16 = (bf16[32,3584]{1,0:T(8,128)(2,1)S(1)}, bf16[32,3584]{1,0:T(8,128)(2,1)S(1)}, u32[]{:S(2)}, u32[]{:S(2)}) collective-permute-start(bf16[32,3584]{1,0:T(8,128)(2,1)S(1)} %get-tuple-element.26), channel_id=1, source_target_pairs={{0,2},{2,0},{4,6},{6,4},{8,10},{10,8},{12,14},{14,12},{1,3},{3,1},... | collective-permute-start | bytes 688136 | tf_op jit(solution)/shard_map/ppermute | solution.py:198
  35.2 5.4 %collective-permute-start.10 = (bf16[32,3584]{1,0:T(8,128)(2,1)S(1)}, bf16[32,3584]{1,0:T(8,128)(2,1)S(1)}, u32[]{:S(2)}, u32[]{:S(2)}) collective-permute-start(bf16[32,3584]{1,0:T(8,128)(2,1)S(1)} %get-tuple-element.24), channel_id=1, source_target_pairs={{0,2},{2,0},{4,6},{6,4},{8,10},{10,8},{12,14},{14,12},{1,3},{3,1},... | collective-permute-start | bytes 688136 | tf_op jit(solution)/shard_map/ppermute | solution.py:198
  39.1 7.0 %collective-permute-start.3 = (bf16[64,3584]{1,0:T(8,128)(2,1)S(1)}, bf16[64,3584]{1,0:T(8,128)(2,1)S(1)}, u32[]{:S(2)}, u32[]{:S(2)}) collective-permute-start(bf16[64,3584]{1,0:T(8,128)(2,1)S(1)} %get-tuple-element.21), channel_id=1, source_target_pairs={{0,2},{2,0},{4,6},{6,4},{8,10},{10,8},{12,14},{14,12},{1,3},{3,1},... | collective-permute-start | bytes 1376264 | tf_op jit(solution)/shard_map/ppermute | solution.py:198
  39.3 6.1 %collective-permute-start.17 = (bf16[16,3584]{1,0:T(8,128)(2,1)S(1)}, bf16[16,3584]{1,0:T(8,128)(2,1)S(1)}, u32[]{:S(2)}, u32[]{:S(2)}) collective-permute-start(bf16[16,3584]{1,0:T(8,128)(2,1)S(1)} %slice.47), channel_id=1, source_target_pairs={{0,1},{1,0},{2,3},{3,2},{4,5},{5,4},{6,7},{7,6},{8,9},{9,8},{10,11... | collective-permute-start | bytes 344072 | tf_op jit(solution)/shard_map/ppermute | solution.py:204
  40.7 6.9 %collective-permute-start.11 = (bf16[16,3584]{1,0:T(8,128)(2,1)S(1)}, bf16[16,3584]{1,0:T(8,128)(2,1)S(1)}, u32[]{:S(2)}, u32[]{:S(2)}) collective-permute-start(bf16[16,3584]{1,0:T(8,128)(2,1)S(1)} %slice.45), channel_id=1, source_target_pairs={{0,1},{1,0},{2,3},{3,2},{4,5},{5,4},{6,7},{7,6},{8,9},{9,8},{10,11... | collective-permute-start | bytes 344072 | tf_op jit(solution)/shard_map/ppermute | solution.py:204
  45.4 6.1 %collective-permute-start.18 = (bf16[16,3584]{1,0:T(8,128)(2,1)S(1)}, bf16[16,3584]{1,0:T(8,128)(2,1)S(1)}, u32[]{:S(2)}, u32[]{:S(2)}) collective-permute-start(bf16[16,3584]{1,0:T(8,128)(2,1)S(1)} %add_convert_fusion.6), channel_id=1, source_target_pairs={{0,4},{2,6},{4,0},{6,2},{8,12},{10,14},{12,8},{14,10},{1,5},{3,7},... | collective-permute-start | bytes 344072 | tf_op jit(solution)/shard_map/ppermute | solution.py:198
  46.2 9.6 %collective-permute-start.4 = (bf16[32,3584]{1,0:T(8,128)(2,1)S(1)}, bf16[32,3584]{1,0:T(8,128)(2,1)S(1)}, u32[]{:S(2)}, u32[]{:S(2)}) collective-permute-start(bf16[32,3584]{1,0:T(8,128)(2,1)S(1)} %add_convert_fusion.3), channel_id=1, source_target_pairs={{0,4},{2,6},{4,0},{6,2},{8,12},{10,14},{12,8},{14,10},{1,5},{3,7},... | collective-permute-start | bytes 688136 | tf_op jit(solution)/shard_map/ppermute | solution.py:198
  51.5 7.9 %collective-permute-start.19 = (bf16[16,3584]{1,0:T(8,128)(2,1)S(1)}, bf16[16,3584]{1,0:T(8,128)(2,1)S(1)}, u32[]{:S(2)}, u32[]{:S(2)}) collective-permute-start(bf16[16,3584]{1,0:T(8,128)(2,1)S(1)} %add_convert_fusion.5), channel_id=1, source_target_pairs={{0,8},{2,10},{4,12},{6,14},{8,0},{10,2},{12,4},{14,6},{1,9},{3,11}... | collective-permute-start | bytes 344072 | tf_op jit(solution)/shard_map/ppermute | solution.py:198
  55.9 4.9 %collective-permute-start.5 = (bf16[16,3584]{1,0:T(8,128)(2,1)S(1)}, bf16[16,3584]{1,0:T(8,128)(2,1)S(1)}, u32[]{:S(2)}, u32[]{:S(2)}) collective-permute-start(bf16[16,3584]{1,0:T(8,128)(2,1)S(1)} %slice.43), channel_id=1, source_target_pairs={{0,1},{1,0},{2,3},{3,2},{4,5},{5,4},{6,7},{7,6},{8,9},{9,8},{10,11... | collective-permute-start | bytes 344072 | tf_op jit(solution)/shard_map/ppermute | solution.py:204
  60.8 4.9 %collective-permute-start.20 = (bf16[16,3584]{1,0:T(8,128)(2,1)S(1)}, bf16[16,3584]{1,0:T(8,128)(2,1)S(1)}, u32[]{:S(2)}, u32[]{:S(2)}) collective-permute-start(bf16[16,3584]{1,0:T(8,128)(2,1)S(1)} %add_convert_fusion.4), channel_id=1, source_target_pairs={{0,1},{1,0},{2,3},{3,2},{4,5},{5,4},{6,7},{7,6},{8,9},{9,8},{10,11... | collective-permute-start | bytes 344072 | tf_op jit(solution)/shard_map/ppermute | solution.py:204

commit v3 on v2

--- a/solution.py
+++ b/solution.py
@@ -138,18 +138,14 @@
         h_ref[:, cols] = (gate / (1.0 + jnp.exp(-gate)) * up).astype(jnp.bfloat16)
     half = row // 2
     wide = 512
-
-    def down(j, carry):
-        cols = pl.ds(pl.multiple_of(j * wide, wide), wide)
+    for start in range(0, width, wide):
+        cols = pl.ds(start, min(wide, width - start))
         y = lax.dot_general(
             h_ref[...], down_ref[cols, :], (((1,), (1,)), ((), ())), preferred_element_type=jnp.float32
         )
         y = (y * w_ref[:, pl.ds(0, 1)]).astype(jnp.bfloat16)
         keep_ref[:, cols] = y[:half]
         send_ref[:, cols] = y[half:]
-        return carry
-
-    lax.fori_loop(0, width // wide, down, 0)
 
 
 def ffn(x_blocks, w_gate, w_up, w_down, expert_at, experts):
@@ -211,30 +207,22 @@
     near = swap(own, 2)
     own_core = core(own)
     weights = load(gate_proj[0], up_proj[0], down_proj[0])
-
-    relay = swap(far, 2)
-    far_pair = pair(far)
-    far_core = core(far)
     near_core = core(near)
     keep, send = run(own, near, own_core, near_core)
     got = core(send)
-    relay_pair = pair(relay)
-    relay_core = core(relay)
-    far_pair_core = core(far_pair)
-    far_keep, far_send = run(far, far_pair, far_core, far_pair_core)
+    near_sum = swap(add(keep[count:], got[count:]), 2)
+    both = add(keep[:count], got[:count], near_sum)
+
+    far_pair = pair(far)
+    blocks = (swap(far, 2), swap(far_pair, 2), far, far_pair)
+    far_keep, far_send = run(*blocks, *[core(b) for b in blocks])
     far_got = core(far_send)
-    near_sum = swap(add(keep[count:], got[count:]), 2)
-    relay_pair_core = core(relay_pair)
-    far_total = add(far_keep, far_got)
-    far_other = pair(far_total[half:])
-    relay_keep, relay_send = run(relay, relay_pair, relay_core, relay_pair_core)
-    relay_got = core(relay_send)
-    relay_total = add(relay_keep, relay_got)
-    relay_other = pair(relay_total[half:])
-    relay_sum = swap(add(relay_total[:half], relay_other), 2)
-    far_sum = swap(add(far_total[:half], far_other, relay_sum), 4)
-    both = add(keep[:count], got[:count], near_sum)
+    total = [add(far_keep[i : i + half], far_got[i : i + half]) for i in range(0, 2 * count, half)]
+    relay_other = pair(total[1])
+    far_other = pair(total[3])
     near_other = pair(both[half:])
+    relay_sum = swap(add(total[0], relay_other), 2)
+    far_sum = swap(add(total[2], far_other, relay_sum), 4)
     final = add(both[:half], near_other, far_sum)
     other = pair(final)
     return jnp.where(

time: 66.5 us -> 59.4 us (0.89)
  Pallas kernels: 15.5 us -> 9.97 us
  waiting for transfers between devices: 30.5 us -> 27.4 us
  starting transfers between devices: 19.1 us -> 20.7 us
    pallas_call x3 -> x2, Pallas kernels: 10.2 us -> 4.65 us  [ffn(): pl.pallas_call(functools.partial(ffn_kernel, experts, len(x_blocks)), out...]
    ppermute x6 -> x5, waiting for transfers between devices: 12.6 us -> 8.84 us  [pair(): return lax.ppermute(value, 'attn', [(0, 1), (1, 0)])]
    ppermute x15, starting transfers between devices: 12.3 us -> 14 us  [swap(): return lax.ppermute(value, 'expert', [(i, i ^ bit) for i in range(experts)])]
    ppermute x6 -> x5, starting transfers between devices: 6.87 us -> 6.72 us  [pair(): return lax.ppermute(value, 'attn', [(0, 1), (1, 0)])]
  transfers between devices with their start and end apart: 21 -> 20, of which waited for: 10 -> 10; matrix products, arithmetic and copies ran while one was open for 1% -> 1% of each run, Pallas kernels for 22% -> 15%
where the time goes in v3:
time: 59.4 us; the launch traced here: 59.3 us
  waiting for transfers between devices  27.4 us (46%)
  starting transfers between devices  20.7 us (35%)
  Pallas kernels  9.97 us (17%)
  other arithmetic  1.07 us (2%)
    ppermute x15, waiting for transfers between devices, swap(): return lax.ppermute(value, 'expert', [(i, i ^ bit) for i in range(experts)])  18.5 us
    ppermute x15, starting transfers between devices, swap(): return lax.ppermute(value, 'expert', [(i, i ^ bit) for i in range(experts)])  14 us
    ppermute x5, waiting for transfers between devices, pair(): return lax.ppermute(value, 'attn', [(0, 1), (1, 0)])  8.84 us
    ppermute x5, starting transfers between devices, pair(): return lax.ppermute(value, 'attn', [(0, 1), (1, 0)])  6.72 us
    pallas_call x2, Pallas kernels, ffn(): pl.pallas_call(functools.partial(ffn_kernel, experts, len(x_blocks)), out...  4.65 us
    pallas_call x1, Pallas kernels, load(): pl.pallas_call(load_kernel, out_shape=tuple((jax.ShapeDtypeStruct(a.shape...  4.23 us
  transfers between devices with their start and end apart: 20, of which 10 were waited for; matrix products, arithmetic and copies ran while one was open for 1% of the time, Pallas kernels for 15%

profile of v3, /device:TPU:0, one launch (start us, length us, event | category | flops | bytes accessed | tf_op | source)
XLA Modules:
  0.0 59.3 jit_solution(8225233749461739895)
XLA Ops:
  0.0 1.1 %prepare.1 = (bf16[32,3712]{1,0:T(8,128)(2,1)S(1)}, bf16[16,3712]{1,0:T(8,128)(2,1)S(1)}) custom-call(s32[1]{0:T(128)} %bitcast.1.at_ref, s32[1]{0:T(128)} %bitcast.expert_ref.at_ref, s32[8]{0:T(128)} %plan_hbm.1, s32[8,32]{1,0:T(8,128)} %bitcast.10, f32[8,32]{1,0:T(8,128)} %bitcast.11, bf16[32,3584]{1,0:T(8,128)(2,1)} %tok_hbm.1), custom_call_target="tpu_custom_call" | custom-call | tf_op jit(solution)/shard_map/prepare/pallas_call | solution.py:71
  1.1 4.1 %collective-permute-start.6 = (bf16[16,3712]{1,0:T(8,128)(2,1)S(1)}, bf16[16,3712]{1,0:T(8,128)(2,1)S(1)}, u32[]{:S(2)}, u32[]{:S(2)}) collective-permute-start(bf16[16,3712]{1,0:T(8,128)(2,1)S(1)} %get-tuple-element.20), channel_id=1, source_target_pairs={{0,8},{2,10},{4,12},{6,14},{8,0},{10,2},{12,4},{14,6},{1,9},{3,11}... | collective-permute-start | bytes 356360 | tf_op jit(solution)/shard_map/ppermute | solution.py:194
  5.2 5.8 %collective-permute-done.6.refs_2_ = bf16[16,3712]{1,0:T(8,128)(2,1)S(1)} collective-permute-done((bf16[16,3712]{1,0:T(8,128)(2,1)S(1)}, bf16[16,3712]{1,0:T(8,128)(2,1)S(1)}, u32[]{:S(2)}, u32[]{:S(2)}) %collective-permute-start.6) | collective-permute-done | bytes 118816 | tf_op jit(solution)/shard_map/ppermute | solution.py:194
  11.0 1.5 %collective-permute-start.8 = (bf16[16,3712]{1,0:T(8,128)(2,1)S(1)}, bf16[16,3712]{1,0:T(8,128)(2,1)S(1)}, u32[]{:S(2)}, u32[]{:S(2)}) collective-permute-start(bf16[16,3712]{1,0:T(8,128)(2,1)S(1)} %collective-permute-done.6.refs_2_), channel_id=1, source_target_pairs={{0,1},{1,0},{2,3},{3,2},{4,5},{5,4},{6,7},{7,6},{8,9},{9,8},{10,11... | collective-permute-start | bytes 356360 | tf_op jit(solution)/shard_map/ppermute | solution.py:200
  12.6 0.7 %collective-permute-start.7 = (bf16[16,3712]{1,0:T(8,128)(2,1)S(1)}, bf16[16,3712]{1,0:T(8,128)(2,1)S(1)}, u32[]{:S(2)}, u32[]{:S(2)}) collective-permute-start(bf16[16,3712]{1,0:T(8,128)(2,1)S(1)} %collective-permute-done.6.refs_2_), channel_id=1, source_target_pairs={{0,4},{2,6},{4,0},{6,2},{8,12},{10,14},{12,8},{14,10},{1,5},{3,7},... | collective-permute-start | bytes 356360 | tf_op jit(solution)/shard_map/ppermute | solution.py:194
  13.2 2.6 %collective-permute-done.8.refs_3_ = bf16[16,3712]{1,0:T(8,128)(2,1)S(1)} collective-permute-done((bf16[16,3712]{1,0:T(8,128)(2,1)S(1)}, bf16[16,3712]{1,0:T(8,128)(2,1)S(1)}, u32[]{:S(2)}, u32[]{:S(2)}) %collective-permute-start.8) | collective-permute-done | bytes 118816 | tf_op jit(solution)/shard_map/ppermute | solution.py:200
  15.8 1.0 %collective-permute-start.9 = (bf16[16,3712]{1,0:T(8,128)(2,1)S(1)}, bf16[16,3712]{1,0:T(8,128)(2,1)S(1)}, u32[]{:S(2)}, u32[]{:S(2)}) collective-permute-start(bf16[16,3712]{1,0:T(8,128)(2,1)S(1)} %collective-permute-done.8.refs_3_), channel_id=1, source_target_pairs={{0,4},{2,6},{4,0},{6,2},{8,12},{10,14},{12,8},{14,10},{1,5},{3,7},... | collective-permute-start | bytes 356360 | tf_op jit(solution)/shard_map/ppermute | solution.py:194
  16.9 0.5 collective-permute-start.13
  17.4 0.5 collective-permute-done.7.refs_0_
  17.9 2.8 %collective-permute-done.9.refs_1_ = bf16[16,3712]{1,0:T(8,128)(2,1)S(1)} collective-permute-done((bf16[16,3712]{1,0:T(8,128)(2,1)S(1)}, bf16[16,3712]{1,0:T(8,128)(2,1)S(1)}, u32[]{:S(2)}, u32[]{:S(2)}) %collective-permute-start.9) | collective-permute-done | bytes 118816 | tf_op jit(solution)/shard_map/ppermute | solution.py:194
  20.7 1.0 %collective-permute-start = (bf16[32,3712]{1,0:T(8,128)(2,1)S(1)}, bf16[32,3712]{1,0:T(8,128)(2,1)S(1)}, u32[]{:S(2)}, u32[]{:S(2)}) collective-permute-start(bf16[32,3712]{1,0:T(8,128)(2,1)S(1)} %get-tuple-element.14.refs_0_), channel_id=1, source_target_pairs={{0,4},{2,6},{4,0},{6,2},{8,12},{10,14},{12,8},{14,10},{1,5},{3,7},... | collective-permute-start | bytes 712712 | tf_op jit(solution)/shard_map/ppermute | solution.py:194
  21.7 4.2 %load.1 = (bf16[3584,512]{1,0:T(8,128)(2,1)S(1)}, bf16[3584,512]{1,0:T(8,128)(2,1)S(1)}, bf16[3584,512]{1,0:T(8,128)(2,1)S(1)}) custom-call(bf16[3584,512]{1,0:T(8,128)(2,1)} %bitcast.7, bf16[3584,512]{1,0:T(8,128)(2,1)} %bitcast.8, bf16[3584,512]{1,0:T(8,128)(2,1)} %bitcast.9), custom_call_target="tpu_custom_call" | custom-call | bytes 22020096 | tf_op jit(solution)/shard_map/load/pallas_call | solution.py:105
  26.0 2.4 %ffn.3 = (bf16[64,3584]{1,0:T(8,128)(2,1)S(1)}, bf16[64,3584]{1,0:T(8,128)(2,1)S(1)}) custom-call(s32[1]{0:T(128)} %bitcast.expert_ref.at_ref, bf16[16,3712]{1,0:T(8,128)(2,1)S(1)} %collective-permute-done.7.refs_0_, bf16[16,3712]{1,0:T(8,128)(2,1)S(1)} %collective-permute-done.9.refs_1_, bf16[16,3712]{1,0:T(8,128)(2,1)S(1)} %collective-permute-done.6.refs_2_, ...), custom_call_target="tpu_custom_call" | custom-call | flops 1409286144 | bytes 14680064 | tf_op jit(solution)/shard_map/ffn/pallas_call | solution.py:155
  28.4 0.3 collective-permute-start.14
  28.7 0.3 collective-permute-start.1
  28.9 0.2 collective-permute-start.2
  29.2 1.4 %collective-permute-done.1.refs_2_ = bf16[32,3712]{1,0:T(8,128)(2,1)S(1)} collective-permute-done((bf16[32,3712]{1,0:T(8,128)(2,1)S(1)}, bf16[32,3712]{1,0:T(8,128)(2,1)S(1)}, u32[]{:S(2)}, u32[]{:S(2)}) %collective-permute-start.1) | collective-permute-done | bytes 237600 | tf_op jit(solution)/shard_map/ppermute | solution.py:194
  30.6 0.3 collective-permute-done.2.refs_3_
  30.9 2.3 %ffn.2 = (bf16[64,3584]{1,0:T(8,128)(2,1)S(1)}, bf16[64,3584]{1,0:T(8,128)(2,1)S(1)}) custom-call(s32[1]{0:T(128)} %bitcast.expert_ref.at_ref, bf16[32,3712]{1,0:T(8,128)(2,1)S(1)} %get-tuple-element.14.refs_0_, bf16[32,3712]{1,0:T(8,128)(2,1)S(1)} %collective-permute-done.refs_1_, bf16[32,3712]{1,0:T(8,128)(2,1)S(1)} %collective-permute-done.1.refs_2_, ...), custom_call_target="tpu_custom_call" | custom-call | flops 1409286144 | bytes 14680064 | tf_op jit(solution)/shard_map/ffn/pallas_call | solution.py:155
  33.2 0.3 collective-permute-start.3
  33.6 1.5 %collective-permute-start.16 = (bf16[16,3584]{1,0:T(8,128)(2,1)S(1)}, bf16[16,3584]{1,0:T(8,128)(2,1)S(1)}, u32[]{:S(2)}, u32[]{:S(2)}) collective-permute-start(bf16[16,3584]{1,0:T(8,128)(2,1)S(1)} %get-tuple-element.24), channel_id=1, source_target_pairs={{0,1},{1,0},{2,3},{3,2},{4,5},{5,4},{6,7},{7,6},{8,9},{9,8},{10,11... | collective-permute-start | bytes 344072 | tf_op jit(solution)/shard_map/ppermute | solution.py:200
  35.1 0.5 collective-permute-start.15
  35.8 1.0 %collective-permute-start.4 = (bf16[32,3584]{1,0:T(8,128)(2,1)S(1)}, bf16[32,3584]{1,0:T(8,128)(2,1)S(1)}, u32[]{:S(2)}, u32[]{:S(2)}) collective-permute-start(bf16[32,3584]{1,0:T(8,128)(2,1)S(1)} %add_convert_fusion.1), channel_id=1, source_target_pairs={{0,4},{2,6},{4,0},{6,2},{8,12},{10,14},{12,8},{14,10},{1,5},{3,7},... | collective-permute-start | bytes 688136 | tf_op jit(solution)/shard_map/ppermute | solution.py:194
  36.8 2.9 %collective-permute-done.16 = bf16[16,3584]{1,0:T(8,128)(2,1)S(1)} collective-permute-done((bf16[16,3584]{1,0:T(8,128)(2,1)S(1)}, bf16[16,3584]{1,0:T(8,128)(2,1)S(1)}, u32[]{:S(2)}, u32[]{:S(2)}) %collective-permute-start.16) | collective-permute-done | bytes 114720 | tf_op jit(solution)/shard_map/ppermute | solution.py:200
  39.7 1.0 %collective-permute-start.17 = (bf16[16,3584]{1,0:T(8,128)(2,1)S(1)}, bf16[16,3584]{1,0:T(8,128)(2,1)S(1)}, u32[]{:S(2)}, u32[]{:S(2)}) collective-permute-start(bf16[16,3584]{1,0:T(8,128)(2,1)S(1)} %add_convert_fusion.4), channel_id=1, source_target_pairs={{0,4},{2,6},{4,0},{6,2},{8,12},{10,14},{12,8},{14,10},{1,5},{3,7},... | collective-permute-start | bytes 344072 | tf_op jit(solution)/shard_map/ppermute | solution.py:194
  40.8 3.5 %collective-permute-done.4 = bf16[32,3584]{1,0:T(8,128)(2,1)S(1)} collective-permute-done((bf16[32,3584]{1,0:T(8,128)(2,1)S(1)}, bf16[32,3584]{1,0:T(8,128)(2,1)S(1)}, u32[]{:S(2)}, u32[]{:S(2)}) %collective-permute-start.4) | collective-permute-done | bytes 229408 | tf_op jit(solution)/shard_map/ppermute | solution.py:194
  44.4 1.6 %collective-permute-start.5 = (bf16[16,3584]{1,0:T(8,128)(2,1)S(1)}, bf16[16,3584]{1,0:T(8,128)(2,1)S(1)}, u32[]{:S(2)}, u32[]{:S(2)}) collective-permute-start(bf16[16,3584]{1,0:T(8,128)(2,1)S(1)} %slice.59), channel_id=1, source_target_pairs={{0,1},{1,0},{2,3},{3,2},{4,5},{5,4},{6,7},{7,6},{8,9},{9,8},{10,11... | collective-permute-start | bytes 344072 | tf_op jit(solution)/shard_map/ppermute | solution.py:200
  46.0 3.4 %collective-permute-start.18 = (bf16[16,3584]{1,0:T(8,128)(2,1)S(1)}, bf16[16,3584]{1,0:T(8,128)(2,1)S(1)}, u32[]{:S(2)}, u32[]{:S(2)}) collective-permute-start(bf16[16,3584]{1,0:T(8,128)(2,1)S(1)} %add_convert_fusion.3), channel_id=1, source_target_pairs={{0,8},{2,10},{4,12},{6,14},{8,0},{10,2},{12,4},{14,6},{1,9},{3,11}... | collective-permute-start | bytes 344072 | tf_op jit(solution)/shard_map/ppermute | solution.py:194
  49.4 4.2 %collective-permute-done.18 = bf16[16,3584]{1,0:T(8,128)(2,1)S(1)} collective-permute-done((bf16[16,3584]{1,0:T(8,128)(2,1)S(1)}, bf16[16,3584]{1,0:T(8,128)(2,1)S(1)}, u32[]{:S(2)}, u32[]{:S(2)}) %collective-permute-start.18) | collective-permute-done | bytes 114720 | tf_op jit(solution)/shard_map/ppermute | solution.py:194
  53.7 1.5 %collective-permute-start.19 = (bf16[16,3584]{1,0:T(8,128)(2,1)S(1)}, bf16[16,3584]{1,0:T(8,128)(2,1)S(1)}, u32[]{:S(2)}, u32[]{:S(2)}) collective-permute-start(bf16[16,3584]{1,0:T(8,128)(2,1)S(1)} %add_convert_fusion.2), channel_id=1, source_target_pairs={{0,1},{1,0},{2,3},{3,2},{4,5},{5,4},{6,7},{7,6},{8,9},{9,8},{10,11... | collective-permute-start | bytes 344072 | tf_op jit(solution)/shard_map/ppermute | solution.py:200
  55.2 3.3 %collective-permute-done.19 = bf16[16,3584]{1,0:T(8,128)(2,1)S(1)} collective-permute-done((bf16[16,3584]{1,0:T(8,128)(2,1)S(1)}, bf16[16,3584]{1,0:T(8,128)(2,1)S(1)}, u32[]{:S(2)}, u32[]{:S(2)}) %collective-permute-start.19) | collective-permute-done | bytes 114720 | tf_op jit(solution)/shard_map/ppermute | solution.py:200
  58.6 0.7 %maximum_select_fusion = bf16[32,3584]{1,0:T(8,128)(2,1)} fusion(bf16[16,3584]{1,0:T(8,128)(2,1)S(1)} %collective-permute-done.19, bf16[16,3584]{1,0:T(8,128)(2,1)S(1)} %add_convert_fusion.2, pred[]{:T(512)S(6)} %eq.3), kind=kLoop, calls=%fused_computation.2 | loop fusion | flops 1032192 | bytes 458753 | tf_op jit(solution)/shard_map/jit(_where)/select_n | solution.py:228
  (20 shorter events, 0.4 us)
Async XLA Ops:
  1.1 9.9 %collective-permute-start.6 = (bf16[16,3712]{1,0:T(8,128)(2,1)S(1)}, bf16[16,3712]{1,0:T(8,128)(2,1)S(1)}, u32[]{:S(2)}, u32[]{:S(2)}) collective-permute-start(bf16[16,3712]{1,0:T(8,128)(2,1)S(1)} %get-tuple-element.20), channel_id=1, source_target_pairs={{0,8},{2,10},{4,12},{6,14},{8,0},{10,2},{12,4},{14,6},{1,9},{3,11}... | collective-permute-start | bytes 356360 | tf_op jit(solution)/shard_map/ppermute | solution.py:194
  11.0 4.8 %collective-permute-start.8 = (bf16[16,3712]{1,0:T(8,128)(2,1)S(1)}, bf16[16,3712]{1,0:T(8,128)(2,1)S(1)}, u32[]{:S(2)}, u32[]{:S(2)}) collective-permute-start(bf16[16,3712]{1,0:T(8,128)(2,1)S(1)} %collective-permute-done.6.refs_2_), channel_id=1, source_target_pairs={{0,1},{1,0},{2,3},{3,2},{4,5},{5,4},{6,7},{7,6},{8,9},{9,8},{10,11... | collective-permute-start | bytes 356360 | tf_op jit(solution)/shard_map/ppermute | solution.py:200
  12.6 5.3 %collective-permute-start.7 = (bf16[16,3712]{1,0:T(8,128)(2,1)S(1)}, bf16[16,3712]{1,0:T(8,128)(2,1)S(1)}, u32[]{:S(2)}, u32[]{:S(2)}) collective-permute-start(bf16[16,3712]{1,0:T(8,128)(2,1)S(1)} %collective-permute-done.6.refs_2_), channel_id=1, source_target_pairs={{0,4},{2,6},{4,0},{6,2},{8,12},{10,14},{12,8},{14,10},{1,5},{3,7},... | collective-permute-start | bytes 356360 | tf_op jit(solution)/shard_map/ppermute | solution.py:194
  15.8 4.8 %collective-permute-start.9 = (bf16[16,3712]{1,0:T(8,128)(2,1)S(1)}, bf16[16,3712]{1,0:T(8,128)(2,1)S(1)}, u32[]{:S(2)}, u32[]{:S(2)}) collective-permute-start(bf16[16,3712]{1,0:T(8,128)(2,1)S(1)} %collective-permute-done.8.refs_3_), channel_id=1, source_target_pairs={{0,4},{2,6},{4,0},{6,2},{8,12},{10,14},{12,8},{14,10},{1,5},{3,7},... | collective-permute-start | bytes 356360 | tf_op jit(solution)/shard_map/ppermute | solution.py:194
  16.9 9.1 %collective-permute-start.12 = (bf16[16,3712]{1,0:T(8,128)(2,1)S(1)}, bf16[16,3712]{1,0:T(8,128)(2,1)S(1)}, u32[]{:S(2)}, u32[]{:S(2)}) collective-permute-start(bf16[16,3712]{1,0:T(8,128)(2,1)S(1)} %collective-permute-done.6.refs_2_), channel_id=1, source_target_pairs={{0,2},{2,0},{4,6},{6,4},{8,10},{10,8},{12,14},{14,12},{1,3},{3,1},... | collective-permute-start | bytes 356360 | tf_op jit(solution)/shard_map/ppermute | solution.py:194
  16.9 9.1 %collective-permute-start.13 = (bf16[16,3712]{1,0:T(8,128)(2,1)S(1)}, bf16[16,3712]{1,0:T(8,128)(2,1)S(1)}, u32[]{:S(2)}, u32[]{:S(2)}) collective-permute-start(bf16[16,3712]{1,0:T(8,128)(2,1)S(1)} %collective-permute-done.8.refs_3_), channel_id=1, source_target_pairs={{0,2},{2,0},{4,6},{6,4},{8,10},{10,8},{12,14},{14,12},{1,3},{3,1},... | collective-permute-start | bytes 356360 | tf_op jit(solution)/shard_map/ppermute | solution.py:194
  17.9 8.1 %collective-permute-start.10 = (bf16[16,3712]{1,0:T(8,128)(2,1)S(1)}, bf16[16,3712]{1,0:T(8,128)(2,1)S(1)}, u32[]{:S(2)}, u32[]{:S(2)}) collective-permute-start(bf16[16,3712]{1,0:T(8,128)(2,1)S(1)} %collective-permute-done.7.refs_0_), channel_id=1, source_target_pairs={{0,2},{2,0},{4,6},{6,4},{8,10},{10,8},{12,14},{14,12},{1,3},{3,1},... | collective-permute-start | bytes 356360 | tf_op jit(solution)/shard_map/ppermute | solution.py:194
  20.7 5.3 %collective-permute-start.11 = (bf16[16,3712]{1,0:T(8,128)(2,1)S(1)}, bf16[16,3712]{1,0:T(8,128)(2,1)S(1)}, u32[]{:S(2)}, u32[]{:S(2)}) collective-permute-start(bf16[16,3712]{1,0:T(8,128)(2,1)S(1)} %collective-permute-done.9.refs_1_), channel_id=1, source_target_pairs={{0,2},{2,0},{4,6},{6,4},{8,10},{10,8},{12,14},{14,12},{1,3},{3,1},... | collective-permute-start | bytes 356360 | tf_op jit(solution)/shard_map/ppermute | solution.py:194
  20.7 8.3 %collective-permute-start = (bf16[32,3712]{1,0:T(8,128)(2,1)S(1)}, bf16[32,3712]{1,0:T(8,128)(2,1)S(1)}, u32[]{:S(2)}, u32[]{:S(2)}) collective-permute-start(bf16[32,3712]{1,0:T(8,128)(2,1)S(1)} %get-tuple-element.14.refs_0_), channel_id=1, source_target_pairs={{0,4},{2,6},{4,0},{6,2},{8,12},{10,14},{12,8},{14,10},{1,5},{3,7},... | collective-permute-start | bytes 712712 | tf_op jit(solution)/shard_map/ppermute | solution.py:194
  28.4 5.2 %collective-permute-start.14 = (bf16[64,3584]{1,0:T(8,128)(2,1)S(1)}, bf16[64,3584]{1,0:T(8,128)(2,1)S(1)}, u32[]{:S(2)}, u32[]{:S(2)}) collective-permute-start(bf16[64,3584]{1,0:T(8,128)(2,1)S(1)} %get-tuple-element.22), channel_id=1, source_target_pairs={{0,2},{2,0},{4,6},{6,4},{8,10},{10,8},{12,14},{14,12},{1,3},{3,1},... | collective-permute-start | bytes 1376264 | tf_op jit(solution)/shard_map/ppermute | solution.py:194
  28.7 1.9 %collective-permute-start.1 = (bf16[32,3712]{1,0:T(8,128)(2,1)S(1)}, bf16[32,3712]{1,0:T(8,128)(2,1)S(1)}, u32[]{:S(2)}, u32[]{:S(2)}) collective-permute-start(bf16[32,3712]{1,0:T(8,128)(2,1)S(1)} %get-tuple-element.14.refs_0_), channel_id=1, source_target_pairs={{0,2},{2,0},{4,6},{6,4},{8,10},{10,8},{12,14},{14,12},{1,3},{3,1},... | collective-permute-start | bytes 712712 | tf_op jit(solution)/shard_map/ppermute | solution.py:194
  28.9 2.0 %collective-permute-start.2 = (bf16[32,3712]{1,0:T(8,128)(2,1)S(1)}, bf16[32,3712]{1,0:T(8,128)(2,1)S(1)}, u32[]{:S(2)}, u32[]{:S(2)}) collective-permute-start(bf16[32,3712]{1,0:T(8,128)(2,1)S(1)} %collective-permute-done.refs_1_), channel_id=1, source_target_pairs={{0,2},{2,0},{4,6},{6,4},{8,10},{10,8},{12,14},{14,12},{1,3},{3,1},... | collective-permute-start | bytes 712712 | tf_op jit(solution)/shard_map/ppermute | solution.py:194
  33.2 2.5 %collective-permute-start.3 = (bf16[64,3584]{1,0:T(8,128)(2,1)S(1)}, bf16[64,3584]{1,0:T(8,128)(2,1)S(1)}, u32[]{:S(2)}, u32[]{:S(2)}) collective-permute-start(bf16[64,3584]{1,0:T(8,128)(2,1)S(1)} %get-tuple-element.19), channel_id=1, source_target_pairs={{0,2},{2,0},{4,6},{6,4},{8,10},{10,8},{12,14},{14,12},{1,3},{3,1},... | collective-permute-start | bytes 1376264 | tf_op jit(solution)/shard_map/ppermute | solution.py:194
  33.6 6.1 %collective-permute-start.16 = (bf16[16,3584]{1,0:T(8,128)(2,1)S(1)}, bf16[16,3584]{1,0:T(8,128)(2,1)S(1)}, u32[]{:S(2)}, u32[]{:S(2)}) collective-permute-start(bf16[16,3584]{1,0:T(8,128)(2,1)S(1)} %get-tuple-element.24), channel_id=1, source_target_pairs={{0,1},{1,0},{2,3},{3,2},{4,5},{5,4},{6,7},{7,6},{8,9},{9,8},{10,11... | collective-permute-start | bytes 344072 | tf_op jit(solution)/shard_map/ppermute | solution.py:200
  35.1 10.8 %collective-permute-start.15 = (bf16[16,3584]{1,0:T(8,128)(2,1)S(1)}, bf16[16,3584]{1,0:T(8,128)(2,1)S(1)}, u32[]{:S(2)}, u32[]{:S(2)}) collective-permute-start(bf16[16,3584]{1,0:T(8,128)(2,1)S(1)} %get-tuple-element.23), channel_id=1, source_target_pairs={{0,1},{1,0},{2,3},{3,2},{4,5},{5,4},{6,7},{7,6},{8,9},{9,8},{10,11... | collective-permute-start | bytes 344072 | tf_op jit(solution)/shard_map/ppermute | solution.py:200
  35.8 8.5 %collective-permute-start.4 = (bf16[32,3584]{1,0:T(8,128)(2,1)S(1)}, bf16[32,3584]{1,0:T(8,128)(2,1)S(1)}, u32[]{:S(2)}, u32[]{:S(2)}) collective-permute-start(bf16[32,3584]{1,0:T(8,128)(2,1)S(1)} %add_convert_fusion.1), channel_id=1, source_target_pairs={{0,4},{2,6},{4,0},{6,2},{8,12},{10,14},{12,8},{14,10},{1,5},{3,7},... | collective-permute-start | bytes 688136 | tf_op jit(solution)/shard_map/ppermute | solution.py:194
  39.7 6.2 %collective-permute-start.17 = (bf16[16,3584]{1,0:T(8,128)(2,1)S(1)}, bf16[16,3584]{1,0:T(8,128)(2,1)S(1)}, u32[]{:S(2)}, u32[]{:S(2)}) collective-permute-start(bf16[16,3584]{1,0:T(8,128)(2,1)S(1)} %add_convert_fusion.4), channel_id=1, source_target_pairs={{0,4},{2,6},{4,0},{6,2},{8,12},{10,14},{12,8},{14,10},{1,5},{3,7},... | collective-permute-start | bytes 344072 | tf_op jit(solution)/shard_map/ppermute | solution.py:194
  44.4 5.1 %collective-permute-start.5 = (bf16[16,3584]{1,0:T(8,128)(2,1)S(1)}, bf16[16,3584]{1,0:T(8,128)(2,1)S(1)}, u32[]{:S(2)}, u32[]{:S(2)}) collective-permute-start(bf16[16,3584]{1,0:T(8,128)(2,1)S(1)} %slice.59), channel_id=1, source_target_pairs={{0,1},{1,0},{2,3},{3,2},{4,5},{5,4},{6,7},{7,6},{8,9},{9,8},{10,11... | collective-permute-start | bytes 344072 | tf_op jit(solution)/shard_map/ppermute | solution.py:200
  46.0 7.6 %collective-permute-start.18 = (bf16[16,3584]{1,0:T(8,128)(2,1)S(1)}, bf16[16,3584]{1,0:T(8,128)(2,1)S(1)}, u32[]{:S(2)}, u32[]{:S(2)}) collective-permute-start(bf16[16,3584]{1,0:T(8,128)(2,1)S(1)} %add_convert_fusion.3), channel_id=1, source_target_pairs={{0,8},{2,10},{4,12},{6,14},{8,0},{10,2},{12,4},{14,6},{1,9},{3,11}... | collective-permute-start | bytes 344072 | tf_op jit(solution)/shard_map/ppermute | solution.py:194
  53.7 4.9 %collective-permute-start.19 = (bf16[16,3584]{1,0:T(8,128)(2,1)S(1)}, bf16[16,3584]{1,0:T(8,128)(2,1)S(1)}, u32[]{:S(2)}, u32[]{:S(2)}) collective-permute-start(bf16[16,3584]{1,0:T(8,128)(2,1)S(1)} %add_convert_fusion.2), channel_id=1, source_target_pairs={{0,1},{1,0},{2,3},{3,2},{4,5},{5,4},{6,7},{7,6},{8,9},{9,8},{10,11... | collective-permute-start | bytes 344072 | tf_op jit(solution)/shard_map/ppermute | solution.py:200

commit v4 on v3

--- a/solution.py
+++ b/solution.py
@@ -199,6 +199,10 @@
     def pair(value):
         return lax.ppermute(value, "attn", [(0, 1), (1, 0)])
 
+    def cross(value, bit):
+        order = [(i, i ^ (2 * bit + 1)) for i in range(2 * experts)]
+        return lax.ppermute(value, ("expert", "attn"), order)
+
     def run(*blocks):
         return ffn(blocks, *weights, expert_at, experts)
 
@@ -213,16 +217,15 @@
     near_sum = swap(add(keep[count:], got[count:]), 2)
     both = add(keep[:count], got[:count], near_sum)
 
-    far_pair = pair(far)
-    blocks = (swap(far, 2), swap(far_pair, 2), far, far_pair)
+    blocks = (far, pair(far), swap(far, 2), cross(far, 2))
     far_keep, far_send = run(*blocks, *[core(b) for b in blocks])
     far_got = core(far_send)
-    total = [add(far_keep[i : i + half], far_got[i : i + half]) for i in range(0, 2 * count, half)]
-    relay_other = pair(total[1])
-    far_other = pair(total[3])
+    parts = [add(far_keep[i : i + half], far_got[i : i + half]) for i in range(0, 2 * count, half)]
+    cross_sum = cross(parts[3], 2)
+    far_other = pair(parts[1])
+    relay_sum = swap(parts[2], 2)
+    far_sum = swap(add(parts[0], far_other, relay_sum, cross_sum), 4)
     near_other = pair(both[half:])
-    relay_sum = swap(add(total[0], relay_other), 2)
-    far_sum = swap(add(total[2], far_other, relay_sum), 4)
     final = add(both[:half], near_other, far_sum)
     other = pair(final)
     return jnp.where(

time: 59.4 us -> 59.7 us (level)
  waiting for transfers between devices: 27.4 us -> 30.6 us
  starting transfers between devices: 20.7 us -> 17.7 us
    ppermute x5 -> x4, starting transfers between devices: 6.72 us -> 2.21 us  [pair(): return lax.ppermute(value, 'attn', [(0, 1), (1, 0)])]
    ppermute x0 -> x2, waiting for transfers between devices: none -> 4.09 us  [cross(): return lax.ppermute(value, ('expert', 'attn'), order)]
    ppermute x15 -> x14, waiting for transfers between devices: 18.5 us -> 15 us  [swap(): return lax.ppermute(value, 'expert', [(i, i ^ bit) for i in range(experts)])]
    ppermute x0 -> x2, starting transfers between devices: none -> 2.72 us  [cross(): return lax.ppermute(value, ('expert', 'attn'), order)]
    ppermute x5 -> x4, waiting for transfers between devices: 8.84 us -> 11.5 us  [pair(): return lax.ppermute(value, 'attn', [(0, 1), (1, 0)])]
    ppermute x15 -> x14, starting transfers between devices: 14 us -> 12.8 us  [swap(): return lax.ppermute(value, 'expert', [(i, i ^ bit) for i in range(experts)])]
  transfers between devices with their start and end apart: 20 -> 20, of which waited for: 10 -> 12; matrix products, arithmetic and copies ran while one was open for 1% -> 1% of each run, Pallas kernels for 15% -> 15%
where the time goes in v4:
time: 59.7 us; the launch traced here: 59.5 us
  waiting for transfers between devices  30.6 us (51%)
  starting transfers between devices  17.7 us (30%)
  Pallas kernels  9.97 us (17%)
  other arithmetic  1.07 us (2%)
    ppermute x14, waiting for transfers between devices, swap(): return lax.ppermute(value, 'expert', [(i, i ^ bit) for i in range(experts)])  15 us
    ppermute x14, starting transfers between devices, swap(): return lax.ppermute(value, 'expert', [(i, i ^ bit) for i in range(experts)])  12.8 us
    ppermute x4, waiting for transfers between devices, pair(): return lax.ppermute(value, 'attn', [(0, 1), (1, 0)])  11.5 us
    pallas_call x2, Pallas kernels, ffn(): pl.pallas_call(functools.partial(ffn_kernel, experts, len(x_blocks)), out...  4.65 us
    pallas_call x1, Pallas kernels, load(): pl.pallas_call(load_kernel, out_shape=tuple((jax.ShapeDtypeStruct(a.shape...  4.23 us
    ppermute x2, waiting for transfers between devices, cross(): return lax.ppermute(value, ('expert', 'attn'), order)  4.09 us
    ppermute x2, starting transfers between devices, cross(): return lax.ppermute(value, ('expert', 'attn'), order)  2.72 us
    ppermute x4, starting transfers between devices, pair(): return lax.ppermute(value, 'attn', [(0, 1), (1, 0)])  2.21 us
  transfers between devices with their start and end apart: 20, of which 12 were waited for; matrix products, arithmetic and copies ran while one was open for 1% of the time, Pallas kernels for 15%

profile of v4, /device:TPU:0, one launch (start us, length us, event | category | flops | bytes accessed | tf_op | source)
XLA Modules:
  0.0 59.5 jit_solution(3598023560724826028)
XLA Ops:
  0.0 1.1 %prepare.1 = (bf16[32,3712]{1,0:T(8,128)(2,1)S(1)}, bf16[16,3712]{1,0:T(8,128)(2,1)S(1)}) custom-call(s32[1]{0:T(128)} %bitcast.1.at_ref, s32[1]{0:T(128)} %bitcast.expert_ref.at_ref, s32[8]{0:T(128)} %plan_hbm.1, s32[8,32]{1,0:T(8,128)} %bitcast.10, f32[8,32]{1,0:T(8,128)} %bitcast.11, bf16[32,3584]{1,0:T(8,128)(2,1)} %tok_hbm.1), custom_call_target="tpu_custom_call" | custom-call | tf_op jit(solution)/shard_map/prepare/pallas_call | solution.py:71
  1.1 4.1 %collective-permute-start.6 = (bf16[16,3712]{1,0:T(8,128)(2,1)S(1)}, bf16[16,3712]{1,0:T(8,128)(2,1)S(1)}, u32[]{:S(2)}, u32[]{:S(2)}) collective-permute-start(bf16[16,3712]{1,0:T(8,128)(2,1)S(1)} %get-tuple-element.20), channel_id=1, source_target_pairs={{0,8},{2,10},{4,12},{6,14},{8,0},{10,2},{12,4},{14,6},{1,9},{3,11}... | collective-permute-start | bytes 356360 | tf_op jit(solution)/shard_map/ppermute | solution.py:194
  5.2 5.8 %collective-permute-done.6.refs_0_ = bf16[16,3712]{1,0:T(8,128)(2,1)S(1)} collective-permute-done((bf16[16,3712]{1,0:T(8,128)(2,1)S(1)}, bf16[16,3712]{1,0:T(8,128)(2,1)S(1)}, u32[]{:S(2)}, u32[]{:S(2)}) %collective-permute-start.6) | collective-permute-done | bytes 118816 | tf_op jit(solution)/shard_map/ppermute | solution.py:194
  11.0 1.5 %collective-permute-start.7 = (bf16[16,3712]{1,0:T(8,128)(2,1)S(1)}, bf16[16,3712]{1,0:T(8,128)(2,1)S(1)}, u32[]{:S(2)}, u32[]{:S(2)}) collective-permute-start(bf16[16,3712]{1,0:T(8,128)(2,1)S(1)} %collective-permute-done.6.refs_0_), channel_id=1, source_target_pairs={{0,1},{1,0},{2,3},{3,2},{4,5},{5,4},{6,7},{7,6},{8,9},{9,8},{10,11... | collective-permute-start | bytes 356360 | tf_op jit(solution)/shard_map/ppermute | solution.py:200
  12.6 0.7 %collective-permute-start.8 = (bf16[16,3712]{1,0:T(8,128)(2,1)S(1)}, bf16[16,3712]{1,0:T(8,128)(2,1)S(1)}, u32[]{:S(2)}, u32[]{:S(2)}) collective-permute-start(bf16[16,3712]{1,0:T(8,128)(2,1)S(1)} %collective-permute-done.6.refs_0_), channel_id=1, source_target_pairs={{0,4},{2,6},{4,0},{6,2},{8,12},{10,14},{12,8},{14,10},{1,5},{3,7},... | collective-permute-start | bytes 356360 | tf_op jit(solution)/shard_map/ppermute | solution.py:194
  13.2 1.3 %collective-permute-start.9 = (bf16[16,3712]{1,0:T(8,128)(2,1)S(1)}, bf16[16,3712]{1,0:T(8,128)(2,1)S(1)}, u32[]{:S(2)}, u32[]{:S(2)}) collective-permute-start(bf16[16,3712]{1,0:T(8,128)(2,1)S(1)} %collective-permute-done.6.refs_0_), channel_id=1, source_target_pairs={{0,5},{1,4},{2,7},{3,6},{4,1},{5,0},{6,3},{7,2},{8,13},{9,12},{10,... | collective-permute-start | bytes 356360 | tf_op jit(solution)/shard_map/ppermute | solution.py:204
  14.5 1.7 %collective-permute-done.7.refs_1_ = bf16[16,3712]{1,0:T(8,128)(2,1)S(1)} collective-permute-done((bf16[16,3712]{1,0:T(8,128)(2,1)S(1)}, bf16[16,3712]{1,0:T(8,128)(2,1)S(1)}, u32[]{:S(2)}, u32[]{:S(2)}) %collective-permute-start.7) | collective-permute-done | bytes 118816 | tf_op jit(solution)/shard_map/ppermute | solution.py:200
  16.2 1.6 %collective-permute-done.8.refs_2_ = bf16[16,3712]{1,0:T(8,128)(2,1)S(1)} collective-permute-done((bf16[16,3712]{1,0:T(8,128)(2,1)S(1)}, bf16[16,3712]{1,0:T(8,128)(2,1)S(1)}, u32[]{:S(2)}, u32[]{:S(2)}) %collective-permute-start.8) | collective-permute-done | bytes 118816 | tf_op jit(solution)/shard_map/ppermute | solution.py:194
  17.8 2.1 %collective-permute-done.9.refs_3_ = bf16[16,3712]{1,0:T(8,128)(2,1)S(1)} collective-permute-done((bf16[16,3712]{1,0:T(8,128)(2,1)S(1)}, bf16[16,3712]{1,0:T(8,128)(2,1)S(1)}, u32[]{:S(2)}, u32[]{:S(2)}) %collective-permute-start.9) | collective-permute-done | bytes 118816 | tf_op jit(solution)/shard_map/ppermute | solution.py:204
  19.9 0.8 %collective-permute-start = (bf16[32,3712]{1,0:T(8,128)(2,1)S(1)}, bf16[32,3712]{1,0:T(8,128)(2,1)S(1)}, u32[]{:S(2)}, u32[]{:S(2)}) collective-permute-start(bf16[32,3712]{1,0:T(8,128)(2,1)S(1)} %get-tuple-element.14.refs_0_), channel_id=1, source_target_pairs={{0,4},{2,6},{4,0},{6,2},{8,12},{10,14},{12,8},{14,10},{1,5},{3,7},... | collective-permute-start | bytes 712712 | tf_op jit(solution)/shard_map/ppermute | solution.py:194
  20.6 4.2 %load.1 = (bf16[3584,512]{1,0:T(8,128)(2,1)S(1)}, bf16[3584,512]{1,0:T(8,128)(2,1)S(1)}, bf16[3584,512]{1,0:T(8,128)(2,1)S(1)}) custom-call(bf16[3584,512]{1,0:T(8,128)(2,1)} %bitcast.7, bf16[3584,512]{1,0:T(8,128)(2,1)} %bitcast.8, bf16[3584,512]{1,0:T(8,128)(2,1)} %bitcast.9), custom_call_target="tpu_custom_call" | custom-call | bytes 22020096 | tf_op jit(solution)/shard_map/load/pallas_call | solution.py:105
  24.9 2.4 %ffn.3 = (bf16[64,3584]{1,0:T(8,128)(2,1)S(1)}, bf16[64,3584]{1,0:T(8,128)(2,1)S(1)}) custom-call(s32[1]{0:T(128)} %bitcast.expert_ref.at_ref, bf16[16,3712]{1,0:T(8,128)(2,1)S(1)} %collective-permute-done.6.refs_0_, bf16[16,3712]{1,0:T(8,128)(2,1)S(1)} %collective-permute-done.7.refs_1_, bf16[16,3712]{1,0:T(8,128)(2,1)S(1)} %collective-permute-done.8.refs_2_, ...), custom_call_target="tpu_custom_call" | custom-call | flops 1409286144 | bytes 14680064 | tf_op jit(solution)/shard_map/ffn/pallas_call | solution.py:155
  27.3 0.3 collective-permute-start.14
  27.5 0.3 collective-permute-start.1
  27.8 0.2 collective-permute-done.refs_1_
  28.1 1.4 %collective-permute-done.1.refs_2_ = bf16[32,3712]{1,0:T(8,128)(2,1)S(1)} collective-permute-done((bf16[32,3712]{1,0:T(8,128)(2,1)S(1)}, bf16[32,3712]{1,0:T(8,128)(2,1)S(1)}, u32[]{:S(2)}, u32[]{:S(2)}) %collective-permute-start.1) | collective-permute-done | bytes 237600 | tf_op jit(solution)/shard_map/ppermute | solution.py:194
  29.5 0.3 collective-permute-done.2.refs_3_
  29.8 2.3 %ffn.2 = (bf16[64,3584]{1,0:T(8,128)(2,1)S(1)}, bf16[64,3584]{1,0:T(8,128)(2,1)S(1)}) custom-call(s32[1]{0:T(128)} %bitcast.expert_ref.at_ref, bf16[32,3712]{1,0:T(8,128)(2,1)S(1)} %get-tuple-element.14.refs_0_, bf16[32,3712]{1,0:T(8,128)(2,1)S(1)} %collective-permute-done.refs_1_, bf16[32,3712]{1,0:T(8,128)(2,1)S(1)} %collective-permute-done.1.refs_2_, ...), custom_call_target="tpu_custom_call" | custom-call | flops 1409286144 | bytes 14680064 | tf_op jit(solution)/shard_map/ffn/pallas_call | solution.py:155
  32.1 0.3 collective-permute-start.3
  32.4 0.1 add_convert_fusion.6
  32.5 1.4 %collective-permute-start.17 = (bf16[16,3584]{1,0:T(8,128)(2,1)S(1)}, bf16[16,3584]{1,0:T(8,128)(2,1)S(1)}, u32[]{:S(2)}, u32[]{:S(2)}) collective-permute-start(bf16[16,3584]{1,0:T(8,128)(2,1)S(1)} %get-tuple-element.24), channel_id=1, source_target_pairs={{0,5},{1,4},{2,7},{3,6},{4,1},{5,0},{6,3},{7,2},{8,13},{9,12},{10,... | collective-permute-start | bytes 344072 | tf_op jit(solution)/shard_map/ppermute | solution.py:204
  34.0 1.6 %collective-permute-start.16 = (bf16[16,3584]{1,0:T(8,128)(2,1)S(1)}, bf16[16,3584]{1,0:T(8,128)(2,1)S(1)}, u32[]{:S(2)}, u32[]{:S(2)}) collective-permute-start(bf16[16,3584]{1,0:T(8,128)(2,1)S(1)} %get-tuple-element.25), channel_id=1, source_target_pairs={{0,4},{2,6},{4,0},{6,2},{8,12},{10,14},{12,8},{14,10},{1,5},{3,7},... | collective-permute-start | bytes 344072 | tf_op jit(solution)/shard_map/ppermute | solution.py:194
  35.5 0.5 collective-permute-start.15
  36.1 1.3 %collective-permute-start.4 = (bf16[32,3584]{1,0:T(8,128)(2,1)S(1)}, bf16[32,3584]{1,0:T(8,128)(2,1)S(1)}, u32[]{:S(2)}, u32[]{:S(2)}) collective-permute-start(bf16[32,3584]{1,0:T(8,128)(2,1)S(1)} %add_convert_fusion.1), channel_id=1, source_target_pairs={{0,4},{2,6},{4,0},{6,2},{8,12},{10,14},{12,8},{14,10},{1,5},{3,7},... | collective-permute-start | bytes 688136 | tf_op jit(solution)/shard_map/ppermute | solution.py:194
  37.5 2.0 %collective-permute-done.17 = bf16[16,3584]{1,0:T(8,128)(2,1)S(1)} collective-permute-done((bf16[16,3584]{1,0:T(8,128)(2,1)S(1)}, bf16[16,3584]{1,0:T(8,128)(2,1)S(1)}, u32[]{:S(2)}, u32[]{:S(2)}) %collective-permute-start.17) | collective-permute-done | bytes 114720 | tf_op jit(solution)/shard_map/ppermute | solution.py:204
  39.5 2.5 %collective-permute-done.16 = bf16[16,3584]{1,0:T(8,128)(2,1)S(1)} collective-permute-done((bf16[16,3584]{1,0:T(8,128)(2,1)S(1)}, bf16[16,3584]{1,0:T(8,128)(2,1)S(1)}, u32[]{:S(2)}, u32[]{:S(2)}) %collective-permute-start.16) | collective-permute-done | bytes 114720 | tf_op jit(solution)/shard_map/ppermute | solution.py:194
  42.1 3.4 %collective-permute-start.18 = (bf16[16,3584]{1,0:T(8,128)(2,1)S(1)}, bf16[16,3584]{1,0:T(8,128)(2,1)S(1)}, u32[]{:S(2)}, u32[]{:S(2)}) collective-permute-start(bf16[16,3584]{1,0:T(8,128)(2,1)S(1)} %add_convert_fusion.3), channel_id=1, source_target_pairs={{0,8},{2,10},{4,12},{6,14},{8,0},{10,2},{12,4},{14,6},{1,9},{3,11}... | collective-permute-start | bytes 344072 | tf_op jit(solution)/shard_map/ppermute | solution.py:194
  45.5 3.2 %collective-permute-done.4 = bf16[32,3584]{1,0:T(8,128)(2,1)S(1)} collective-permute-done((bf16[32,3584]{1,0:T(8,128)(2,1)S(1)}, bf16[32,3584]{1,0:T(8,128)(2,1)S(1)}, u32[]{:S(2)}, u32[]{:S(2)}) %collective-permute-start.4) | collective-permute-done | bytes 229408 | tf_op jit(solution)/shard_map/ppermute | solution.py:194
  48.7 0.1 add_convert_fusion
  48.9 5.0 %collective-permute-done.5 = bf16[16,3584]{1,0:T(8,128)(2,1)S(1)} collective-permute-done((bf16[16,3584]{1,0:T(8,128)(2,1)S(1)}, bf16[16,3584]{1,0:T(8,128)(2,1)S(1)}, u32[]{:S(2)}, u32[]{:S(2)}) %collective-permute-start.5) | collective-permute-done | bytes 114720 | tf_op jit(solution)/shard_map/ppermute | solution.py:200
  54.0 4.8 %collective-permute-done.19 = bf16[16,3584]{1,0:T(8,128)(2,1)S(1)} collective-permute-done((bf16[16,3584]{1,0:T(8,128)(2,1)S(1)}, bf16[16,3584]{1,0:T(8,128)(2,1)S(1)}, u32[]{:S(2)}, u32[]{:S(2)}) %collective-permute-start.19) | collective-permute-done | bytes 114720 | tf_op jit(solution)/shard_map/ppermute | solution.py:200
  58.8 0.7 %maximum_select_fusion = bf16[32,3584]{1,0:T(8,128)(2,1)} fusion(bf16[16,3584]{1,0:T(8,128)(2,1)S(1)} %collective-permute-done.19, bf16[16,3584]{1,0:T(8,128)(2,1)S(1)} %add_convert_fusion.2, pred[]{:T(512)S(6)} %eq.3), kind=kLoop, calls=%fused_computation.2 | loop fusion | flops 1032192 | bytes 458753 | tf_op jit(solution)/shard_map/jit(_where)/select_n | solution.py:231
  (19 shorter events, 0.4 us)
Async XLA Ops:
  1.1 9.9 %collective-permute-start.6 = (bf16[16,3712]{1,0:T(8,128)(2,1)S(1)}, bf16[16,3712]{1,0:T(8,128)(2,1)S(1)}, u32[]{:S(2)}, u32[]{:S(2)}) collective-permute-start(bf16[16,3712]{1,0:T(8,128)(2,1)S(1)} %get-tuple-element.20), channel_id=1, source_target_pairs={{0,8},{2,10},{4,12},{6,14},{8,0},{10,2},{12,4},{14,6},{1,9},{3,11}... | collective-permute-start | bytes 356360 | tf_op jit(solution)/shard_map/ppermute | solution.py:194
  11.0 5.2 %collective-permute-start.7 = (bf16[16,3712]{1,0:T(8,128)(2,1)S(1)}, bf16[16,3712]{1,0:T(8,128)(2,1)S(1)}, u32[]{:S(2)}, u32[]{:S(2)}) collective-permute-start(bf16[16,3712]{1,0:T(8,128)(2,1)S(1)} %collective-permute-done.6.refs_0_), channel_id=1, source_target_pairs={{0,1},{1,0},{2,3},{3,2},{4,5},{5,4},{6,7},{7,6},{8,9},{9,8},{10,11... | collective-permute-start | bytes 356360 | tf_op jit(solution)/shard_map/ppermute | solution.py:200
  12.6 5.2 %collective-permute-start.8 = (bf16[16,3712]{1,0:T(8,128)(2,1)S(1)}, bf16[16,3712]{1,0:T(8,128)(2,1)S(1)}, u32[]{:S(2)}, u32[]{:S(2)}) collective-permute-start(bf16[16,3712]{1,0:T(8,128)(2,1)S(1)} %collective-permute-done.6.refs_0_), channel_id=1, source_target_pairs={{0,4},{2,6},{4,0},{6,2},{8,12},{10,14},{12,8},{14,10},{1,5},{3,7},... | collective-permute-start | bytes 356360 | tf_op jit(solution)/shard_map/ppermute | solution.py:194
  13.2 6.6 %collective-permute-start.9 = (bf16[16,3712]{1,0:T(8,128)(2,1)S(1)}, bf16[16,3712]{1,0:T(8,128)(2,1)S(1)}, u32[]{:S(2)}, u32[]{:S(2)}) collective-permute-start(bf16[16,3712]{1,0:T(8,128)(2,1)S(1)} %collective-permute-done.6.refs_0_), channel_id=1, source_target_pairs={{0,5},{1,4},{2,7},{3,6},{4,1},{5,0},{6,3},{7,2},{8,13},{9,12},{10,... | collective-permute-start | bytes 356360 | tf_op jit(solution)/shard_map/ppermute | solution.py:204
  14.5 10.4 %collective-permute-start.10 = (bf16[16,3712]{1,0:T(8,128)(2,1)S(1)}, bf16[16,3712]{1,0:T(8,128)(2,1)S(1)}, u32[]{:S(2)}, u32[]{:S(2)}) collective-permute-start(bf16[16,3712]{1,0:T(8,128)(2,1)S(1)} %collective-permute-done.6.refs_0_), channel_id=1, source_target_pairs={{0,2},{2,0},{4,6},{6,4},{8,10},{10,8},{12,14},{14,12},{1,3},{3,1},... | collective-permute-start | bytes 356360 | tf_op jit(solution)/shard_map/ppermute | solution.py:194
  16.2 8.7 %collective-permute-start.11 = (bf16[16,3712]{1,0:T(8,128)(2,1)S(1)}, bf16[16,3712]{1,0:T(8,128)(2,1)S(1)}, u32[]{:S(2)}, u32[]{:S(2)}) collective-permute-start(bf16[16,3712]{1,0:T(8,128)(2,1)S(1)} %collective-permute-done.7.refs_1_), channel_id=1, source_target_pairs={{0,2},{2,0},{4,6},{6,4},{8,10},{10,8},{12,14},{14,12},{1,3},{3,1},... | collective-permute-start | bytes 356360 | tf_op jit(solution)/shard_map/ppermute | solution.py:194
  17.8 7.1 %collective-permute-start.12 = (bf16[16,3712]{1,0:T(8,128)(2,1)S(1)}, bf16[16,3712]{1,0:T(8,128)(2,1)S(1)}, u32[]{:S(2)}, u32[]{:S(2)}) collective-permute-start(bf16[16,3712]{1,0:T(8,128)(2,1)S(1)} %collective-permute-done.8.refs_2_), channel_id=1, source_target_pairs={{0,2},{2,0},{4,6},{6,4},{8,10},{10,8},{12,14},{14,12},{1,3},{3,1},... | collective-permute-start | bytes 356360 | tf_op jit(solution)/shard_map/ppermute | solution.py:194
  19.9 5.0 %collective-permute-start.13 = (bf16[16,3712]{1,0:T(8,128)(2,1)S(1)}, bf16[16,3712]{1,0:T(8,128)(2,1)S(1)}, u32[]{:S(2)}, u32[]{:S(2)}) collective-permute-start(bf16[16,3712]{1,0:T(8,128)(2,1)S(1)} %collective-permute-done.9.refs_3_), channel_id=1, source_target_pairs={{0,2},{2,0},{4,6},{6,4},{8,10},{10,8},{12,14},{14,12},{1,3},{3,1},... | collective-permute-start | bytes 356360 | tf_op jit(solution)/shard_map/ppermute | solution.py:194
  19.9 8.2 %collective-permute-start = (bf16[32,3712]{1,0:T(8,128)(2,1)S(1)}, bf16[32,3712]{1,0:T(8,128)(2,1)S(1)}, u32[]{:S(2)}, u32[]{:S(2)}) collective-permute-start(bf16[32,3712]{1,0:T(8,128)(2,1)S(1)} %get-tuple-element.14.refs_0_), channel_id=1, source_target_pairs={{0,4},{2,6},{4,0},{6,2},{8,12},{10,14},{12,8},{14,10},{1,5},{3,7},... | collective-permute-start | bytes 712712 | tf_op jit(solution)/shard_map/ppermute | solution.py:194
  27.3 5.2 %collective-permute-start.14 = (bf16[64,3584]{1,0:T(8,128)(2,1)S(1)}, bf16[64,3584]{1,0:T(8,128)(2,1)S(1)}, u32[]{:S(2)}, u32[]{:S(2)}) collective-permute-start(bf16[64,3584]{1,0:T(8,128)(2,1)S(1)} %get-tuple-element.22), channel_id=1, source_target_pairs={{0,2},{2,0},{4,6},{6,4},{8,10},{10,8},{12,14},{14,12},{1,3},{3,1},... | collective-permute-start | bytes 1376264 | tf_op jit(solution)/shard_map/ppermute | solution.py:194
  27.5 1.9 %collective-permute-start.1 = (bf16[32,3712]{1,0:T(8,128)(2,1)S(1)}, bf16[32,3712]{1,0:T(8,128)(2,1)S(1)}, u32[]{:S(2)}, u32[]{:S(2)}) collective-permute-start(bf16[32,3712]{1,0:T(8,128)(2,1)S(1)} %get-tuple-element.14.refs_0_), channel_id=1, source_target_pairs={{0,2},{2,0},{4,6},{6,4},{8,10},{10,8},{12,14},{14,12},{1,3},{3,1},... | collective-permute-start | bytes 712712 | tf_op jit(solution)/shard_map/ppermute | solution.py:194
  28.1 1.8 %collective-permute-start.2 = (bf16[32,3712]{1,0:T(8,128)(2,1)S(1)}, bf16[32,3712]{1,0:T(8,128)(2,1)S(1)}, u32[]{:S(2)}, u32[]{:S(2)}) collective-permute-start(bf16[32,3712]{1,0:T(8,128)(2,1)S(1)} %collective-permute-done.refs_1_), channel_id=1, source_target_pairs={{0,2},{2,0},{4,6},{6,4},{8,10},{10,8},{12,14},{14,12},{1,3},{3,1},... | collective-permute-start | bytes 712712 | tf_op jit(solution)/shard_map/ppermute | solution.py:194
  32.1 3.9 %collective-permute-start.3 = (bf16[64,3584]{1,0:T(8,128)(2,1)S(1)}, bf16[64,3584]{1,0:T(8,128)(2,1)S(1)}, u32[]{:S(2)}, u32[]{:S(2)}) collective-permute-start(bf16[64,3584]{1,0:T(8,128)(2,1)S(1)} %get-tuple-element.19), channel_id=1, source_target_pairs={{0,2},{2,0},{4,6},{6,4},{8,10},{10,8},{12,14},{14,12},{1,3},{3,1},... | collective-permute-start | bytes 1376264 | tf_op jit(solution)/shard_map/ppermute | solution.py:194
  32.5 7.0 %collective-permute-start.17 = (bf16[16,3584]{1,0:T(8,128)(2,1)S(1)}, bf16[16,3584]{1,0:T(8,128)(2,1)S(1)}, u32[]{:S(2)}, u32[]{:S(2)}) collective-permute-start(bf16[16,3584]{1,0:T(8,128)(2,1)S(1)} %get-tuple-element.24), channel_id=1, source_target_pairs={{0,5},{1,4},{2,7},{3,6},{4,1},{5,0},{6,3},{7,2},{8,13},{9,12},{10,... | collective-permute-start | bytes 344072 | tf_op jit(solution)/shard_map/ppermute | solution.py:204
  34.0 8.0 %collective-permute-start.16 = (bf16[16,3584]{1,0:T(8,128)(2,1)S(1)}, bf16[16,3584]{1,0:T(8,128)(2,1)S(1)}, u32[]{:S(2)}, u32[]{:S(2)}) collective-permute-start(bf16[16,3584]{1,0:T(8,128)(2,1)S(1)} %get-tuple-element.25), channel_id=1, source_target_pairs={{0,4},{2,6},{4,0},{6,2},{8,12},{10,14},{12,8},{14,10},{1,5},{3,7},... | collective-permute-start | bytes 344072 | tf_op jit(solution)/shard_map/ppermute | solution.py:194
  35.5 6.5 %collective-permute-start.15 = (bf16[16,3584]{1,0:T(8,128)(2,1)S(1)}, bf16[16,3584]{1,0:T(8,128)(2,1)S(1)}, u32[]{:S(2)}, u32[]{:S(2)}) collective-permute-start(bf16[16,3584]{1,0:T(8,128)(2,1)S(1)} %get-tuple-element.23), channel_id=1, source_target_pairs={{0,1},{1,0},{2,3},{3,2},{4,5},{5,4},{6,7},{7,6},{8,9},{9,8},{10,11... | collective-permute-start | bytes 344072 | tf_op jit(solution)/shard_map/ppermute | solution.py:200
  36.1 12.5 %collective-permute-start.4 = (bf16[32,3584]{1,0:T(8,128)(2,1)S(1)}, bf16[32,3584]{1,0:T(8,128)(2,1)S(1)}, u32[]{:S(2)}, u32[]{:S(2)}) collective-permute-start(bf16[32,3584]{1,0:T(8,128)(2,1)S(1)} %add_convert_fusion.1), channel_id=1, source_target_pairs={{0,4},{2,6},{4,0},{6,2},{8,12},{10,14},{12,8},{14,10},{1,5},{3,7},... | collective-permute-start | bytes 688136 | tf_op jit(solution)/shard_map/ppermute | solution.py:194
  42.1 6.8 %collective-permute-start.18 = (bf16[16,3584]{1,0:T(8,128)(2,1)S(1)}, bf16[16,3584]{1,0:T(8,128)(2,1)S(1)}, u32[]{:S(2)}, u32[]{:S(2)}) collective-permute-start(bf16[16,3584]{1,0:T(8,128)(2,1)S(1)} %add_convert_fusion.3), channel_id=1, source_target_pairs={{0,8},{2,10},{4,12},{6,14},{8,0},{10,2},{12,4},{14,6},{1,9},{3,11}... | collective-permute-start | bytes 344072 | tf_op jit(solution)/shard_map/ppermute | solution.py:194
  48.8 5.1 %collective-permute-start.5 = (bf16[16,3584]{1,0:T(8,128)(2,1)S(1)}, bf16[16,3584]{1,0:T(8,128)(2,1)S(1)}, u32[]{:S(2)}, u32[]{:S(2)}) collective-permute-start(bf16[16,3584]{1,0:T(8,128)(2,1)S(1)} %slice.59), channel_id=1, source_target_pairs={{0,1},{1,0},{2,3},{3,2},{4,5},{5,4},{6,7},{7,6},{8,9},{9,8},{10,11... | collective-permute-start | bytes 344072 | tf_op jit(solution)/shard_map/ppermute | solution.py:200
  53.9 4.9 %collective-permute-start.19 = (bf16[16,3584]{1,0:T(8,128)(2,1)S(1)}, bf16[16,3584]{1,0:T(8,128)(2,1)S(1)}, u32[]{:S(2)}, u32[]{:S(2)}) collective-permute-start(bf16[16,3584]{1,0:T(8,128)(2,1)S(1)} %add_convert_fusion.2), channel_id=1, source_target_pairs={{0,1},{1,0},{2,3},{3,2},{4,5},{5,4},{6,7},{7,6},{8,9},{9,8},{10,11... | collective-permute-start | bytes 344072 | tf_op jit(solution)/shard_map/ppermute | solution.py:200

commit v5 on v4

--- a/solution.py
+++ b/solution.py
@@ -88,32 +88,49 @@
     )(attn_at.reshape(1), expert_at.reshape(1), *given)
 
 
-def load_kernel(*refs):
-    count = len(refs) // 2
-    sources, targets, sems = refs[:count], refs[count : 2 * count], refs[-1]
+def load_kernel(gate_hbm, up_hbm, down_hbm, gate_ref, up_ref, down_ref, rows_ref, sems):
+    width = down_hbm.shape[0]
+    part = width // 2 if width % (2 * LANES) == 0 else width
+    parts = range(0, width, part)
     copies = [
-        pltpu.make_async_copy(source, target, sems.at[i])
-        for i, (source, target) in enumerate(zip(sources, targets))
-    ]
-    for copy in copies:
+        pltpu.make_async_copy(
+            down_hbm.at[pl.ds(at, part), :], rows_ref.at[pl.ds(at, part), :], sems.at[2 + i]
+        )
+        for i, at in enumerate(parts)
+    ]
+    others = [
+        pltpu.make_async_copy(gate_hbm, gate_ref, sems.at[0]),
+        pltpu.make_async_copy(up_hbm, up_ref, sems.at[1]),
+    ]
+    for copy in copies + others:
         copy.start()
-    for copy in copies:
-        copy.wait()
-
-
-def load(*arrays):
+    for copy, at in zip(copies, parts):
+        copy.wait()
+        tile = 256 if part % 256 == 0 else LANES
+        for row in range(at, at + part, tile):
+            down_ref[:, pl.ds(row, tile)] = rows_ref[pl.ds(row, tile), :].T
+    for copy in others:
+        copy.wait()
+
+
+def load(gate, up, down):
+    given = (gate, up, down)
     return pl.pallas_call(
         load_kernel,
-        out_shape=tuple(jax.ShapeDtypeStruct(a.shape, a.dtype) for a in arrays),
-        in_specs=[pl.BlockSpec(memory_space=pltpu.HBM)] * len(arrays),
-        out_specs=(VMEM,) * len(arrays),
-        scratch_shapes=[pltpu.SemaphoreType.DMA((len(arrays),))],
-        compiler_params=pltpu.CompilerParams(vmem_limit_bytes=SMALL),
+        out_shape=(
+            jax.ShapeDtypeStruct(gate.shape, gate.dtype),
+            jax.ShapeDtypeStruct(up.shape, up.dtype),
+            jax.ShapeDtypeStruct(down.shape[::-1], down.dtype),
+        ),
+        in_specs=[pl.BlockSpec(memory_space=pltpu.HBM)] * 3,
+        out_specs=(VMEM,) * 3,
+        scratch_shapes=[pltpu.VMEM(down.shape, down.dtype), pltpu.SemaphoreType.DMA((4,))],
+        compiler_params=pltpu.CompilerParams(vmem_limit_bytes=2 * SMALL),
         cost_estimate=pl.CostEstimate(
-            flops=0, transcendentals=0, bytes_accessed=sum(2 * a.size * a.dtype.itemsize for a in arrays)
+            flops=0, transcendentals=0, bytes_accessed=sum(2 * a.size * a.dtype.itemsize for a in given)
         ),
         name="load",
-    )(*[pltpu.with_memory_space_constraint(a, pltpu.HBM) for a in arrays])
+    )(*[pltpu.with_memory_space_constraint(a, pltpu.HBM) for a in given])
 
 
 def ffn_kernel(experts, blocks, at_ref, *refs):
@@ -140,9 +157,7 @@
     wide = 512
     for start in range(0, width, wide):
         cols = pl.ds(start, min(wide, width - start))
-        y = lax.dot_general(
-            h_ref[...], down_ref[cols, :], (((1,), (1,)), ((), ())), preferred_element_type=jnp.float32
-        )
+        y = jnp.dot(h_ref[...], down_ref[:, cols], preferred_element_type=jnp.float32)
         y = (y * w_ref[:, pl.ds(0, 1)]).astype(jnp.bfloat16)
         keep_ref[:, cols] = y[:half]
         send_ref[:, cols] = y[half:]

time: 59.7 us -> 58.5 us (0.980)
  Pallas kernels: 9.97 us -> 8.81 us
    pallas_call x2, Pallas kernels: 4.65 us -> 3.48 us  [ffn(): pl.pallas_call(functools.partial(ffn_kernel, experts, len(x_blocks)), out...]
    ppermute x14, starting transfers between devices: 12.8 us -> 12 us  [swap(): return lax.ppermute(value, 'expert', [(i, i ^ bit) for i in range(experts)])]
  transfers between devices with their start and end apart: 20 -> 20, of which waited for: 12 -> 12; matrix products, arithmetic and copies ran while one was open for 1% -> 1% of each run, Pallas kernels for 15% -> 13%
where the time goes in v5:
time: 58.5 us; the launch traced here: 58.4 us
  waiting for transfers between devices  30.9 us (53%)
  starting transfers between devices  17.4 us (30%)
  Pallas kernels  8.81 us (15%)
  other arithmetic  1.1 us (2%)
    ppermute x14, waiting for transfers between devices, swap(): return lax.ppermute(value, 'expert', [(i, i ^ bit) for i in range(experts)])  15.1 us
    ppermute x14, starting transfers between devices, swap(): return lax.ppermute(value, 'expert', [(i, i ^ bit) for i in range(experts)])  12 us
    ppermute x4, waiting for transfers between devices, pair(): return lax.ppermute(value, 'attn', [(0, 1), (1, 0)])  11.5 us
    ppermute x2, waiting for transfers between devices, cross(): return lax.ppermute(value, ('expert', 'attn'), order)  4.31 us
    pallas_call x1, Pallas kernels, load(): pl.pallas_call(load_kernel, out_shape=(jax.ShapeDtypeStruct(gate.shape, g...  4.23 us
    pallas_call x2, Pallas kernels, ffn(): pl.pallas_call(functools.partial(ffn_kernel, experts, len(x_blocks)), out...  3.48 us
    ppermute x2, starting transfers between devices, cross(): return lax.ppermute(value, ('expert', 'attn'), order)  3.03 us
    ppermute x4, starting transfers between devices, pair(): return lax.ppermute(value, 'attn', [(0, 1), (1, 0)])  2.44 us
  transfers between devices with their start and end apart: 20, of which 12 were waited for; matrix products, arithmetic and copies ran while one was open for 1% of the time, Pallas kernels for 13%

profile of v5, /device:TPU:0, one launch (start us, length us, event | category | flops | bytes accessed | tf_op | source)
XLA Modules:
  0.0 58.4 jit_solution(4265505608986157923)
XLA Ops:
  0.0 1.1 %prepare.1 = (bf16[32,3712]{1,0:T(8,128)(2,1)S(1)}, bf16[16,3712]{1,0:T(8,128)(2,1)S(1)}) custom-call(s32[1]{0:T(128)} %bitcast.1.at_ref, s32[1]{0:T(128)} %bitcast.expert_ref.at_ref, s32[8]{0:T(128)} %plan_hbm.1, s32[8,32]{1,0:T(8,128)} %bitcast.10, f32[8,32]{1,0:T(8,128)} %bitcast.11, bf16[32,3584]{1,0:T(8,128)(2,1)} %tok_hbm.1), custom_call_target="tpu_custom_call" | custom-call | tf_op jit(solution)/shard_map/prepare/pallas_call | solution.py:71
  1.1 4.1 %collective-permute-start.6 = (bf16[16,3712]{1,0:T(8,128)(2,1)S(1)}, bf16[16,3712]{1,0:T(8,128)(2,1)S(1)}, u32[]{:S(2)}, u32[]{:S(2)}) collective-permute-start(bf16[16,3712]{1,0:T(8,128)(2,1)S(1)} %get-tuple-element.20), channel_id=1, source_target_pairs={{0,8},{2,10},{4,12},{6,14},{8,0},{10,2},{12,4},{14,6},{1,9},{3,11}... | collective-permute-start | bytes 356360 | tf_op jit(solution)/shard_map/ppermute | solution.py:209
  5.2 5.8 %collective-permute-done.6.refs_0_ = bf16[16,3712]{1,0:T(8,128)(2,1)S(1)} collective-permute-done((bf16[16,3712]{1,0:T(8,128)(2,1)S(1)}, bf16[16,3712]{1,0:T(8,128)(2,1)S(1)}, u32[]{:S(2)}, u32[]{:S(2)}) %collective-permute-start.6) | collective-permute-done | bytes 118816 | tf_op jit(solution)/shard_map/ppermute | solution.py:209
  11.0 1.5 %collective-permute-start.7 = (bf16[16,3712]{1,0:T(8,128)(2,1)S(1)}, bf16[16,3712]{1,0:T(8,128)(2,1)S(1)}, u32[]{:S(2)}, u32[]{:S(2)}) collective-permute-start(bf16[16,3712]{1,0:T(8,128)(2,1)S(1)} %collective-permute-done.6.refs_0_), channel_id=1, source_target_pairs={{0,1},{1,0},{2,3},{3,2},{4,5},{5,4},{6,7},{7,6},{8,9},{9,8},{10,11... | collective-permute-start | bytes 356360 | tf_op jit(solution)/shard_map/ppermute | solution.py:215
  12.6 0.7 %collective-permute-start.8 = (bf16[16,3712]{1,0:T(8,128)(2,1)S(1)}, bf16[16,3712]{1,0:T(8,128)(2,1)S(1)}, u32[]{:S(2)}, u32[]{:S(2)}) collective-permute-start(bf16[16,3712]{1,0:T(8,128)(2,1)S(1)} %collective-permute-done.6.refs_0_), channel_id=1, source_target_pairs={{0,4},{2,6},{4,0},{6,2},{8,12},{10,14},{12,8},{14,10},{1,5},{3,7},... | collective-permute-start | bytes 356360 | tf_op jit(solution)/shard_map/ppermute | solution.py:209
  13.2 1.3 %collective-permute-start.9 = (bf16[16,3712]{1,0:T(8,128)(2,1)S(1)}, bf16[16,3712]{1,0:T(8,128)(2,1)S(1)}, u32[]{:S(2)}, u32[]{:S(2)}) collective-permute-start(bf16[16,3712]{1,0:T(8,128)(2,1)S(1)} %collective-permute-done.6.refs_0_), channel_id=1, source_target_pairs={{0,5},{1,4},{2,7},{3,6},{4,1},{5,0},{6,3},{7,2},{8,13},{9,12},{10,... | collective-permute-start | bytes 356360 | tf_op jit(solution)/shard_map/ppermute | solution.py:219
  14.5 1.7 %collective-permute-done.7.refs_1_ = bf16[16,3712]{1,0:T(8,128)(2,1)S(1)} collective-permute-done((bf16[16,3712]{1,0:T(8,128)(2,1)S(1)}, bf16[16,3712]{1,0:T(8,128)(2,1)S(1)}, u32[]{:S(2)}, u32[]{:S(2)}) %collective-permute-start.7) | collective-permute-done | bytes 118816 | tf_op jit(solution)/shard_map/ppermute | solution.py:215
  16.2 1.6 %collective-permute-done.8.refs_2_ = bf16[16,3712]{1,0:T(8,128)(2,1)S(1)} collective-permute-done((bf16[16,3712]{1,0:T(8,128)(2,1)S(1)}, bf16[16,3712]{1,0:T(8,128)(2,1)S(1)}, u32[]{:S(2)}, u32[]{:S(2)}) %collective-permute-start.8) | collective-permute-done | bytes 118816 | tf_op jit(solution)/shard_map/ppermute | solution.py:209
  17.8 2.1 %collective-permute-done.9.refs_3_ = bf16[16,3712]{1,0:T(8,128)(2,1)S(1)} collective-permute-done((bf16[16,3712]{1,0:T(8,128)(2,1)S(1)}, bf16[16,3712]{1,0:T(8,128)(2,1)S(1)}, u32[]{:S(2)}, u32[]{:S(2)}) %collective-permute-start.9) | collective-permute-done | bytes 118816 | tf_op jit(solution)/shard_map/ppermute | solution.py:219
  19.9 0.8 %collective-permute-start = (bf16[32,3712]{1,0:T(8,128)(2,1)S(1)}, bf16[32,3712]{1,0:T(8,128)(2,1)S(1)}, u32[]{:S(2)}, u32[]{:S(2)}) collective-permute-start(bf16[32,3712]{1,0:T(8,128)(2,1)S(1)} %get-tuple-element.14.refs_0_), channel_id=1, source_target_pairs={{0,4},{2,6},{4,0},{6,2},{8,12},{10,14},{12,8},{14,10},{1,5},{3,7},... | collective-permute-start | bytes 712712 | tf_op jit(solution)/shard_map/ppermute | solution.py:209
  20.6 4.2 %load.1 = (bf16[3584,512]{1,0:T(8,128)(2,1)S(1)}, bf16[3584,512]{1,0:T(8,128)(2,1)S(1)}, bf16[512,3584]{1,0:T(8,128)(2,1)S(1)}) custom-call(bf16[3584,512]{1,0:T(8,128)(2,1)} %bitcast.7, bf16[3584,512]{1,0:T(8,128)(2,1)} %bitcast.8, bf16[3584,512]{1,0:T(8,128)(2,1)} %bitcast.9), custom_call_target="tpu_custom_call" | custom-call | bytes 22020096 | tf_op jit(solution)/shard_map/load/pallas_call | solution.py:118
  24.9 1.8 %ffn.3 = (bf16[64,3584]{1,0:T(8,128)(2,1)S(1)}, bf16[64,3584]{1,0:T(8,128)(2,1)S(1)}) custom-call(s32[1]{0:T(128)} %bitcast.expert_ref.at_ref, bf16[16,3712]{1,0:T(8,128)(2,1)S(1)} %collective-permute-done.6.refs_0_, bf16[16,3712]{1,0:T(8,128)(2,1)S(1)} %collective-permute-done.7.refs_1_, bf16[16,3712]{1,0:T(8,128)(2,1)S(1)} %collective-permute-done.8.refs_2_, ...), custom_call_target="tpu_custom_call" | custom-call | flops 1409286144 | bytes 14680064 | tf_op jit(solution)/shard_map/ffn/pallas_call | solution.py:170
  26.7 0.3 collective-permute-start.14
  27.0 0.3 collective-permute-start.1
  27.3 0.8 %collective-permute-done.refs_1_ = bf16[32,3712]{1,0:T(8,128)(2,1)S(1)} collective-permute-done((bf16[32,3712]{1,0:T(8,128)(2,1)S(1)}, bf16[32,3712]{1,0:T(8,128)(2,1)S(1)}, u32[]{:S(2)}, u32[]{:S(2)}) %collective-permute-start) | collective-permute-done | bytes 237600 | tf_op jit(solution)/shard_map/ppermute | solution.py:209
  28.1 0.9 %collective-permute-done.1.refs_2_ = bf16[32,3712]{1,0:T(8,128)(2,1)S(1)} collective-permute-done((bf16[32,3712]{1,0:T(8,128)(2,1)S(1)}, bf16[32,3712]{1,0:T(8,128)(2,1)S(1)}, u32[]{:S(2)}, u32[]{:S(2)}) %collective-permute-start.1) | collective-permute-done | bytes 237600 | tf_op jit(solution)/shard_map/ppermute | solution.py:209
  28.9 0.6 %collective-permute-done.2.refs_3_ = bf16[32,3712]{1,0:T(8,128)(2,1)S(1)} collective-permute-done((bf16[32,3712]{1,0:T(8,128)(2,1)S(1)}, bf16[32,3712]{1,0:T(8,128)(2,1)S(1)}, u32[]{:S(2)}, u32[]{:S(2)}) %collective-permute-start.2) | collective-permute-done | bytes 237600 | tf_op jit(solution)/shard_map/ppermute | solution.py:209
  29.6 1.7 %ffn.2 = (bf16[64,3584]{1,0:T(8,128)(2,1)S(1)}, bf16[64,3584]{1,0:T(8,128)(2,1)S(1)}) custom-call(s32[1]{0:T(128)} %bitcast.expert_ref.at_ref, bf16[32,3712]{1,0:T(8,128)(2,1)S(1)} %get-tuple-element.14.refs_0_, bf16[32,3712]{1,0:T(8,128)(2,1)S(1)} %collective-permute-done.refs_1_, bf16[32,3712]{1,0:T(8,128)(2,1)S(1)} %collective-permute-done.1.refs_2_, ...), custom_call_target="tpu_custom_call" | custom-call | flops 1409286144 | bytes 14680064 | tf_op jit(solution)/shard_map/ffn/pallas_call | solution.py:170
  31.3 0.2 collective-permute-start.3
  31.5 0.1 add_convert_fusion.6
  31.6 1.8 %collective-permute-start.17 = (bf16[16,3584]{1,0:T(8,128)(2,1)S(1)}, bf16[16,3584]{1,0:T(8,128)(2,1)S(1)}, u32[]{:S(2)}, u32[]{:S(2)}) collective-permute-start(bf16[16,3584]{1,0:T(8,128)(2,1)S(1)} %get-tuple-element.24), channel_id=1, source_target_pairs={{0,5},{1,4},{2,7},{3,6},{4,1},{5,0},{6,3},{7,2},{8,13},{9,12},{10,... | collective-permute-start | bytes 344072 | tf_op jit(solution)/shard_map/ppermute | solution.py:219
  33.3 1.0 %collective-permute-start.16 = (bf16[16,3584]{1,0:T(8,128)(2,1)S(1)}, bf16[16,3584]{1,0:T(8,128)(2,1)S(1)}, u32[]{:S(2)}, u32[]{:S(2)}) collective-permute-start(bf16[16,3584]{1,0:T(8,128)(2,1)S(1)} %get-tuple-element.25), channel_id=1, source_target_pairs={{0,4},{2,6},{4,0},{6,2},{8,12},{10,14},{12,8},{14,10},{1,5},{3,7},... | collective-permute-start | bytes 344072 | tf_op jit(solution)/shard_map/ppermute | solution.py:209
  34.4 0.8 %collective-permute-start.15 = (bf16[16,3584]{1,0:T(8,128)(2,1)S(1)}, bf16[16,3584]{1,0:T(8,128)(2,1)S(1)}, u32[]{:S(2)}, u32[]{:S(2)}) collective-permute-start(bf16[16,3584]{1,0:T(8,128)(2,1)S(1)} %get-tuple-element.23), channel_id=1, source_target_pairs={{0,1},{1,0},{2,3},{3,2},{4,5},{5,4},{6,7},{7,6},{8,9},{9,8},{10,11... | collective-permute-start | bytes 344072 | tf_op jit(solution)/shard_map/ppermute | solution.py:215
  35.2 1.1 %collective-permute-start.4 = (bf16[32,3584]{1,0:T(8,128)(2,1)S(1)}, bf16[32,3584]{1,0:T(8,128)(2,1)S(1)}, u32[]{:S(2)}, u32[]{:S(2)}) collective-permute-start(bf16[32,3584]{1,0:T(8,128)(2,1)S(1)} %add_convert_fusion.1), channel_id=1, source_target_pairs={{0,4},{2,6},{4,0},{6,2},{8,12},{10,14},{12,8},{14,10},{1,5},{3,7},... | collective-permute-start | bytes 688136 | tf_op jit(solution)/shard_map/ppermute | solution.py:209
  36.3 2.3 %collective-permute-done.17 = bf16[16,3584]{1,0:T(8,128)(2,1)S(1)} collective-permute-done((bf16[16,3584]{1,0:T(8,128)(2,1)S(1)}, bf16[16,3584]{1,0:T(8,128)(2,1)S(1)}, u32[]{:S(2)}, u32[]{:S(2)}) %collective-permute-start.17) | collective-permute-done | bytes 114720 | tf_op jit(solution)/shard_map/ppermute | solution.py:219
  38.6 2.3 %collective-permute-done.16 = bf16[16,3584]{1,0:T(8,128)(2,1)S(1)} collective-permute-done((bf16[16,3584]{1,0:T(8,128)(2,1)S(1)}, bf16[16,3584]{1,0:T(8,128)(2,1)S(1)}, u32[]{:S(2)}, u32[]{:S(2)}) %collective-permute-start.16) | collective-permute-done | bytes 114720 | tf_op jit(solution)/shard_map/ppermute | solution.py:209
  40.9 3.5 %collective-permute-start.18 = (bf16[16,3584]{1,0:T(8,128)(2,1)S(1)}, bf16[16,3584]{1,0:T(8,128)(2,1)S(1)}, u32[]{:S(2)}, u32[]{:S(2)}) collective-permute-start(bf16[16,3584]{1,0:T(8,128)(2,1)S(1)} %add_convert_fusion.3), channel_id=1, source_target_pairs={{0,8},{2,10},{4,12},{6,14},{8,0},{10,2},{12,4},{14,6},{1,9},{3,11}... | collective-permute-start | bytes 344072 | tf_op jit(solution)/shard_map/ppermute | solution.py:209
  44.3 3.2 %collective-permute-done.4 = bf16[32,3584]{1,0:T(8,128)(2,1)S(1)} collective-permute-done((bf16[32,3584]{1,0:T(8,128)(2,1)S(1)}, bf16[32,3584]{1,0:T(8,128)(2,1)S(1)}, u32[]{:S(2)}, u32[]{:S(2)}) %collective-permute-start.4) | collective-permute-done | bytes 229408 | tf_op jit(solution)/shard_map/ppermute | solution.py:209
  47.5 0.1 add_convert_fusion
  47.7 5.0 %collective-permute-done.5 = bf16[16,3584]{1,0:T(8,128)(2,1)S(1)} collective-permute-done((bf16[16,3584]{1,0:T(8,128)(2,1)S(1)}, bf16[16,3584]{1,0:T(8,128)(2,1)S(1)}, u32[]{:S(2)}, u32[]{:S(2)}) %collective-permute-start.5) | collective-permute-done | bytes 114720 | tf_op jit(solution)/shard_map/ppermute | solution.py:215
  52.9 4.8 %collective-permute-done.19 = bf16[16,3584]{1,0:T(8,128)(2,1)S(1)} collective-permute-done((bf16[16,3584]{1,0:T(8,128)(2,1)S(1)}, bf16[16,3584]{1,0:T(8,128)(2,1)S(1)}, u32[]{:S(2)}, u32[]{:S(2)}) %collective-permute-start.19) | collective-permute-done | bytes 114720 | tf_op jit(solution)/shard_map/ppermute | solution.py:215
  57.6 0.7 %maximum_select_fusion = bf16[32,3584]{1,0:T(8,128)(2,1)} fusion(bf16[16,3584]{1,0:T(8,128)(2,1)S(1)} %collective-permute-done.19, bf16[16,3584]{1,0:T(8,128)(2,1)S(1)} %add_convert_fusion.2, pred[]{:T(512)S(6)} %eq.3), kind=kLoop, calls=%fused_computation.2 | loop fusion | flops 1032192 | bytes 458753 | tf_op jit(solution)/shard_map/jit(_where)/select_n | solution.py:246
  (19 shorter events, 0.4 us)
Async XLA Ops:
  1.1 9.9 %collective-permute-start.6 = (bf16[16,3712]{1,0:T(8,128)(2,1)S(1)}, bf16[16,3712]{1,0:T(8,128)(2,1)S(1)}, u32[]{:S(2)}, u32[]{:S(2)}) collective-permute-start(bf16[16,3712]{1,0:T(8,128)(2,1)S(1)} %get-tuple-element.20), channel_id=1, source_target_pairs={{0,8},{2,10},{4,12},{6,14},{8,0},{10,2},{12,4},{14,6},{1,9},{3,11}... | collective-permute-start | bytes 356360 | tf_op jit(solution)/shard_map/ppermute | solution.py:209
  11.0 5.2 %collective-permute-start.7 = (bf16[16,3712]{1,0:T(8,128)(2,1)S(1)}, bf16[16,3712]{1,0:T(8,128)(2,1)S(1)}, u32[]{:S(2)}, u32[]{:S(2)}) collective-permute-start(bf16[16,3712]{1,0:T(8,128)(2,1)S(1)} %collective-permute-done.6.refs_0_), channel_id=1, source_target_pairs={{0,1},{1,0},{2,3},{3,2},{4,5},{5,4},{6,7},{7,6},{8,9},{9,8},{10,11... | collective-permute-start | bytes 356360 | tf_op jit(solution)/shard_map/ppermute | solution.py:215
  12.6 5.2 %collective-permute-start.8 = (bf16[16,3712]{1,0:T(8,128)(2,1)S(1)}, bf16[16,3712]{1,0:T(8,128)(2,1)S(1)}, u32[]{:S(2)}, u32[]{:S(2)}) collective-permute-start(bf16[16,3712]{1,0:T(8,128)(2,1)S(1)} %collective-permute-done.6.refs_0_), channel_id=1, source_target_pairs={{0,4},{2,6},{4,0},{6,2},{8,12},{10,14},{12,8},{14,10},{1,5},{3,7},... | collective-permute-start | bytes 356360 | tf_op jit(solution)/shard_map/ppermute | solution.py:209
  13.2 6.6 %collective-permute-start.9 = (bf16[16,3712]{1,0:T(8,128)(2,1)S(1)}, bf16[16,3712]{1,0:T(8,128)(2,1)S(1)}, u32[]{:S(2)}, u32[]{:S(2)}) collective-permute-start(bf16[16,3712]{1,0:T(8,128)(2,1)S(1)} %collective-permute-done.6.refs_0_), channel_id=1, source_target_pairs={{0,5},{1,4},{2,7},{3,6},{4,1},{5,0},{6,3},{7,2},{8,13},{9,12},{10,... | collective-permute-start | bytes 356360 | tf_op jit(solution)/shard_map/ppermute | solution.py:219
  14.5 10.4 %collective-permute-start.10 = (bf16[16,3712]{1,0:T(8,128)(2,1)S(1)}, bf16[16,3712]{1,0:T(8,128)(2,1)S(1)}, u32[]{:S(2)}, u32[]{:S(2)}) collective-permute-start(bf16[16,3712]{1,0:T(8,128)(2,1)S(1)} %collective-permute-done.6.refs_0_), channel_id=1, source_target_pairs={{0,2},{2,0},{4,6},{6,4},{8,10},{10,8},{12,14},{14,12},{1,3},{3,1},... | collective-permute-start | bytes 356360 | tf_op jit(solution)/shard_map/ppermute | solution.py:209
  16.2 8.7 %collective-permute-start.11 = (bf16[16,3712]{1,0:T(8,128)(2,1)S(1)}, bf16[16,3712]{1,0:T(8,128)(2,1)S(1)}, u32[]{:S(2)}, u32[]{:S(2)}) collective-permute-start(bf16[16,3712]{1,0:T(8,128)(2,1)S(1)} %collective-permute-done.7.refs_1_), channel_id=1, source_target_pairs={{0,2},{2,0},{4,6},{6,4},{8,10},{10,8},{12,14},{14,12},{1,3},{3,1},... | collective-permute-start | bytes 356360 | tf_op jit(solution)/shard_map/ppermute | solution.py:209
  17.8 7.1 %collective-permute-start.12 = (bf16[16,3712]{1,0:T(8,128)(2,1)S(1)}, bf16[16,3712]{1,0:T(8,128)(2,1)S(1)}, u32[]{:S(2)}, u32[]{:S(2)}) collective-permute-start(bf16[16,3712]{1,0:T(8,128)(2,1)S(1)} %collective-permute-done.8.refs_2_), channel_id=1, source_target_pairs={{0,2},{2,0},{4,6},{6,4},{8,10},{10,8},{12,14},{14,12},{1,3},{3,1},... | collective-permute-start | bytes 356360 | tf_op jit(solution)/shard_map/ppermute | solution.py:209
  19.9 5.0 %collective-permute-start.13 = (bf16[16,3712]{1,0:T(8,128)(2,1)S(1)}, bf16[16,3712]{1,0:T(8,128)(2,1)S(1)}, u32[]{:S(2)}, u32[]{:S(2)}) collective-permute-start(bf16[16,3712]{1,0:T(8,128)(2,1)S(1)} %collective-permute-done.9.refs_3_), channel_id=1, source_target_pairs={{0,2},{2,0},{4,6},{6,4},{8,10},{10,8},{12,14},{14,12},{1,3},{3,1},... | collective-permute-start | bytes 356360 | tf_op jit(solution)/shard_map/ppermute | solution.py:209
  19.9 8.2 %collective-permute-start = (bf16[32,3712]{1,0:T(8,128)(2,1)S(1)}, bf16[32,3712]{1,0:T(8,128)(2,1)S(1)}, u32[]{:S(2)}, u32[]{:S(2)}) collective-permute-start(bf16[32,3712]{1,0:T(8,128)(2,1)S(1)} %get-tuple-element.14.refs_0_), channel_id=1, source_target_pairs={{0,4},{2,6},{4,0},{6,2},{8,12},{10,14},{12,8},{14,10},{1,5},{3,7},... | collective-permute-start | bytes 712712 | tf_op jit(solution)/shard_map/ppermute | solution.py:209
  26.7 4.8 %collective-permute-start.14 = (bf16[64,3584]{1,0:T(8,128)(2,1)S(1)}, bf16[64,3584]{1,0:T(8,128)(2,1)S(1)}, u32[]{:S(2)}, u32[]{:S(2)}) collective-permute-start(bf16[64,3584]{1,0:T(8,128)(2,1)S(1)} %get-tuple-element.22), channel_id=1, source_target_pairs={{0,2},{2,0},{4,6},{6,4},{8,10},{10,8},{12,14},{14,12},{1,3},{3,1},... | collective-permute-start | bytes 1376264 | tf_op jit(solution)/shard_map/ppermute | solution.py:209
  27.0 1.9 %collective-permute-start.1 = (bf16[32,3712]{1,0:T(8,128)(2,1)S(1)}, bf16[32,3712]{1,0:T(8,128)(2,1)S(1)}, u32[]{:S(2)}, u32[]{:S(2)}) collective-permute-start(bf16[32,3712]{1,0:T(8,128)(2,1)S(1)} %get-tuple-element.14.refs_0_), channel_id=1, source_target_pairs={{0,2},{2,0},{4,6},{6,4},{8,10},{10,8},{12,14},{14,12},{1,3},{3,1},... | collective-permute-start | bytes 712712 | tf_op jit(solution)/shard_map/ppermute | solution.py:209
  28.1 1.5 %collective-permute-start.2 = (bf16[32,3712]{1,0:T(8,128)(2,1)S(1)}, bf16[32,3712]{1,0:T(8,128)(2,1)S(1)}, u32[]{:S(2)}, u32[]{:S(2)}) collective-permute-start(bf16[32,3712]{1,0:T(8,128)(2,1)S(1)} %collective-permute-done.refs_1_), channel_id=1, source_target_pairs={{0,2},{2,0},{4,6},{6,4},{8,10},{10,8},{12,14},{14,12},{1,3},{3,1},... | collective-permute-start | bytes 712712 | tf_op jit(solution)/shard_map/ppermute | solution.py:209
  31.3 3.9 %collective-permute-start.3 = (bf16[64,3584]{1,0:T(8,128)(2,1)S(1)}, bf16[64,3584]{1,0:T(8,128)(2,1)S(1)}, u32[]{:S(2)}, u32[]{:S(2)}) collective-permute-start(bf16[64,3584]{1,0:T(8,128)(2,1)S(1)} %get-tuple-element.19), channel_id=1, source_target_pairs={{0,2},{2,0},{4,6},{6,4},{8,10},{10,8},{12,14},{14,12},{1,3},{3,1},... | collective-permute-start | bytes 1376264 | tf_op jit(solution)/shard_map/ppermute | solution.py:209
  31.6 7.0 %collective-permute-start.17 = (bf16[16,3584]{1,0:T(8,128)(2,1)S(1)}, bf16[16,3584]{1,0:T(8,128)(2,1)S(1)}, u32[]{:S(2)}, u32[]{:S(2)}) collective-permute-start(bf16[16,3584]{1,0:T(8,128)(2,1)S(1)} %get-tuple-element.24), channel_id=1, source_target_pairs={{0,5},{1,4},{2,7},{3,6},{4,1},{5,0},{6,3},{7,2},{8,13},{9,12},{10,... | collective-permute-start | bytes 344072 | tf_op jit(solution)/shard_map/ppermute | solution.py:219
  33.3 7.5 %collective-permute-start.16 = (bf16[16,3584]{1,0:T(8,128)(2,1)S(1)}, bf16[16,3584]{1,0:T(8,128)(2,1)S(1)}, u32[]{:S(2)}, u32[]{:S(2)}) collective-permute-start(bf16[16,3584]{1,0:T(8,128)(2,1)S(1)} %get-tuple-element.25), channel_id=1, source_target_pairs={{0,4},{2,6},{4,0},{6,2},{8,12},{10,14},{12,8},{14,10},{1,5},{3,7},... | collective-permute-start | bytes 344072 | tf_op jit(solution)/shard_map/ppermute | solution.py:209
  34.4 6.5 %collective-permute-start.15 = (bf16[16,3584]{1,0:T(8,128)(2,1)S(1)}, bf16[16,3584]{1,0:T(8,128)(2,1)S(1)}, u32[]{:S(2)}, u32[]{:S(2)}) collective-permute-start(bf16[16,3584]{1,0:T(8,128)(2,1)S(1)} %get-tuple-element.23), channel_id=1, source_target_pairs={{0,1},{1,0},{2,3},{3,2},{4,5},{5,4},{6,7},{7,6},{8,9},{9,8},{10,11... | collective-permute-start | bytes 344072 | tf_op jit(solution)/shard_map/ppermute | solution.py:215
  35.2 12.3 %collective-permute-start.4 = (bf16[32,3584]{1,0:T(8,128)(2,1)S(1)}, bf16[32,3584]{1,0:T(8,128)(2,1)S(1)}, u32[]{:S(2)}, u32[]{:S(2)}) collective-permute-start(bf16[32,3584]{1,0:T(8,128)(2,1)S(1)} %add_convert_fusion.1), channel_id=1, source_target_pairs={{0,4},{2,6},{4,0},{6,2},{8,12},{10,14},{12,8},{14,10},{1,5},{3,7},... | collective-permute-start | bytes 688136 | tf_op jit(solution)/shard_map/ppermute | solution.py:209
  40.9 6.8 %collective-permute-start.18 = (bf16[16,3584]{1,0:T(8,128)(2,1)S(1)}, bf16[16,3584]{1,0:T(8,128)(2,1)S(1)}, u32[]{:S(2)}, u32[]{:S(2)}) collective-permute-start(bf16[16,3584]{1,0:T(8,128)(2,1)S(1)} %add_convert_fusion.3), channel_id=1, source_target_pairs={{0,8},{2,10},{4,12},{6,14},{8,0},{10,2},{12,4},{14,6},{1,9},{3,11}... | collective-permute-start | bytes 344072 | tf_op jit(solution)/shard_map/ppermute | solution.py:209
  47.6 5.1 %collective-permute-start.5 = (bf16[16,3584]{1,0:T(8,128)(2,1)S(1)}, bf16[16,3584]{1,0:T(8,128)(2,1)S(1)}, u32[]{:S(2)}, u32[]{:S(2)}) collective-permute-start(bf16[16,3584]{1,0:T(8,128)(2,1)S(1)} %slice.59), channel_id=1, source_target_pairs={{0,1},{1,0},{2,3},{3,2},{4,5},{5,4},{6,7},{7,6},{8,9},{9,8},{10,11... | collective-permute-start | bytes 344072 | tf_op jit(solution)/shard_map/ppermute | solution.py:215
  52.8 4.9 %collective-permute-start.19 = (bf16[16,3584]{1,0:T(8,128)(2,1)S(1)}, bf16[16,3584]{1,0:T(8,128)(2,1)S(1)}, u32[]{:S(2)}, u32[]{:S(2)}) collective-permute-start(bf16[16,3584]{1,0:T(8,128)(2,1)S(1)} %add_convert_fusion.2), channel_id=1, source_target_pairs={{0,1},{1,0},{2,3},{3,2},{4,5},{5,4},{6,7},{7,6},{8,9},{9,8},{10,11... | collective-permute-start | bytes 344072 | tf_op jit(solution)/shard_map/ppermute | solution.py:215

commit v6 on v5

--- a/solution.py
+++ b/solution.py
@@ -227,27 +227,25 @@
     own_core = core(own)
     weights = load(gate_proj[0], up_proj[0], down_proj[0])
     near_core = core(near)
-    keep, send = run(own, near, own_core, near_core)
+    far_core = core(far)
+    keep, send = run(own, near, far, own_core, near_core, far_core)
     got = core(send)
     near_sum = swap(add(keep[count:], got[count:]), 2)
-    both = add(keep[:count], got[:count], near_sum)
-
-    blocks = (far, pair(far), swap(far, 2), cross(far, 2))
+    both = add(keep[:count], got[:count], near_sum[:count])
+
+    blocks = (pair(far), swap(far, 2), cross(far, 2))
     far_keep, far_send = run(*blocks, *[core(b) for b in blocks])
     far_got = core(far_send)
-    parts = [add(far_keep[i : i + half], far_got[i : i + half]) for i in range(0, 2 * count, half)]
-    cross_sum = cross(parts[3], 2)
-    far_other = pair(parts[1])
-    relay_sum = swap(parts[2], 2)
-    far_sum = swap(add(parts[0], far_other, relay_sum, cross_sum), 4)
+    parts = [add(far_keep[i : i + half], far_got[i : i + half]) for i in range(0, 3 * half, half)]
+    far_other = pair(parts[2])
+    cross_sum = cross(parts[0], 2)
+    far_sum = swap(add(parts[1], far_other, near_sum[count:], cross_sum), 6)
     near_other = pair(both[half:])
     final = add(both[:half], near_other, far_sum)
     other = pair(final)
-    return jnp.where(
-        attn_at == 0,
-        jnp.concatenate([final, other], axis=0),
-        jnp.concatenate([other, final], axis=0),
-    )
+    result = jnp.zeros((count, final.shape[1]), final.dtype)
+    result = lax.dynamic_update_slice(result, final, (attn_at * half, 0))
+    return lax.dynamic_update_slice(result, other, ((1 - attn_at) * half, 0))
 
 
 def body_any(tokens, gates, slots, plan, gate_proj, up_proj, down_proj):

time: 58.5 us -> 59.4 us (1.015)
  starting transfers between devices: 17.4 us -> 20.7 us
  waiting for transfers between devices: 30.9 us -> 28 us
  other arithmetic: 1.1 us -> 0.36 us
  local copies, waits for them, and re-layouts: 0.01 us -> 0.69 us
    ppermute x4, waiting for transfers between devices: 11.5 us -> 5.73 us  [pair(): return lax.ppermute(value, 'attn', [(0, 1), (1, 0)])]
    ppermute x14 -> x13, waiting for transfers between devices: 15.1 us -> 19.4 us  [swap(): return lax.ppermute(value, 'expert', [(i, i ^ bit) for i in range(experts)])]
    ppermute x4, starting transfers between devices: 2.44 us -> 5.35 us  [pair(): return lax.ppermute(value, 'attn', [(0, 1), (1, 0)])]
    ppermute x14 -> x13, starting transfers between devices: 12 us -> 14.1 us  [swap(): return lax.ppermute(value, 'expert', [(i, i ^ bit) for i in range(experts)])]
    ppermute x2, starting transfers between devices: 3.03 us -> 1.32 us  [cross(): return lax.ppermute(value, ('expert', 'attn'), order)]
    ppermute x2, waiting for transfers between devices: 4.31 us -> 2.86 us  [cross(): return lax.ppermute(value, ('expert', 'attn'), order)]
    select_n x1 -> x0, other arithmetic: 0.73 us -> none  [line(): jnp.where(attn_at == 0, jnp.concatenate([final, other], axis=0), jnp.conc...]
    dynamic_update_slice x0 -> x1, local copies, waits for them, and re-layouts: none -> 0.65 us  [line(): return lax.dynamic_update_slice(result, other, ((1 - attn_at) * half, 0))]
  transfers between devices with their start and end apart: 20 -> 19, of which waited for: 12 -> 9; matrix products, arithmetic and copies ran while one was open for 1% -> 1% of each run, Pallas kernels for 13% -> 10%
where the time goes in v6:
time: 59.4 us; the launch traced here: 59.3 us
  waiting for transfers between devices  28 us (47%)
  starting transfers between devices  20.7 us (35%)
  Pallas kernels  9.37 us (16%)
  local copies, waits for them, and re-layouts  0.69 us (1%)
    ppermute x13, waiting for transfers between devices, swap(): return lax.ppermute(value, 'expert', [(i, i ^ bit) for i in range(experts)])  19.4 us
    ppermute x13, starting transfers between devices, swap(): return lax.ppermute(value, 'expert', [(i, i ^ bit) for i in range(experts)])  14.1 us
    ppermute x4, waiting for transfers between devices, pair(): return lax.ppermute(value, 'attn', [(0, 1), (1, 0)])  5.73 us
    ppermute x4, starting transfers between devices, pair(): return lax.ppermute(value, 'attn', [(0, 1), (1, 0)])  5.35 us
    pallas_call x1, Pallas kernels, load(): pl.pallas_call(load_kernel, out_shape=(jax.ShapeDtypeStruct(gate.shape, g...  4.23 us
    pallas_call x2, Pallas kernels, ffn(): pl.pallas_call(functools.partial(ffn_kernel, experts, len(x_blocks)), out...  4.05 us
    ppermute x2, waiting for transfers between devices, cross(): return lax.ppermute(value, ('expert', 'attn'), order)  2.86 us
    ppermute x2, starting transfers between devices, cross(): return lax.ppermute(value, ('expert', 'attn'), order)  1.32 us
  transfers between devices with their start and end apart: 19, of which 9 were waited for; matrix products, arithmetic and copies ran while one was open for 1% of the time, Pallas kernels for 10%

profile of v6, /device:TPU:0, one launch (start us, length us, event | category | flops | bytes accessed | tf_op | source)
XLA Modules:
  0.0 59.3 jit_solution(10949725353052382746)
XLA Ops:
  0.0 1.1 %prepare.1 = (bf16[32,3712]{1,0:T(8,128)(2,1)S(1)}, bf16[16,3712]{1,0:T(8,128)(2,1)S(1)}) custom-call(s32[1]{0:T(128)} %bitcast.1.at_ref, s32[1]{0:T(128)} %bitcast.expert_ref.at_ref, s32[8]{0:T(128)} %plan_hbm.1, s32[8,32]{1,0:T(8,128)} %bitcast.10, f32[8,32]{1,0:T(8,128)} %bitcast.11, bf16[32,3584]{1,0:T(8,128)(2,1)} %tok_hbm.1), custom_call_target="tpu_custom_call" | custom-call | tf_op jit(solution)/shard_map/prepare/pallas_call | solution.py:71
  1.1 3.1 %collective-permute-start = (bf16[32,3712]{1,0:T(8,128)(2,1)S(1)}, bf16[32,3712]{1,0:T(8,128)(2,1)S(1)}, u32[]{:S(2)}, u32[]{:S(2)}) collective-permute-start(bf16[32,3712]{1,0:T(8,128)(2,1)S(1)} %get-tuple-element.14.refs_0_), channel_id=1, source_target_pairs={{0,4},{2,6},{4,0},{6,2},{8,12},{10,14},{12,8},{14,10},{1,5},{3,7},... | collective-permute-start | bytes 712712 | tf_op jit(solution)/shard_map/ppermute | solution.py:209
  4.2 2.6 %collective-permute-start.1 = (bf16[16,3712]{1,0:T(8,128)(2,1)S(1)}, bf16[16,3712]{1,0:T(8,128)(2,1)S(1)}, u32[]{:S(2)}, u32[]{:S(2)}) collective-permute-start(bf16[16,3712]{1,0:T(8,128)(2,1)S(1)} %get-tuple-element.15), channel_id=1, source_target_pairs={{0,8},{2,10},{4,12},{6,14},{8,0},{10,2},{12,4},{14,6},{1,9},{3,11}... | collective-permute-start | bytes 356360 | tf_op jit(solution)/shard_map/ppermute | solution.py:209
  6.8 5.7 %collective-permute-done.refs_1_ = bf16[32,3712]{1,0:T(8,128)(2,1)S(1)} collective-permute-done((bf16[32,3712]{1,0:T(8,128)(2,1)S(1)}, bf16[32,3712]{1,0:T(8,128)(2,1)S(1)}, u32[]{:S(2)}, u32[]{:S(2)}) %collective-permute-start) | collective-permute-done | bytes 237600 | tf_op jit(solution)/shard_map/ppermute | solution.py:209
  12.6 0.5 collective-permute-start.4
  13.1 4.2 %load.1 = (bf16[3584,512]{1,0:T(8,128)(2,1)S(1)}, bf16[3584,512]{1,0:T(8,128)(2,1)S(1)}, bf16[512,3584]{1,0:T(8,128)(2,1)S(1)}) custom-call(bf16[3584,512]{1,0:T(8,128)(2,1)} %bitcast.7, bf16[3584,512]{1,0:T(8,128)(2,1)} %bitcast.8, bf16[3584,512]{1,0:T(8,128)(2,1)} %bitcast.9), custom_call_target="tpu_custom_call" | custom-call | bytes 22020096 | tf_op jit(solution)/shard_map/load/pallas_call | solution.py:118
  17.3 2.1 %ffn.2 = (bf16[80,3584]{1,0:T(8,128)(2,1)S(1)}, bf16[80,3584]{1,0:T(8,128)(2,1)S(1)}) custom-call(s32[1]{0:T(128)} %bitcast.expert_ref.at_ref, bf16[32,3712]{1,0:T(8,128)(2,1)S(1)} %get-tuple-element.14.refs_0_, bf16[32,3712]{1,0:T(8,128)(2,1)S(1)} %collective-permute-done.refs_1_, bf16[16,3712]{1,0:T(8,128)(2,1)S(1)} %collective-permute-done.1.refs_2_, ...), custom_call_target="tpu_custom_call" | custom-call | flops 1761607680 | bytes 15597568 | tf_op jit(solution)/shard_map/ffn/pallas_call | solution.py:170
  19.4 0.1 collective-permute-start.5
  19.5 1.7 %collective-permute-start.8 = (bf16[16,3712]{1,0:T(8,128)(2,1)S(1)}, bf16[16,3712]{1,0:T(8,128)(2,1)S(1)}, u32[]{:S(2)}, u32[]{:S(2)}) collective-permute-start(bf16[16,3712]{1,0:T(8,128)(2,1)S(1)} %collective-permute-done.1.refs_2_), channel_id=1, source_target_pairs={{0,1},{1,0},{2,3},{3,2},{4,5},{5,4},{6,7},{7,6},{8,9},{9,8},{10,11... | collective-permute-start | bytes 356360 | tf_op jit(solution)/shard_map/ppermute | solution.py:215
  21.2 2.5 %collective-permute-start.9 = (bf16[16,3712]{1,0:T(8,128)(2,1)S(1)}, bf16[16,3712]{1,0:T(8,128)(2,1)S(1)}, u32[]{:S(2)}, u32[]{:S(2)}) collective-permute-start(bf16[16,3712]{1,0:T(8,128)(2,1)S(1)} %collective-permute-done.1.refs_2_), channel_id=1, source_target_pairs={{0,4},{2,6},{4,0},{6,2},{8,12},{10,14},{12,8},{14,10},{1,5},{3,7},... | collective-permute-start | bytes 356360 | tf_op jit(solution)/shard_map/ppermute | solution.py:209
  23.7 1.4 %collective-permute-done.8.refs_0_ = bf16[16,3712]{1,0:T(8,128)(2,1)S(1)} collective-permute-done((bf16[16,3712]{1,0:T(8,128)(2,1)S(1)}, bf16[16,3712]{1,0:T(8,128)(2,1)S(1)}, u32[]{:S(2)}, u32[]{:S(2)}) %collective-permute-start.8) | collective-permute-done | bytes 118816 | tf_op jit(solution)/shard_map/ppermute | solution.py:215
  25.1 2.7 %collective-permute-done.9.refs_1_ = bf16[16,3712]{1,0:T(8,128)(2,1)S(1)} collective-permute-done((bf16[16,3712]{1,0:T(8,128)(2,1)S(1)}, bf16[16,3712]{1,0:T(8,128)(2,1)S(1)}, u32[]{:S(2)}, u32[]{:S(2)}) %collective-permute-start.9) | collective-permute-done | bytes 118816 | tf_op jit(solution)/shard_map/ppermute | solution.py:209
  27.8 1.6 %collective-permute-done.10.refs_2_ = bf16[16,3712]{1,0:T(8,128)(2,1)S(1)} collective-permute-done((bf16[16,3712]{1,0:T(8,128)(2,1)S(1)}, bf16[16,3712]{1,0:T(8,128)(2,1)S(1)}, u32[]{:S(2)}, u32[]{:S(2)}) %collective-permute-start.10) | collective-permute-done | bytes 118816 | tf_op jit(solution)/shard_map/ppermute | solution.py:219
  29.5 1.3 %collective-permute-done.13.refs_5_ = bf16[16,3712]{1,0:T(8,128)(2,1)S(1)} collective-permute-done((bf16[16,3712]{1,0:T(8,128)(2,1)S(1)}, bf16[16,3712]{1,0:T(8,128)(2,1)S(1)}, u32[]{:S(2)}, u32[]{:S(2)}) %collective-permute-start.13) | collective-permute-done | bytes 118816 | tf_op jit(solution)/shard_map/ppermute | solution.py:209
  30.8 2.0 %ffn.3 = (bf16[48,3584]{1,0:T(8,128)(2,1)S(1)}, bf16[48,3584]{1,0:T(8,128)(2,1)S(1)}) custom-call(s32[1]{0:T(128)} %bitcast.expert_ref.at_ref, bf16[16,3712]{1,0:T(8,128)(2,1)S(1)} %collective-permute-done.8.refs_0_, bf16[16,3712]{1,0:T(8,128)(2,1)S(1)} %collective-permute-done.9.refs_1_, bf16[16,3712]{1,0:T(8,128)(2,1)S(1)} %collective-permute-done.10.refs_2_, ...), custom_call_target="tpu_custom_call" | custom-call | flops 1056964608 | bytes 13762560 | tf_op jit(solution)/shard_map/ffn/pallas_call | solution.py:170
  32.8 0.2 collective-permute-start.14
  33.0 0.1 add_convert_fusion
  33.1 1.8 %collective-permute-start.6 = (bf16[48,3584]{1,0:T(8,128)(2,1)S(1)}, bf16[48,3584]{1,0:T(8,128)(2,1)S(1)}, u32[]{:S(2)}, u32[]{:S(2)}) collective-permute-start(bf16[48,3584]{1,0:T(8,128)(2,1)S(1)} %add_convert_fusion), channel_id=1, source_target_pairs={{0,4},{2,6},{4,0},{6,2},{8,12},{10,14},{12,8},{14,10},{1,5},{3,7},... | collective-permute-start | bytes 1032200 | tf_op jit(solution)/shard_map/ppermute | solution.py:209
  34.9 0.1 add_convert_fusion.5
  34.9 1.6 %collective-permute-start.15 = (bf16[16,3584]{1,0:T(8,128)(2,1)S(1)}, bf16[16,3584]{1,0:T(8,128)(2,1)S(1)}, u32[]{:S(2)}, u32[]{:S(2)}) collective-permute-start(bf16[16,3584]{1,0:T(8,128)(2,1)S(1)} %get-tuple-element.25), channel_id=1, source_target_pairs={{0,1},{1,0},{2,3},{3,2},{4,5},{5,4},{6,7},{7,6},{8,9},{9,8},{10,11... | collective-permute-start | bytes 344072 | tf_op jit(solution)/shard_map/ppermute | solution.py:215
  36.5 1.3 %collective-permute-start.16 = (bf16[16,3584]{1,0:T(8,128)(2,1)S(1)}, bf16[16,3584]{1,0:T(8,128)(2,1)S(1)}, u32[]{:S(2)}, u32[]{:S(2)}) collective-permute-start(bf16[16,3584]{1,0:T(8,128)(2,1)S(1)} %get-tuple-element.26), channel_id=1, source_target_pairs={{0,5},{1,4},{2,7},{3,6},{4,1},{5,0},{6,3},{7,2},{8,13},{9,12},{10,... | collective-permute-start | bytes 344072 | tf_op jit(solution)/shard_map/ppermute | solution.py:219
  37.8 6.3 %collective-permute-done.6 = bf16[48,3584]{1,0:T(8,128)(2,1)S(1)} collective-permute-done((bf16[48,3584]{1,0:T(8,128)(2,1)S(1)}, bf16[48,3584]{1,0:T(8,128)(2,1)S(1)}, u32[]{:S(2)}, u32[]{:S(2)}) %collective-permute-start.6) | collective-permute-done | bytes 344096 | tf_op jit(solution)/shard_map/ppermute | solution.py:209
  44.1 0.1 add_convert_fusion.1
  44.2 1.5 %collective-permute-start.7 = (bf16[16,3584]{1,0:T(8,128)(2,1)S(1)}, bf16[16,3584]{1,0:T(8,128)(2,1)S(1)}, u32[]{:S(2)}, u32[]{:S(2)}) collective-permute-start(bf16[16,3584]{1,0:T(8,128)(2,1)S(1)} %slice.60), channel_id=1, source_target_pairs={{0,1},{1,0},{2,3},{3,2},{4,5},{5,4},{6,7},{7,6},{8,9},{9,8},{10,11... | collective-permute-start | bytes 344072 | tf_op jit(solution)/shard_map/ppermute | solution.py:215
  45.7 1.2 %collective-permute-done.16 = bf16[16,3584]{1,0:T(8,128)(2,1)S(1)} collective-permute-done((bf16[16,3584]{1,0:T(8,128)(2,1)S(1)}, bf16[16,3584]{1,0:T(8,128)(2,1)S(1)}, u32[]{:S(2)}, u32[]{:S(2)}) %collective-permute-start.16) | collective-permute-done | bytes 114720 | tf_op jit(solution)/shard_map/ppermute | solution.py:219
  46.9 0.1 add_convert_fusion.3
  47.0 3.3 %collective-permute-start.17 = (bf16[16,3584]{1,0:T(8,128)(2,1)S(1)}, bf16[16,3584]{1,0:T(8,128)(2,1)S(1)}, u32[]{:S(2)}, u32[]{:S(2)}) collective-permute-start(bf16[16,3584]{1,0:T(8,128)(2,1)S(1)} %add_convert_fusion.3), channel_id=1, source_target_pairs={{0,12},{2,14},{4,8},{6,10},{8,4},{10,6},{12,0},{14,2},{1,13},{3,15... | collective-permute-start | bytes 344072 | tf_op jit(solution)/shard_map/ppermute | solution.py:209
  50.3 3.4 %collective-permute-done.17 = bf16[16,3584]{1,0:T(8,128)(2,1)S(1)} collective-permute-done((bf16[16,3584]{1,0:T(8,128)(2,1)S(1)}, bf16[16,3584]{1,0:T(8,128)(2,1)S(1)}, u32[]{:S(2)}, u32[]{:S(2)}) %collective-permute-start.17) | collective-permute-done | bytes 114720 | tf_op jit(solution)/shard_map/ppermute | solution.py:209
  53.7 0.1 constant_dynamic-update-slice_fusion.1
  53.8 0.5 collective-permute-start.18
  54.3 4.3 %collective-permute-done.18 = bf16[16,3584]{1,0:T(8,128)(2,1)S(1)} collective-permute-done((bf16[16,3584]{1,0:T(8,128)(2,1)S(1)}, bf16[16,3584]{1,0:T(8,128)(2,1)S(1)}, u32[]{:S(2)}, u32[]{:S(2)}) %collective-permute-start.18) | collective-permute-done | bytes 114720 | tf_op jit(solution)/shard_map/ppermute | solution.py:215
  58.6 0.7 %constant_dynamic-update-slice_fusion = bf16[32,3584]{1,0:T(8,128)(2,1)} fusion(bf16[32,3584]{1,0:T(8,128)(2,1)} %copy-done, bf16[16,3584]{1,0:T(8,128)(2,1)S(1)} %collective-permute-done.18, s32[]{:T(128)S(6)} %select_n.7), kind=kLoop, calls=%fused_computation.7 | loop fusion | bytes 229380 | tf_op jit(solution)/shard_map/dynamic_update_slice | solution.py:248
  (20 shorter events, 0.1 us)
Async XLA Ops:
  1.1 11.4 %collective-permute-start = (bf16[32,3712]{1,0:T(8,128)(2,1)S(1)}, bf16[32,3712]{1,0:T(8,128)(2,1)S(1)}, u32[]{:S(2)}, u32[]{:S(2)}) collective-permute-start(bf16[32,3712]{1,0:T(8,128)(2,1)S(1)} %get-tuple-element.14.refs_0_), channel_id=1, source_target_pairs={{0,4},{2,6},{4,0},{6,2},{8,12},{10,14},{12,8},{14,10},{1,5},{3,7},... | collective-permute-start | bytes 712712 | tf_op jit(solution)/shard_map/ppermute | solution.py:209
  4.2 8.3 %collective-permute-start.1 = (bf16[16,3712]{1,0:T(8,128)(2,1)S(1)}, bf16[16,3712]{1,0:T(8,128)(2,1)S(1)}, u32[]{:S(2)}, u32[]{:S(2)}) collective-permute-start(bf16[16,3712]{1,0:T(8,128)(2,1)S(1)} %get-tuple-element.15), channel_id=1, source_target_pairs={{0,8},{2,10},{4,12},{6,14},{8,0},{10,2},{12,4},{14,6},{1,9},{3,11}... | collective-permute-start | bytes 356360 | tf_op jit(solution)/shard_map/ppermute | solution.py:209
  6.8 10.5 %collective-permute-start.2 = (bf16[32,3712]{1,0:T(8,128)(2,1)S(1)}, bf16[32,3712]{1,0:T(8,128)(2,1)S(1)}, u32[]{:S(2)}, u32[]{:S(2)}) collective-permute-start(bf16[32,3712]{1,0:T(8,128)(2,1)S(1)} %get-tuple-element.14.refs_0_), channel_id=1, source_target_pairs={{0,2},{2,0},{4,6},{6,4},{8,10},{10,8},{12,14},{14,12},{1,3},{3,1},... | collective-permute-start | bytes 712712 | tf_op jit(solution)/shard_map/ppermute | solution.py:209
  12.5 4.8 %collective-permute-start.3 = (bf16[32,3712]{1,0:T(8,128)(2,1)S(1)}, bf16[32,3712]{1,0:T(8,128)(2,1)S(1)}, u32[]{:S(2)}, u32[]{:S(2)}) collective-permute-start(bf16[32,3712]{1,0:T(8,128)(2,1)S(1)} %collective-permute-done.refs_1_), channel_id=1, source_target_pairs={{0,2},{2,0},{4,6},{6,4},{8,10},{10,8},{12,14},{14,12},{1,3},{3,1},... | collective-permute-start | bytes 712712 | tf_op jit(solution)/shard_map/ppermute | solution.py:209
  12.6 4.8 %collective-permute-start.4 = (bf16[16,3712]{1,0:T(8,128)(2,1)S(1)}, bf16[16,3712]{1,0:T(8,128)(2,1)S(1)}, u32[]{:S(2)}, u32[]{:S(2)}) collective-permute-start(bf16[16,3712]{1,0:T(8,128)(2,1)S(1)} %collective-permute-done.1.refs_2_), channel_id=1, source_target_pairs={{0,2},{2,0},{4,6},{6,4},{8,10},{10,8},{12,14},{14,12},{1,3},{3,1},... | collective-permute-start | bytes 356360 | tf_op jit(solution)/shard_map/ppermute | solution.py:209
  19.4 13.6 %collective-permute-start.5 = (bf16[80,3584]{1,0:T(8,128)(2,1)S(1)}, bf16[80,3584]{1,0:T(8,128)(2,1)S(1)}, u32[]{:S(2)}, u32[]{:S(2)}) collective-permute-start(bf16[80,3584]{1,0:T(8,128)(2,1)S(1)} %get-tuple-element.20), channel_id=1, source_target_pairs={{0,2},{2,0},{4,6},{6,4},{8,10},{10,8},{12,14},{14,12},{1,3},{3,1},... | collective-permute-start | bytes 1720328 | tf_op jit(solution)/shard_map/ppermute | solution.py:209
  19.5 5.6 %collective-permute-start.8 = (bf16[16,3712]{1,0:T(8,128)(2,1)S(1)}, bf16[16,3712]{1,0:T(8,128)(2,1)S(1)}, u32[]{:S(2)}, u32[]{:S(2)}) collective-permute-start(bf16[16,3712]{1,0:T(8,128)(2,1)S(1)} %collective-permute-done.1.refs_2_), channel_id=1, source_target_pairs={{0,1},{1,0},{2,3},{3,2},{4,5},{5,4},{6,7},{7,6},{8,9},{9,8},{10,11... | collective-permute-start | bytes 356360 | tf_op jit(solution)/shard_map/ppermute | solution.py:215
  21.2 6.6 %collective-permute-start.9 = (bf16[16,3712]{1,0:T(8,128)(2,1)S(1)}, bf16[16,3712]{1,0:T(8,128)(2,1)S(1)}, u32[]{:S(2)}, u32[]{:S(2)}) collective-permute-start(bf16[16,3712]{1,0:T(8,128)(2,1)S(1)} %collective-permute-done.1.refs_2_), channel_id=1, source_target_pairs={{0,4},{2,6},{4,0},{6,2},{8,12},{10,14},{12,8},{14,10},{1,5},{3,7},... | collective-permute-start | bytes 356360 | tf_op jit(solution)/shard_map/ppermute | solution.py:209
  23.7 5.7 %collective-permute-start.10 = (bf16[16,3712]{1,0:T(8,128)(2,1)S(1)}, bf16[16,3712]{1,0:T(8,128)(2,1)S(1)}, u32[]{:S(2)}, u32[]{:S(2)}) collective-permute-start(bf16[16,3712]{1,0:T(8,128)(2,1)S(1)} %collective-permute-done.1.refs_2_), channel_id=1, source_target_pairs={{0,5},{1,4},{2,7},{3,6},{4,1},{5,0},{6,3},{7,2},{8,13},{9,12},{10,... | collective-permute-start | bytes 356360 | tf_op jit(solution)/shard_map/ppermute | solution.py:219
  25.1 4.3 %collective-permute-start.11 = (bf16[16,3712]{1,0:T(8,128)(2,1)S(1)}, bf16[16,3712]{1,0:T(8,128)(2,1)S(1)}, u32[]{:S(2)}, u32[]{:S(2)}) collective-permute-start(bf16[16,3712]{1,0:T(8,128)(2,1)S(1)} %collective-permute-done.8.refs_0_), channel_id=1, source_target_pairs={{0,2},{2,0},{4,6},{6,4},{8,10},{10,8},{12,14},{14,12},{1,3},{3,1},... | collective-permute-start | bytes 356360 | tf_op jit(solution)/shard_map/ppermute | solution.py:209
  27.8 1.7 %collective-permute-start.12 = (bf16[16,3712]{1,0:T(8,128)(2,1)S(1)}, bf16[16,3712]{1,0:T(8,128)(2,1)S(1)}, u32[]{:S(2)}, u32[]{:S(2)}) collective-permute-start(bf16[16,3712]{1,0:T(8,128)(2,1)S(1)} %collective-permute-done.9.refs_1_), channel_id=1, source_target_pairs={{0,2},{2,0},{4,6},{6,4},{8,10},{10,8},{12,14},{14,12},{1,3},{3,1},... | collective-permute-start | bytes 356360 | tf_op jit(solution)/shard_map/ppermute | solution.py:209
  29.5 1.3 %collective-permute-start.13 = (bf16[16,3712]{1,0:T(8,128)(2,1)S(1)}, bf16[16,3712]{1,0:T(8,128)(2,1)S(1)}, u32[]{:S(2)}, u32[]{:S(2)}) collective-permute-start(bf16[16,3712]{1,0:T(8,128)(2,1)S(1)} %collective-permute-done.10.refs_2_), channel_id=1, source_target_pairs={{0,2},{2,0},{4,6},{6,4},{8,10},{10,8},{12,14},{14,12},{1,3},{3,1},... | collective-permute-start | bytes 356360 | tf_op jit(solution)/shard_map/ppermute | solution.py:209
  32.8 2.1 %collective-permute-start.14 = (bf16[48,3584]{1,0:T(8,128)(2,1)S(1)}, bf16[48,3584]{1,0:T(8,128)(2,1)S(1)}, u32[]{:S(2)}, u32[]{:S(2)}) collective-permute-start(bf16[48,3584]{1,0:T(8,128)(2,1)S(1)} %get-tuple-element.22), channel_id=1, source_target_pairs={{0,2},{2,0},{4,6},{6,4},{8,10},{10,8},{12,14},{14,12},{1,3},{3,1},... | collective-permute-start | bytes 1032200 | tf_op jit(solution)/shard_map/ppermute | solution.py:209
  33.1 11.0 %collective-permute-start.6 = (bf16[48,3584]{1,0:T(8,128)(2,1)S(1)}, bf16[48,3584]{1,0:T(8,128)(2,1)S(1)}, u32[]{:S(2)}, u32[]{:S(2)}) collective-permute-start(bf16[48,3584]{1,0:T(8,128)(2,1)S(1)} %add_convert_fusion), channel_id=1, source_target_pairs={{0,4},{2,6},{4,0},{6,2},{8,12},{10,14},{12,8},{14,10},{1,5},{3,7},... | collective-permute-start | bytes 1032200 | tf_op jit(solution)/shard_map/ppermute | solution.py:209
  34.9 10.8 %collective-permute-start.15 = (bf16[16,3584]{1,0:T(8,128)(2,1)S(1)}, bf16[16,3584]{1,0:T(8,128)(2,1)S(1)}, u32[]{:S(2)}, u32[]{:S(2)}) collective-permute-start(bf16[16,3584]{1,0:T(8,128)(2,1)S(1)} %get-tuple-element.25), channel_id=1, source_target_pairs={{0,1},{1,0},{2,3},{3,2},{4,5},{5,4},{6,7},{7,6},{8,9},{9,8},{10,11... | collective-permute-start | bytes 344072 | tf_op jit(solution)/shard_map/ppermute | solution.py:215
  36.5 10.4 %collective-permute-start.16 = (bf16[16,3584]{1,0:T(8,128)(2,1)S(1)}, bf16[16,3584]{1,0:T(8,128)(2,1)S(1)}, u32[]{:S(2)}, u32[]{:S(2)}) collective-permute-start(bf16[16,3584]{1,0:T(8,128)(2,1)S(1)} %get-tuple-element.26), channel_id=1, source_target_pairs={{0,5},{1,4},{2,7},{3,6},{4,1},{5,0},{6,3},{7,2},{8,13},{9,12},{10,... | collective-permute-start | bytes 344072 | tf_op jit(solution)/shard_map/ppermute | solution.py:219
  44.2 6.1 %collective-permute-start.7 = (bf16[16,3584]{1,0:T(8,128)(2,1)S(1)}, bf16[16,3584]{1,0:T(8,128)(2,1)S(1)}, u32[]{:S(2)}, u32[]{:S(2)}) collective-permute-start(bf16[16,3584]{1,0:T(8,128)(2,1)S(1)} %slice.60), channel_id=1, source_target_pairs={{0,1},{1,0},{2,3},{3,2},{4,5},{5,4},{6,7},{7,6},{8,9},{9,8},{10,11... | collective-permute-start | bytes 344072 | tf_op jit(solution)/shard_map/ppermute | solution.py:215
  47.0 6.7 %collective-permute-start.17 = (bf16[16,3584]{1,0:T(8,128)(2,1)S(1)}, bf16[16,3584]{1,0:T(8,128)(2,1)S(1)}, u32[]{:S(2)}, u32[]{:S(2)}) collective-permute-start(bf16[16,3584]{1,0:T(8,128)(2,1)S(1)} %add_convert_fusion.3), channel_id=1, source_target_pairs={{0,12},{2,14},{4,8},{6,10},{8,4},{10,6},{12,0},{14,2},{1,13},{3,15... | collective-permute-start | bytes 344072 | tf_op jit(solution)/shard_map/ppermute | solution.py:209
  53.7 4.9 %copy-start = (bf16[32,3584]{1,0:T(8,128)(2,1)}, bf16[32,3584]{1,0:T(8,128)(2,1)S(1)}, u32[]{:S(2)}) copy-start(bf16[32,3584]{1,0:T(8,128)(2,1)S(1)} %get-tuple-element.23) | copy-start | bytes 688132
  53.8 4.9 %collective-permute-start.18 = (bf16[16,3584]{1,0:T(8,128)(2,1)S(1)}, bf16[16,3584]{1,0:T(8,128)(2,1)S(1)}, u32[]{:S(2)}, u32[]{:S(2)}) collective-permute-start(bf16[16,3584]{1,0:T(8,128)(2,1)S(1)} %get-tuple-element.24), channel_id=1, source_target_pairs={{0,1},{1,0},{2,3},{3,2},{4,5},{5,4},{6,7},{7,6},{8,9},{9,8},{10,11... | collective-permute-start | bytes 344072 | tf_op jit(solution)/shard_map/ppermute | solution.py:215

commit v7 on v6

--- a/solution.py
+++ b/solution.py
@@ -143,6 +143,10 @@
         x_ref[pl.ds(row, size), :] = ref[:, pl.ds(0, width)]
         w_ref[pl.ds(row, size), :] = ref[:, pl.ds(width, LANES)].astype(jnp.float32)
         row += size
+    spare = x_ref.shape[0] - row
+    if spare:
+        x_ref[pl.ds(row, spare), :] = jnp.zeros((spare, width), x_ref.dtype)
+        w_ref[pl.ds(row, spare), :] = jnp.zeros((spare, LANES), w_ref.dtype)
     lane = lax.broadcasted_iota(jnp.int32, (1, LANES), 1)
     own = (lane == at_ref[0]) | (lane == at_ref[0] + experts)
     weight = jnp.sum(jnp.where(own, w_ref[...], 0.0), axis=1, keepdims=True)
@@ -160,7 +164,7 @@
         y = jnp.dot(h_ref[...], down_ref[:, cols], preferred_element_type=jnp.float32)
         y = (y * w_ref[:, pl.ds(0, 1)]).astype(jnp.bfloat16)
         keep_ref[:, cols] = y[:half]
-        send_ref[:, cols] = y[half:]
+        send_ref[:, cols] = y[half:row]
 
 
 def ffn(x_blocks, w_gate, w_up, w_down, expert_at, experts):
@@ -173,9 +177,9 @@
         in_specs=[SMEM] + [VMEM] * (len(x_blocks) + 3),
         out_specs=(VMEM, VMEM),
         scratch_shapes=[
-            pltpu.VMEM((rows, width), jnp.bfloat16),
-            pltpu.VMEM((rows, units), jnp.bfloat16),
-            pltpu.VMEM((rows, LANES), jnp.float32),
+            pltpu.VMEM((max(rows, LANES), width), jnp.bfloat16),
+            pltpu.VMEM((max(rows, LANES), units), jnp.bfloat16),
+            pltpu.VMEM((max(rows, LANES), LANES), jnp.float32),
         ],
         cost_estimate=pl.CostEstimate(
             flops=6 * rows * width * units,

time: 59.4 us -> 59.2 us (level)
  no operation moved by 1% of the time
where the time goes in v7:
time: 59.2 us; the launch traced here: 59.1 us
  waiting for transfers between devices  28 us (47%)
  starting transfers between devices  20.7 us (35%)
  Pallas kernels  9.14 us (15%)
  local copies, waits for them, and re-layouts  0.69 us (1%)
    ppermute x13, waiting for transfers between devices, swap(): return lax.ppermute(value, 'expert', [(i, i ^ bit) for i in range(experts)])  19.4 us
    ppermute x13, starting transfers between devices, swap(): return lax.ppermute(value, 'expert', [(i, i ^ bit) for i in range(experts)])  14.1 us
    ppermute x4, waiting for transfers between devices, pair(): return lax.ppermute(value, 'attn', [(0, 1), (1, 0)])  5.73 us
    ppermute x4, starting transfers between devices, pair(): return lax.ppermute(value, 'attn', [(0, 1), (1, 0)])  5.36 us
    pallas_call x1, Pallas kernels, load(): pl.pallas_call(load_kernel, out_shape=(jax.ShapeDtypeStruct(gate.shape, g...  4.23 us
    pallas_call x2, Pallas kernels, ffn(): pl.pallas_call(functools.partial(ffn_kernel, experts, len(x_blocks)), out...  3.82 us
    ppermute x2, waiting for transfers between devices, cross(): return lax.ppermute(value, ('expert', 'attn'), order)  2.86 us
    ppermute x2, starting transfers between devices, cross(): return lax.ppermute(value, ('expert', 'attn'), order)  1.32 us
  transfers between devices with their start and end apart: 19, of which 9 were waited for; matrix products, arithmetic and copies ran while one was open for 1% of the time, Pallas kernels for 10%

profile of v7, /device:TPU:0, one launch (start us, length us, event | category | flops | bytes accessed | tf_op | source)
XLA Modules:
  0.0 59.1 jit_solution(7927492195337585905)
XLA Ops:
  0.0 1.1 %prepare.1 = (bf16[32,3712]{1,0:T(8,128)(2,1)S(1)}, bf16[16,3712]{1,0:T(8,128)(2,1)S(1)}) custom-call(s32[1]{0:T(128)} %bitcast.1.at_ref, s32[1]{0:T(128)} %bitcast.expert_ref.at_ref, s32[8]{0:T(128)} %plan_hbm.1, s32[8,32]{1,0:T(8,128)} %bitcast.10, f32[8,32]{1,0:T(8,128)} %bitcast.11, bf16[32,3584]{1,0:T(8,128)(2,1)} %tok_hbm.1), custom_call_target="tpu_custom_call" | custom-call | tf_op jit(solution)/shard_map/prepare/pallas_call | solution.py:71
  1.1 3.1 %collective-permute-start = (bf16[32,3712]{1,0:T(8,128)(2,1)S(1)}, bf16[32,3712]{1,0:T(8,128)(2,1)S(1)}, u32[]{:S(2)}, u32[]{:S(2)}) collective-permute-start(bf16[32,3712]{1,0:T(8,128)(2,1)S(1)} %get-tuple-element.14.refs_0_), channel_id=1, source_target_pairs={{0,4},{2,6},{4,0},{6,2},{8,12},{10,14},{12,8},{14,10},{1,5},{3,7},... | collective-permute-start | bytes 712712 | tf_op jit(solution)/shard_map/ppermute | solution.py:213
  4.2 2.6 %collective-permute-start.1 = (bf16[16,3712]{1,0:T(8,128)(2,1)S(1)}, bf16[16,3712]{1,0:T(8,128)(2,1)S(1)}, u32[]{:S(2)}, u32[]{:S(2)}) collective-permute-start(bf16[16,3712]{1,0:T(8,128)(2,1)S(1)} %get-tuple-element.15), channel_id=1, source_target_pairs={{0,8},{2,10},{4,12},{6,14},{8,0},{10,2},{12,4},{14,6},{1,9},{3,11}... | collective-permute-start | bytes 356360 | tf_op jit(solution)/shard_map/ppermute | solution.py:213
  6.8 5.7 %collective-permute-done.refs_1_ = bf16[32,3712]{1,0:T(8,128)(2,1)S(1)} collective-permute-done((bf16[32,3712]{1,0:T(8,128)(2,1)S(1)}, bf16[32,3712]{1,0:T(8,128)(2,1)S(1)}, u32[]{:S(2)}, u32[]{:S(2)}) %collective-permute-start) | collective-permute-done | bytes 237600 | tf_op jit(solution)/shard_map/ppermute | solution.py:213
  12.6 0.5 collective-permute-start.4
  13.1 4.2 %load.1 = (bf16[3584,512]{1,0:T(8,128)(2,1)S(1)}, bf16[3584,512]{1,0:T(8,128)(2,1)S(1)}, bf16[512,3584]{1,0:T(8,128)(2,1)S(1)}) custom-call(bf16[3584,512]{1,0:T(8,128)(2,1)} %bitcast.7, bf16[3584,512]{1,0:T(8,128)(2,1)} %bitcast.8, bf16[3584,512]{1,0:T(8,128)(2,1)} %bitcast.9), custom_call_target="tpu_custom_call" | custom-call | bytes 22020096 | tf_op jit(solution)/shard_map/load/pallas_call | solution.py:118
  17.3 2.1 %ffn.2 = (bf16[80,3584]{1,0:T(8,128)(2,1)S(1)}, bf16[80,3584]{1,0:T(8,128)(2,1)S(1)}) custom-call(s32[1]{0:T(128)} %bitcast.expert_ref.at_ref, bf16[32,3712]{1,0:T(8,128)(2,1)S(1)} %get-tuple-element.14.refs_0_, bf16[32,3712]{1,0:T(8,128)(2,1)S(1)} %collective-permute-done.refs_1_, bf16[16,3712]{1,0:T(8,128)(2,1)S(1)} %collective-permute-done.1.refs_2_, ...), custom_call_target="tpu_custom_call" | custom-call | flops 1761607680 | bytes 15597568 | tf_op jit(solution)/shard_map/ffn/pallas_call | solution.py:174
  19.4 0.1 collective-permute-start.5
  19.5 1.7 %collective-permute-start.8 = (bf16[16,3712]{1,0:T(8,128)(2,1)S(1)}, bf16[16,3712]{1,0:T(8,128)(2,1)S(1)}, u32[]{:S(2)}, u32[]{:S(2)}) collective-permute-start(bf16[16,3712]{1,0:T(8,128)(2,1)S(1)} %collective-permute-done.1.refs_2_), channel_id=1, source_target_pairs={{0,1},{1,0},{2,3},{3,2},{4,5},{5,4},{6,7},{7,6},{8,9},{9,8},{10,11... | collective-permute-start | bytes 356360 | tf_op jit(solution)/shard_map/ppermute | solution.py:219
  21.2 2.5 %collective-permute-start.9 = (bf16[16,3712]{1,0:T(8,128)(2,1)S(1)}, bf16[16,3712]{1,0:T(8,128)(2,1)S(1)}, u32[]{:S(2)}, u32[]{:S(2)}) collective-permute-start(bf16[16,3712]{1,0:T(8,128)(2,1)S(1)} %collective-permute-done.1.refs_2_), channel_id=1, source_target_pairs={{0,4},{2,6},{4,0},{6,2},{8,12},{10,14},{12,8},{14,10},{1,5},{3,7},... | collective-permute-start | bytes 356360 | tf_op jit(solution)/shard_map/ppermute | solution.py:213
  23.7 1.4 %collective-permute-done.8.refs_0_ = bf16[16,3712]{1,0:T(8,128)(2,1)S(1)} collective-permute-done((bf16[16,3712]{1,0:T(8,128)(2,1)S(1)}, bf16[16,3712]{1,0:T(8,128)(2,1)S(1)}, u32[]{:S(2)}, u32[]{:S(2)}) %collective-permute-start.8) | collective-permute-done | bytes 118816 | tf_op jit(solution)/shard_map/ppermute | solution.py:219
  25.1 2.7 %collective-permute-done.9.refs_1_ = bf16[16,3712]{1,0:T(8,128)(2,1)S(1)} collective-permute-done((bf16[16,3712]{1,0:T(8,128)(2,1)S(1)}, bf16[16,3712]{1,0:T(8,128)(2,1)S(1)}, u32[]{:S(2)}, u32[]{:S(2)}) %collective-permute-start.9) | collective-permute-done | bytes 118816 | tf_op jit(solution)/shard_map/ppermute | solution.py:213
  27.8 1.6 %collective-permute-done.10.refs_2_ = bf16[16,3712]{1,0:T(8,128)(2,1)S(1)} collective-permute-done((bf16[16,3712]{1,0:T(8,128)(2,1)S(1)}, bf16[16,3712]{1,0:T(8,128)(2,1)S(1)}, u32[]{:S(2)}, u32[]{:S(2)}) %collective-permute-start.10) | collective-permute-done | bytes 118816 | tf_op jit(solution)/shard_map/ppermute | solution.py:223
  29.5 1.3 %collective-permute-done.13.refs_5_ = bf16[16,3712]{1,0:T(8,128)(2,1)S(1)} collective-permute-done((bf16[16,3712]{1,0:T(8,128)(2,1)S(1)}, bf16[16,3712]{1,0:T(8,128)(2,1)S(1)}, u32[]{:S(2)}, u32[]{:S(2)}) %collective-permute-start.13) | collective-permute-done | bytes 118816 | tf_op jit(solution)/shard_map/ppermute | solution.py:213
  30.8 1.7 %ffn.3 = (bf16[48,3584]{1,0:T(8,128)(2,1)S(1)}, bf16[48,3584]{1,0:T(8,128)(2,1)S(1)}) custom-call(s32[1]{0:T(128)} %bitcast.expert_ref.at_ref, bf16[16,3712]{1,0:T(8,128)(2,1)S(1)} %collective-permute-done.8.refs_0_, bf16[16,3712]{1,0:T(8,128)(2,1)S(1)} %collective-permute-done.9.refs_1_, bf16[16,3712]{1,0:T(8,128)(2,1)S(1)} %collective-permute-done.10.refs_2_, ...), custom_call_target="tpu_custom_call" | custom-call | flops 1056964608 | bytes 13762560 | tf_op jit(solution)/shard_map/ffn/pallas_call | solution.py:174
  32.5 0.2 collective-permute-start.14
  32.8 0.1 add_convert_fusion
  32.8 1.8 %collective-permute-start.6 = (bf16[48,3584]{1,0:T(8,128)(2,1)S(1)}, bf16[48,3584]{1,0:T(8,128)(2,1)S(1)}, u32[]{:S(2)}, u32[]{:S(2)}) collective-permute-start(bf16[48,3584]{1,0:T(8,128)(2,1)S(1)} %add_convert_fusion), channel_id=1, source_target_pairs={{0,4},{2,6},{4,0},{6,2},{8,12},{10,14},{12,8},{14,10},{1,5},{3,7},... | collective-permute-start | bytes 1032200 | tf_op jit(solution)/shard_map/ppermute | solution.py:213
  34.6 0.1 add_convert_fusion.5
  34.7 1.6 %collective-permute-start.15 = (bf16[16,3584]{1,0:T(8,128)(2,1)S(1)}, bf16[16,3584]{1,0:T(8,128)(2,1)S(1)}, u32[]{:S(2)}, u32[]{:S(2)}) collective-permute-start(bf16[16,3584]{1,0:T(8,128)(2,1)S(1)} %get-tuple-element.25), channel_id=1, source_target_pairs={{0,1},{1,0},{2,3},{3,2},{4,5},{5,4},{6,7},{7,6},{8,9},{9,8},{10,11... | collective-permute-start | bytes 344072 | tf_op jit(solution)/shard_map/ppermute | solution.py:219
  36.3 1.3 %collective-permute-start.16 = (bf16[16,3584]{1,0:T(8,128)(2,1)S(1)}, bf16[16,3584]{1,0:T(8,128)(2,1)S(1)}, u32[]{:S(2)}, u32[]{:S(2)}) collective-permute-start(bf16[16,3584]{1,0:T(8,128)(2,1)S(1)} %get-tuple-element.26), channel_id=1, source_target_pairs={{0,5},{1,4},{2,7},{3,6},{4,1},{5,0},{6,3},{7,2},{8,13},{9,12},{10,... | collective-permute-start | bytes 344072 | tf_op jit(solution)/shard_map/ppermute | solution.py:223
  37.6 6.3 %collective-permute-done.6 = bf16[48,3584]{1,0:T(8,128)(2,1)S(1)} collective-permute-done((bf16[48,3584]{1,0:T(8,128)(2,1)S(1)}, bf16[48,3584]{1,0:T(8,128)(2,1)S(1)}, u32[]{:S(2)}, u32[]{:S(2)}) %collective-permute-start.6) | collective-permute-done | bytes 344096 | tf_op jit(solution)/shard_map/ppermute | solution.py:213
  43.8 0.1 add_convert_fusion.1
  43.9 1.5 %collective-permute-start.7 = (bf16[16,3584]{1,0:T(8,128)(2,1)S(1)}, bf16[16,3584]{1,0:T(8,128)(2,1)S(1)}, u32[]{:S(2)}, u32[]{:S(2)}) collective-permute-start(bf16[16,3584]{1,0:T(8,128)(2,1)S(1)} %slice.60), channel_id=1, source_target_pairs={{0,1},{1,0},{2,3},{3,2},{4,5},{5,4},{6,7},{7,6},{8,9},{9,8},{10,11... | collective-permute-start | bytes 344072 | tf_op jit(solution)/shard_map/ppermute | solution.py:219
  45.5 1.2 %collective-permute-done.16 = bf16[16,3584]{1,0:T(8,128)(2,1)S(1)} collective-permute-done((bf16[16,3584]{1,0:T(8,128)(2,1)S(1)}, bf16[16,3584]{1,0:T(8,128)(2,1)S(1)}, u32[]{:S(2)}, u32[]{:S(2)}) %collective-permute-start.16) | collective-permute-done | bytes 114720 | tf_op jit(solution)/shard_map/ppermute | solution.py:223
  46.7 0.1 add_convert_fusion.3
  46.8 3.3 %collective-permute-start.17 = (bf16[16,3584]{1,0:T(8,128)(2,1)S(1)}, bf16[16,3584]{1,0:T(8,128)(2,1)S(1)}, u32[]{:S(2)}, u32[]{:S(2)}) collective-permute-start(bf16[16,3584]{1,0:T(8,128)(2,1)S(1)} %add_convert_fusion.3), channel_id=1, source_target_pairs={{0,12},{2,14},{4,8},{6,10},{8,4},{10,6},{12,0},{14,2},{1,13},{3,15... | collective-permute-start | bytes 344072 | tf_op jit(solution)/shard_map/ppermute | solution.py:213
  50.0 3.4 %collective-permute-done.17 = bf16[16,3584]{1,0:T(8,128)(2,1)S(1)} collective-permute-done((bf16[16,3584]{1,0:T(8,128)(2,1)S(1)}, bf16[16,3584]{1,0:T(8,128)(2,1)S(1)}, u32[]{:S(2)}, u32[]{:S(2)}) %collective-permute-start.17) | collective-permute-done | bytes 114720 | tf_op jit(solution)/shard_map/ppermute | solution.py:213
  53.5 0.1 constant_dynamic-update-slice_fusion.1
  53.5 0.5 collective-permute-start.18
  54.1 4.3 %collective-permute-done.18 = bf16[16,3584]{1,0:T(8,128)(2,1)S(1)} collective-permute-done((bf16[16,3584]{1,0:T(8,128)(2,1)S(1)}, bf16[16,3584]{1,0:T(8,128)(2,1)S(1)}, u32[]{:S(2)}, u32[]{:S(2)}) %collective-permute-start.18) | collective-permute-done | bytes 114720 | tf_op jit(solution)/shard_map/ppermute | solution.py:219
  58.4 0.7 %constant_dynamic-update-slice_fusion = bf16[32,3584]{1,0:T(8,128)(2,1)} fusion(bf16[32,3584]{1,0:T(8,128)(2,1)} %copy-done, bf16[16,3584]{1,0:T(8,128)(2,1)S(1)} %collective-permute-done.18, s32[]{:T(128)S(6)} %select_n.7), kind=kLoop, calls=%fused_computation.7 | loop fusion | bytes 229380 | tf_op jit(solution)/shard_map/dynamic_update_slice | solution.py:252
  (20 shorter events, 0.1 us)
Async XLA Ops:
  1.1 11.4 %collective-permute-start = (bf16[32,3712]{1,0:T(8,128)(2,1)S(1)}, bf16[32,3712]{1,0:T(8,128)(2,1)S(1)}, u32[]{:S(2)}, u32[]{:S(2)}) collective-permute-start(bf16[32,3712]{1,0:T(8,128)(2,1)S(1)} %get-tuple-element.14.refs_0_), channel_id=1, source_target_pairs={{0,4},{2,6},{4,0},{6,2},{8,12},{10,14},{12,8},{14,10},{1,5},{3,7},... | collective-permute-start | bytes 712712 | tf_op jit(solution)/shard_map/ppermute | solution.py:213
  4.2 8.3 %collective-permute-start.1 = (bf16[16,3712]{1,0:T(8,128)(2,1)S(1)}, bf16[16,3712]{1,0:T(8,128)(2,1)S(1)}, u32[]{:S(2)}, u32[]{:S(2)}) collective-permute-start(bf16[16,3712]{1,0:T(8,128)(2,1)S(1)} %get-tuple-element.15), channel_id=1, source_target_pairs={{0,8},{2,10},{4,12},{6,14},{8,0},{10,2},{12,4},{14,6},{1,9},{3,11}... | collective-permute-start | bytes 356360 | tf_op jit(solution)/shard_map/ppermute | solution.py:213
  6.8 10.5 %collective-permute-start.2 = (bf16[32,3712]{1,0:T(8,128)(2,1)S(1)}, bf16[32,3712]{1,0:T(8,128)(2,1)S(1)}, u32[]{:S(2)}, u32[]{:S(2)}) collective-permute-start(bf16[32,3712]{1,0:T(8,128)(2,1)S(1)} %get-tuple-element.14.refs_0_), channel_id=1, source_target_pairs={{0,2},{2,0},{4,6},{6,4},{8,10},{10,8},{12,14},{14,12},{1,3},{3,1},... | collective-permute-start | bytes 712712 | tf_op jit(solution)/shard_map/ppermute | solution.py:213
  12.5 4.8 %collective-permute-start.3 = (bf16[32,3712]{1,0:T(8,128)(2,1)S(1)}, bf16[32,3712]{1,0:T(8,128)(2,1)S(1)}, u32[]{:S(2)}, u32[]{:S(2)}) collective-permute-start(bf16[32,3712]{1,0:T(8,128)(2,1)S(1)} %collective-permute-done.refs_1_), channel_id=1, source_target_pairs={{0,2},{2,0},{4,6},{6,4},{8,10},{10,8},{12,14},{14,12},{1,3},{3,1},... | collective-permute-start | bytes 712712 | tf_op jit(solution)/shard_map/ppermute | solution.py:213
  12.6 4.8 %collective-permute-start.4 = (bf16[16,3712]{1,0:T(8,128)(2,1)S(1)}, bf16[16,3712]{1,0:T(8,128)(2,1)S(1)}, u32[]{:S(2)}, u32[]{:S(2)}) collective-permute-start(bf16[16,3712]{1,0:T(8,128)(2,1)S(1)} %collective-permute-done.1.refs_2_), channel_id=1, source_target_pairs={{0,2},{2,0},{4,6},{6,4},{8,10},{10,8},{12,14},{14,12},{1,3},{3,1},... | collective-permute-start | bytes 356360 | tf_op jit(solution)/shard_map/ppermute | solution.py:213
  19.4 13.3 %collective-permute-start.5 = (bf16[80,3584]{1,0:T(8,128)(2,1)S(1)}, bf16[80,3584]{1,0:T(8,128)(2,1)S(1)}, u32[]{:S(2)}, u32[]{:S(2)}) collective-permute-start(bf16[80,3584]{1,0:T(8,128)(2,1)S(1)} %get-tuple-element.20), channel_id=1, source_target_pairs={{0,2},{2,0},{4,6},{6,4},{8,10},{10,8},{12,14},{14,12},{1,3},{3,1},... | collective-permute-start | bytes 1720328 | tf_op jit(solution)/shard_map/ppermute | solution.py:213
  19.5 5.6 %collective-permute-start.8 = (bf16[16,3712]{1,0:T(8,128)(2,1)S(1)}, bf16[16,3712]{1,0:T(8,128)(2,1)S(1)}, u32[]{:S(2)}, u32[]{:S(2)}) collective-permute-start(bf16[16,3712]{1,0:T(8,128)(2,1)S(1)} %collective-permute-done.1.refs_2_), channel_id=1, source_target_pairs={{0,1},{1,0},{2,3},{3,2},{4,5},{5,4},{6,7},{7,6},{8,9},{9,8},{10,11... | collective-permute-start | bytes 356360 | tf_op jit(solution)/shard_map/ppermute | solution.py:219
  21.2 6.6 %collective-permute-start.9 = (bf16[16,3712]{1,0:T(8,128)(2,1)S(1)}, bf16[16,3712]{1,0:T(8,128)(2,1)S(1)}, u32[]{:S(2)}, u32[]{:S(2)}) collective-permute-start(bf16[16,3712]{1,0:T(8,128)(2,1)S(1)} %collective-permute-done.1.refs_2_), channel_id=1, source_target_pairs={{0,4},{2,6},{4,0},{6,2},{8,12},{10,14},{12,8},{14,10},{1,5},{3,7},... | collective-permute-start | bytes 356360 | tf_op jit(solution)/shard_map/ppermute | solution.py:213
  23.7 5.7 %collective-permute-start.10 = (bf16[16,3712]{1,0:T(8,128)(2,1)S(1)}, bf16[16,3712]{1,0:T(8,128)(2,1)S(1)}, u32[]{:S(2)}, u32[]{:S(2)}) collective-permute-start(bf16[16,3712]{1,0:T(8,128)(2,1)S(1)} %collective-permute-done.1.refs_2_), channel_id=1, source_target_pairs={{0,5},{1,4},{2,7},{3,6},{4,1},{5,0},{6,3},{7,2},{8,13},{9,12},{10,... | collective-permute-start | bytes 356360 | tf_op jit(solution)/shard_map/ppermute | solution.py:223
  25.1 4.3 %collective-permute-start.11 = (bf16[16,3712]{1,0:T(8,128)(2,1)S(1)}, bf16[16,3712]{1,0:T(8,128)(2,1)S(1)}, u32[]{:S(2)}, u32[]{:S(2)}) collective-permute-start(bf16[16,3712]{1,0:T(8,128)(2,1)S(1)} %collective-permute-done.8.refs_0_), channel_id=1, source_target_pairs={{0,2},{2,0},{4,6},{6,4},{8,10},{10,8},{12,14},{14,12},{1,3},{3,1},... | collective-permute-start | bytes 356360 | tf_op jit(solution)/shard_map/ppermute | solution.py:213
  27.8 1.7 %collective-permute-start.12 = (bf16[16,3712]{1,0:T(8,128)(2,1)S(1)}, bf16[16,3712]{1,0:T(8,128)(2,1)S(1)}, u32[]{:S(2)}, u32[]{:S(2)}) collective-permute-start(bf16[16,3712]{1,0:T(8,128)(2,1)S(1)} %collective-permute-done.9.refs_1_), channel_id=1, source_target_pairs={{0,2},{2,0},{4,6},{6,4},{8,10},{10,8},{12,14},{14,12},{1,3},{3,1},... | collective-permute-start | bytes 356360 | tf_op jit(solution)/shard_map/ppermute | solution.py:213
  29.5 1.3 %collective-permute-start.13 = (bf16[16,3712]{1,0:T(8,128)(2,1)S(1)}, bf16[16,3712]{1,0:T(8,128)(2,1)S(1)}, u32[]{:S(2)}, u32[]{:S(2)}) collective-permute-start(bf16[16,3712]{1,0:T(8,128)(2,1)S(1)} %collective-permute-done.10.refs_2_), channel_id=1, source_target_pairs={{0,2},{2,0},{4,6},{6,4},{8,10},{10,8},{12,14},{14,12},{1,3},{3,1},... | collective-permute-start | bytes 356360 | tf_op jit(solution)/shard_map/ppermute | solution.py:213
  32.5 2.1 %collective-permute-start.14 = (bf16[48,3584]{1,0:T(8,128)(2,1)S(1)}, bf16[48,3584]{1,0:T(8,128)(2,1)S(1)}, u32[]{:S(2)}, u32[]{:S(2)}) collective-permute-start(bf16[48,3584]{1,0:T(8,128)(2,1)S(1)} %get-tuple-element.22), channel_id=1, source_target_pairs={{0,2},{2,0},{4,6},{6,4},{8,10},{10,8},{12,14},{14,12},{1,3},{3,1},... | collective-permute-start | bytes 1032200 | tf_op jit(solution)/shard_map/ppermute | solution.py:213
  32.8 11.0 %collective-permute-start.6 = (bf16[48,3584]{1,0:T(8,128)(2,1)S(1)}, bf16[48,3584]{1,0:T(8,128)(2,1)S(1)}, u32[]{:S(2)}, u32[]{:S(2)}) collective-permute-start(bf16[48,3584]{1,0:T(8,128)(2,1)S(1)} %add_convert_fusion), channel_id=1, source_target_pairs={{0,4},{2,6},{4,0},{6,2},{8,12},{10,14},{12,8},{14,10},{1,5},{3,7},... | collective-permute-start | bytes 1032200 | tf_op jit(solution)/shard_map/ppermute | solution.py:213
  34.7 10.8 %collective-permute-start.15 = (bf16[16,3584]{1,0:T(8,128)(2,1)S(1)}, bf16[16,3584]{1,0:T(8,128)(2,1)S(1)}, u32[]{:S(2)}, u32[]{:S(2)}) collective-permute-start(bf16[16,3584]{1,0:T(8,128)(2,1)S(1)} %get-tuple-element.25), channel_id=1, source_target_pairs={{0,1},{1,0},{2,3},{3,2},{4,5},{5,4},{6,7},{7,6},{8,9},{9,8},{10,11... | collective-permute-start | bytes 344072 | tf_op jit(solution)/shard_map/ppermute | solution.py:219
  36.3 10.5 %collective-permute-start.16 = (bf16[16,3584]{1,0:T(8,128)(2,1)S(1)}, bf16[16,3584]{1,0:T(8,128)(2,1)S(1)}, u32[]{:S(2)}, u32[]{:S(2)}) collective-permute-start(bf16[16,3584]{1,0:T(8,128)(2,1)S(1)} %get-tuple-element.26), channel_id=1, source_target_pairs={{0,5},{1,4},{2,7},{3,6},{4,1},{5,0},{6,3},{7,2},{8,13},{9,12},{10,... | collective-permute-start | bytes 344072 | tf_op jit(solution)/shard_map/ppermute | solution.py:223
  43.9 6.1 %collective-permute-start.7 = (bf16[16,3584]{1,0:T(8,128)(2,1)S(1)}, bf16[16,3584]{1,0:T(8,128)(2,1)S(1)}, u32[]{:S(2)}, u32[]{:S(2)}) collective-permute-start(bf16[16,3584]{1,0:T(8,128)(2,1)S(1)} %slice.60), channel_id=1, source_target_pairs={{0,1},{1,0},{2,3},{3,2},{4,5},{5,4},{6,7},{7,6},{8,9},{9,8},{10,11... | collective-permute-start | bytes 344072 | tf_op jit(solution)/shard_map/ppermute | solution.py:219
  46.8 6.7 %collective-permute-start.17 = (bf16[16,3584]{1,0:T(8,128)(2,1)S(1)}, bf16[16,3584]{1,0:T(8,128)(2,1)S(1)}, u32[]{:S(2)}, u32[]{:S(2)}) collective-permute-start(bf16[16,3584]{1,0:T(8,128)(2,1)S(1)} %add_convert_fusion.3), channel_id=1, source_target_pairs={{0,12},{2,14},{4,8},{6,10},{8,4},{10,6},{12,0},{14,2},{1,13},{3,15... | collective-permute-start | bytes 344072 | tf_op jit(solution)/shard_map/ppermute | solution.py:213
  53.5 4.9 %copy-start = (bf16[32,3584]{1,0:T(8,128)(2,1)}, bf16[32,3584]{1,0:T(8,128)(2,1)S(1)}, u32[]{:S(2)}) copy-start(bf16[32,3584]{1,0:T(8,128)(2,1)S(1)} %get-tuple-element.23) | copy-start | bytes 688132
  53.5 4.9 %collective-permute-start.18 = (bf16[16,3584]{1,0:T(8,128)(2,1)S(1)}, bf16[16,3584]{1,0:T(8,128)(2,1)S(1)}, u32[]{:S(2)}, u32[]{:S(2)}) collective-permute-start(bf16[16,3584]{1,0:T(8,128)(2,1)S(1)} %get-tuple-element.24), channel_id=1, source_target_pairs={{0,1},{1,0},{2,3},{3,2},{4,5},{5,4},{6,7},{7,6},{8,9},{9,8},{10,11... | collective-permute-start | bytes 344072 | tf_op jit(solution)/shard_map/ppermute | solution.py:219
